TPU v7x, 32 devices: a whole 2x2x4 slice. The times are simulated.
32 devices in a mesh: dp: 8 (over z, y), mp: 4 (over x, core).
Axes of the slice: x: 2, y: 2, z: 4, core: 2. Of those that a mesh axis runs over, the one named last changes fastest.
Arguments:
- doc_tokens: bfloat16 [16, 1024, 768], P('dp', 'mp'), may hold values from -6 to 6
- query_tokens: bfloat16 [64, 32, 768], P(('dp', 'mp')), may hold values from -6 to 6
- doc_segments: int32 [16, 1024], P('dp'), may hold values from 0 to 3, never falling along the last dimension, each value on 1 to 512 neighbouring positions
- query_keep: int32 [64, 32], replicated, may hold values from 0 to 1, as said below
- retrieved: int32 [64, 32, 64], P(None, None, 'dp'), may hold values 0 or 1
- positives: int32 [64], replicated, may hold values from 0 to 63
- attn_gain: bfloat16 [768], replicated, may hold values from 0.5 to 1.5
- query_weight: bfloat16 [768, 768], P(None, 'mp'), may hold values from -0.02734375 to 0.02734375
- key_weight: bfloat16 [768, 768], P(None, 'mp'), may hold values from -0.21875 to 0.21875
- value_weight: bfloat16 [768, 768], P(None, 'mp'), may hold values from -0.21875 to 0.21875
- output_weight: bfloat16 [768, 768], P('mp'), may hold values from -0.625 to 0.625
- position_bias: bfloat16 [32, 12], P(None, 'mp'), may hold values from -4 to 4
- ffn_gain: bfloat16 [768], replicated, may hold values from 0.5 to 1.5
- gate_weight: bfloat16 [768, 2048], P(None, 'mp'), may hold values from -0.21875 to 0.21875
- up_weight: bfloat16 [768, 2048], P(None, 'mp'), may hold values from -0.21875 to 0.21875
- down_weight: bfloat16 [2048, 768], P('mp'), may hold values from -0.125 to 0.125
- final_gain: bfloat16 [768], replicated, may hold values from 0.5 to 1.5
- proj_weight: bfloat16 [768, 128], replicated, may hold values from -0.21875 to 0.21875
Outputs:
- loss_value: float32 [], replicated
- found_share: float32 [], replicated
- doc_grad: float32 [16, 1024, 768], P('dp', 'mp')
- query_grad: float32 [64, 32, 768], P(('dp', 'mp'))
- attn_gain_grad: float32 [768], replicated
- query_weight_grad: float32 [768, 768], P(None, 'mp')
- key_weight_grad: float32 [768, 768], P(None, 'mp')
- value_weight_grad: float32 [768, 768], P(None, 'mp')
- output_weight_grad: float32 [768, 768], P('mp')
- position_bias_grad: float32 [32, 12], P(None, 'mp')
- ffn_gain_grad: float32 [768], replicated
- switch_matrix_derivative: float32 [768, 2048], P(None, 'mp')
- up_weight_grad: float32 [768, 2048], P(None, 'mp')
- down_weight_grad: float32 [2048, 768], P('mp')
- final_gain_grad: float32 [768], replicated
- proj_weight_grad: float32 [768, 128], replicated
Inputs may be any that keep to these rules, and one draw needn't show every extreme that they name: `doc_segments`: each row holds 4 documents, numbered in order and never falling. `query_keep`: each query keeps a prefix of its tokens, at least 8 of them.
All inputs are finite; a program needn't handle non-finite values. No bound on the sum of `retrieved` on one device may be relied on, other than what follows from the above.
Results may differ from a plain program's by a relative error of at most 0.035.
Values may be sent and summed in bfloat16 or wider, within the bound.
No kernel may reach another device: no remote copies, remote signals or barrier semaphores. Data moves between devices by JAX's collectives and lax.ppermute only.
A program may use at most 192 MiB of HBM per device.

v0:
```python
import jax
import jax.numpy as jnp
import numpy as np
from jax import lax
from jax.sharding import PartitionSpec as P

epsilon = 1e-06
sharpness = 16.0
smoothing_divisor = 0.05
masked_score = -1e30


def bucket_table(length, buckets):
    offsets = np.arange(-(length - 1), length)
    half_count = buckets // 2
    exact_count = half_count // 2
    distance = np.abs(offsets)
    scaled = (
        np.log(np.maximum(distance, 1) / exact_count)
        / np.log(128.0 / exact_count)
        * (half_count - exact_count)
    )
    far_bucket = np.minimum(exact_count + np.floor(np.maximum(scaled, 0.0)), half_count - 1)
    bucket = np.where(distance < exact_count, distance, far_bucket) + np.where(
        offsets > 0, half_count, 0
    )
    return bucket.astype(np.int32)


def bucket_line(length, buckets, block_rows):
    return jnp.pad(jnp.asarray(bucket_table(length, buckets)).astype(jnp.int32), block_rows + 1)


def offset_onehot(line_ids, row_start, block_rows, length, buckets):
    ids = lax.dynamic_slice_in_dim(
        jnp.asarray(line_ids), length - row_start, length + block_rows + 1, 0
    )
    return (ids[None, :] == jnp.arange(buckets)[:, None]).astype(jnp.float32)


def skewed_bias(bias_table, onehot, block_rows, length):
    by_offset = jnp.dot(jnp.transpose(bias_table), onehot, precision=lax.Precision.HIGHEST)
    head_count = by_offset.shape[0]
    wide = length + block_rows
    rows = jnp.broadcast_to(by_offset[:, None, :], (head_count, block_rows, wide + 1))
    flat = rows.reshape(head_count, block_rows * (wide + 1))[:, : block_rows * wide]
    return flat.reshape(head_count, block_rows, wide)[:, :, block_rows : block_rows + length]


def diagonal_sums(gradient):
    head_count, block_rows, length = gradient.shape
    wide = length + block_rows
    padded = jnp.pad(gradient, ((0, 0), (0, 0), (block_rows, 0))).reshape(
        head_count, block_rows * wide
    )
    padded = jnp.pad(padded, ((0, 0), (0, block_rows))).reshape(head_count, block_rows, wide + 1)
    return jnp.sum(padded, axis=1)


def left_dot(left_side, right_side):
    return lax.dot_general(
        left_side, right_side, (((0,), (0,)), ((), ())), preferred_element_type=jnp.float32
    )


def right_dot(left_side, right_side):
    return lax.dot_general(
        left_side, right_side, (((1,), (1,)), ((), ())), preferred_element_type=jnp.float32
    )


def joined(doc_part, query_part):
    return jnp.concatenate(
        [doc_part.reshape(-1, doc_part.shape[-1]), query_part.reshape(-1, query_part.shape[-1])],
        axis=0,
    )


def parted(flat, doc_shape, query_shape):
    passage_length = doc_shape[0] * doc_shape[1]
    return (
        flat[:passage_length].reshape(doc_shape + (flat.shape[-1],)),
        flat[passage_length:].reshape(query_shape + (flat.shape[-1],)),
    )


def rms_scale(values):
    return lax.rsqrt(jnp.mean(values * values, axis=-1, keepdims=True) + epsilon)


def rms_back(values, scale_values, gain_values, gradient):
    weighted = gradient * gain_values
    average = jnp.mean(weighted * values, axis=-1, keepdims=True)
    input_grad = (
        scale_values * weighted - values * (scale_values * scale_values * scale_values) * average
    )
    gain_grad = jnp.sum((gradient * values * scale_values).reshape(-1, values.shape[-1]), axis=0)
    return (input_grad, gain_grad)


def split_heads(projected, inner_width, head_count, position):
    portion = projected[..., position * inner_width : (position + 1) * inner_width]
    return portion.reshape(portion.shape[:-1] + (head_count, inner_width // head_count))


def start_onehots(line_ids, per_row, block_rows, length, buckets):
    return jnp.stack(
        [
            offset_onehot(line_ids, start * block_rows, block_rows, length, buckets)
            for start in range(per_row)
        ],
        axis=0,
    )


def doc_attention(
    search_requests, key_heads, value_heads, segments, bias_table, line_ids, block_rows
):
    row_count, length, head_count, head_size = search_requests.shape
    per_row = length // block_rows
    onehots = start_onehots(line_ids, per_row, block_rows, length, bias_table.shape[0])
    bias_stack = jnp.stack(
        [skewed_bias(bias_table, onehots[start], block_rows, length) for start in range(per_row)],
        axis=0,
    )

    def attend_block(block_index):
        row_index = block_index // per_row
        row_start = block_index % per_row * block_rows
        row_queries = lax.dynamic_index_in_dim(search_requests, row_index, 0, keepdims=False)
        row_keys = lax.dynamic_index_in_dim(key_heads, row_index, 0, keepdims=False)
        row_values = lax.dynamic_index_in_dim(value_heads, row_index, 0, keepdims=False)
        row_segments = lax.dynamic_index_in_dim(segments, row_index, 0, keepdims=False)
        block_queries = lax.dynamic_slice_in_dim(row_queries, row_start, block_rows, 0)
        block_segments = lax.dynamic_slice_in_dim(row_segments, row_start, block_rows, 0)
        pairing_ratings = jnp.einsum(
            "ihd,jhd->hij", block_queries, row_keys, preferred_element_type=jnp.float32
        )
        pairing_ratings = pairing_ratings + lax.dynamic_index_in_dim(
            bias_stack, block_index % per_row, 0, keepdims=False
        )
        allowed = block_segments[:, None] == row_segments[None, :]
        pairing_ratings = jnp.where(allowed[None], pairing_ratings, masked_score)
        largest = jnp.max(pairing_ratings, axis=-1, keepdims=True)
        powered_scores = jnp.exp(pairing_ratings - largest)
        pooled_sum = jnp.sum(powered_scores, axis=-1, keepdims=True)
        weights = (powered_scores / pooled_sum).astype(jnp.bfloat16)
        attended = jnp.einsum(
            "hij,jhd->ihd", weights, row_values, preferred_element_type=jnp.float32
        )
        return (attended.astype(jnp.bfloat16), (largest + jnp.log(pooled_sum))[..., 0])

    attended, log_totals = lax.map(attend_block, jnp.arange(row_count * per_row))
    return (attended.reshape(row_count, length, head_count * head_size), log_totals)


def doc_attention_back(
    search_requests,
    key_heads,
    value_heads,
    segments,
    bias_table,
    line_ids,
    block_rows,
    log_totals,
    context_grad,
):
    row_count, length, head_count, head_size = search_requests.shape
    per_row = length // block_rows
    onehots = start_onehots(line_ids, per_row, block_rows, length, bias_table.shape[0])
    bias_stack = jnp.stack(
        [skewed_bias(bias_table, onehots[start], block_rows, length) for start in range(per_row)],
        axis=0,
    )

    def doc_block_back(running, block_index):
        key_grads, value_grads, offset_grads = running
        row_index = block_index // per_row
        start_index = block_index % per_row
        row_start = start_index * block_rows
        row_queries = lax.dynamic_index_in_dim(search_requests, row_index, 0, keepdims=False)
        row_keys = lax.dynamic_index_in_dim(key_heads, row_index, 0, keepdims=False)
        row_values = lax.dynamic_index_in_dim(value_heads, row_index, 0, keepdims=False)
        row_segments = lax.dynamic_index_in_dim(segments, row_index, 0, keepdims=False)
        row_grads = lax.dynamic_index_in_dim(context_grad, row_index, 0, keepdims=False)
        block_queries = lax.dynamic_slice_in_dim(row_queries, row_start, block_rows, 0)
        block_segments = lax.dynamic_slice_in_dim(row_segments, row_start, block_rows, 0)
        block_grad = lax.dynamic_slice_in_dim(row_grads, row_start, block_rows, 0)
        pairing_ratings = jnp.einsum(
            "ihd,jhd->hij", block_queries, row_keys, preferred_element_type=jnp.float32
        )
        pairing_ratings = pairing_ratings + lax.dynamic_index_in_dim(
            bias_stack, start_index, 0, keepdims=False
        )
        allowed = block_segments[:, None] == row_segments[None, :]
        pairing_ratings = jnp.where(allowed[None], pairing_ratings, masked_score)
        weights = jnp.exp(pairing_ratings - log_totals[block_index][..., None])
        weight_grad = jnp.einsum(
            "ihd,jhd->hij", block_grad, row_values, preferred_element_type=jnp.float32
        )
        score_grad = (
            weights * (weight_grad - jnp.sum(weights * weight_grad, axis=-1, keepdims=True))
        ).astype(jnp.bfloat16)
        query_grad = jnp.einsum(
            "hij,jhd->ihd", score_grad, row_keys, preferred_element_type=jnp.float32
        )
        key_part = jnp.einsum(
            "hij,ihd->jhd", score_grad, block_queries, preferred_element_type=jnp.float32
        )
        value_part = jnp.einsum(
            "hij,ihd->jhd",
            weights.astype(jnp.bfloat16),
            block_grad,
            preferred_element_type=jnp.float32,
        )
        offset_part = diagonal_sums(score_grad.astype(jnp.float32))
        key_grads = lax.dynamic_update_index_in_dim(
            key_grads,
            lax.dynamic_index_in_dim(key_grads, row_index, 0, keepdims=False) + key_part,
            row_index,
            0,
        )
        value_grads = lax.dynamic_update_index_in_dim(
            value_grads,
            lax.dynamic_index_in_dim(value_grads, row_index, 0, keepdims=False) + value_part,
            row_index,
            0,
        )
        offset_grads = lax.dynamic_update_index_in_dim(
            offset_grads,
            lax.dynamic_index_in_dim(offset_grads, start_index, 0, keepdims=False) + offset_part,
            start_index,
            0,
        )
        return ((key_grads, value_grads, offset_grads), query_grad)

    zeroed = jnp.zeros(search_requests.shape, jnp.float32)
    offset_zero = jnp.zeros((per_row, head_count, length + block_rows + 1), jnp.float32)
    running, query_grads = lax.scan(
        doc_block_back, (zeroed, zeroed, offset_zero), jnp.arange(row_count * per_row)
    )
    bias_grad = jnp.einsum("rhc,rbc->bh", running[2], onehots, precision=lax.Precision.HIGHEST)
    return (query_grads.reshape(search_requests.shape), running[0], running[1], bias_grad)


def query_attention(search_requests, key_heads, value_heads, keep_mask, bias_table, line_ids):
    group_count, query_len, head_count, head_size = search_requests.shape
    onehot = offset_onehot(line_ids, 0, query_len, query_len, bias_table.shape[0])
    bias_values = skewed_bias(bias_table, onehot, query_len, query_len)
    pairing_ratings = (
        jnp.einsum(
            "bihd,bjhd->bhij", search_requests, key_heads, preferred_element_type=jnp.float32
        )
        + bias_values[None]
    )
    pairing_ratings = jnp.where(keep_mask[:, None, None, :] > 0, pairing_ratings, masked_score)
    largest = jnp.max(pairing_ratings, axis=-1, keepdims=True)
    powered_scores = jnp.exp(pairing_ratings - largest)
    pooled_sum = jnp.sum(powered_scores, axis=-1, keepdims=True)
    weights = (powered_scores / pooled_sum).astype(jnp.bfloat16)
    attended = jnp.einsum(
        "bhij,bjhd->bihd", weights, value_heads, preferred_element_type=jnp.float32
    )
    return (
        attended.astype(jnp.bfloat16).reshape(group_count, query_len, head_count * head_size),
        (largest + jnp.log(pooled_sum))[..., 0],
    )


def query_attention_back(
    search_requests,
    key_heads,
    value_heads,
    keep_mask,
    bias_table,
    line_ids,
    log_totals,
    context_grad,
):
    query_len = search_requests.shape[1]
    onehot = offset_onehot(line_ids, 0, query_len, query_len, bias_table.shape[0])
    bias_values = skewed_bias(bias_table, onehot, query_len, query_len)
    pairing_ratings = (
        jnp.einsum(
            "bihd,bjhd->bhij", search_requests, key_heads, preferred_element_type=jnp.float32
        )
        + bias_values[None]
    )
    pairing_ratings = jnp.where(keep_mask[:, None, None, :] > 0, pairing_ratings, masked_score)
    weights = jnp.exp(pairing_ratings - log_totals[..., None])
    weight_grad = jnp.einsum(
        "bihd,bjhd->bhij", context_grad, value_heads, preferred_element_type=jnp.float32
    )
    score_grad = (
        weights * (weight_grad - jnp.sum(weights * weight_grad, axis=-1, keepdims=True))
    ).astype(jnp.bfloat16)
    query_grad = jnp.einsum(
        "bhij,bjhd->bihd", score_grad, key_heads, preferred_element_type=jnp.float32
    )
    key_grad = jnp.einsum(
        "bhij,bihd->bjhd", score_grad, search_requests, preferred_element_type=jnp.float32
    )
    value_grad = jnp.einsum(
        "bhij,bihd->bjhd",
        weights.astype(jnp.bfloat16),
        context_grad,
        preferred_element_type=jnp.float32,
    )
    offset_grad = diagonal_sums(jnp.sum(score_grad.astype(jnp.float32), axis=0))
    bias_grad = jnp.transpose(
        jnp.dot(offset_grad, jnp.transpose(onehot), precision=lax.Precision.HIGHEST)
    )
    return (query_grad, key_grad, value_grad, bias_grad)


def gated_unit(gate_values, up_values):
    return jax.nn.gelu(gate_values, approximate=True) * up_values


def shards(
    doc_tokens,
    query_tokens,
    doc_segments,
    query_keep,
    retrieved,
    positives,
    attn_gain,
    query_weight,
    key_weight,
    value_weight,
    output_weight,
    position_bias,
    ffn_gain,
    gate_weight,
    up_weight,
    down_weight,
    final_gain,
    proj_weight,
):
    tensor_size = lax.axis_size("mp")
    row_count, shard_len, width = doc_tokens.shape
    length = shard_len * tensor_size
    query_local, query_len = (query_tokens.shape[0], query_tokens.shape[1])
    query_group = query_local * tensor_size
    head_count = position_bias.shape[1]
    inner_width = query_weight.shape[1]
    hidden_local = gate_weight.shape[1]
    doc_local = retrieved.shape[2]
    docs_per_row = doc_local // row_count
    query_total = query_keep.shape[0]
    vector_width = proj_weight.shape[1]
    block_rows = min(512, length)
    doc_line = bucket_line(length, position_bias.shape[0], block_rows)
    query_line = bucket_line(query_len, position_bias.shape[0], query_len)
    bias_table = position_bias.astype(jnp.float32)
    doc_shape = (row_count, length)
    query_shape = (query_group, query_len)
    local_doc_shape = (row_count, shard_len)
    local_query_shape = (query_local, query_len)
    group_keep = lax.dynamic_slice_in_dim(
        query_keep, lax.axis_index("dp") * query_group, query_group, 0
    )
    doc_input = doc_tokens.astype(jnp.float32)
    query_input = query_tokens.astype(jnp.float32)
    gain_attn = attn_gain.astype(jnp.float32)
    gain_ffn = ffn_gain.astype(jnp.float32)
    gain_final = final_gain.astype(jnp.float32)
    doc_scale_attn = rms_scale(doc_input)
    query_scale_attn = rms_scale(query_input)
    doc_normed, query_normed = (
        lax.all_gather(
            (doc_input * doc_scale_attn * gain_attn).astype(jnp.bfloat16), "mp", axis=1, tiled=True
        ),
        lax.all_gather(
            (query_input * query_scale_attn * gain_attn).astype(jnp.bfloat16),
            "mp",
            axis=0,
            tiled=True,
        ),
    )
    normed_attn = joined(doc_normed, query_normed)
    projection_weight = jnp.concatenate([query_weight, key_weight, value_weight], axis=1)
    projected_heads = jnp.dot(
        normed_attn, projection_weight, preferred_element_type=jnp.float32
    ).astype(jnp.bfloat16)
    doc_heads, query_heads = parted(projected_heads, doc_shape, query_shape)
    doc_queries = split_heads(doc_heads, inner_width, head_count, 0)
    doc_keys = split_heads(doc_heads, inner_width, head_count, 1)
    doc_values = split_heads(doc_heads, inner_width, head_count, 2)
    group_queries = split_heads(query_heads, inner_width, head_count, 0)
    group_keys = split_heads(query_heads, inner_width, head_count, 1)
    group_values = split_heads(query_heads, inner_width, head_count, 2)
    doc_context, doc_log_totals = doc_attention(
        doc_queries, doc_keys, doc_values, doc_segments, bias_table, doc_line, block_rows
    )
    query_context, query_log_totals = query_attention(
        group_queries, group_keys, group_values, group_keep, bias_table, query_line
    )
    context = joined(doc_context, query_context)
    attn_partial = jnp.dot(context, output_weight, preferred_element_type=jnp.float32)
    doc_attn_part, query_attn_part = parted(attn_partial, doc_shape, query_shape)
    doc_attn, query_attn = (
        lax.psum_scatter(
            doc_attn_part.astype(jnp.bfloat16), "mp", scatter_dimension=1, tiled=True
        ).astype(jnp.float32),
        lax.psum_scatter(
            query_attn_part.astype(jnp.bfloat16), "mp", scatter_dimension=0, tiled=True
        ).astype(jnp.float32),
    )
    doc_mid = doc_input + doc_attn
    query_mid = query_input + query_attn
    doc_scale_ffn = rms_scale(doc_mid)
    query_scale_ffn = rms_scale(query_mid)
    doc_normed_ffn, request_rescaled_feedforward = (
        lax.all_gather(
            (doc_mid * doc_scale_ffn * gain_ffn).astype(jnp.bfloat16), "mp", axis=1, tiled=True
        ),
        lax.all_gather(
            (query_mid * query_scale_ffn * gain_ffn).astype(jnp.bfloat16), "mp", axis=0, tiled=True
        ),
    )
    normed_ffn = joined(doc_normed_ffn, request_rescaled_feedforward)
    gate_up_weight = jnp.concatenate([gate_weight, up_weight], axis=1)
    gate_up = jnp.dot(normed_ffn, gate_up_weight, preferred_element_type=jnp.float32)
    hidden_f32, gated_pullback = jax.vjp(
        gated_unit, gate_up[:, :hidden_local], gate_up[:, hidden_local:]
    )
    hidden = hidden_f32.astype(jnp.bfloat16)
    ffn_partial = jnp.dot(hidden, down_weight, preferred_element_type=jnp.float32)
    doc_ffn_part, query_ffn_part = parted(ffn_partial, doc_shape, query_shape)
    doc_ffn, query_ffn = (
        lax.psum_scatter(
            doc_ffn_part.astype(jnp.bfloat16), "mp", scatter_dimension=1, tiled=True
        ).astype(jnp.float32),
        lax.psum_scatter(
            query_ffn_part.astype(jnp.bfloat16), "mp", scatter_dimension=0, tiled=True
        ).astype(jnp.float32),
    )
    doc_out = doc_mid + doc_ffn
    query_out = query_mid + query_ffn
    doc_scale_final = rms_scale(doc_out)
    query_scale_final = rms_scale(query_out)
    final_normed = joined(
        (doc_out * doc_scale_final * gain_final).astype(jnp.bfloat16),
        (query_out * query_scale_final * gain_final).astype(jnp.bfloat16),
    )
    projected = jnp.dot(final_normed, proj_weight, preferred_element_type=jnp.float32)
    proj_scale = lax.rsqrt(jnp.sum(projected * projected, axis=-1, keepdims=True) + epsilon)
    unit_vectors = projected * proj_scale
    embedded = unit_vectors.astype(jnp.bfloat16)
    doc_token_count = row_count * shard_len
    doc_embedded = embedded[:doc_token_count]
    query_embedded = embedded[doc_token_count:].reshape(query_local, query_len, vector_width)
    all_queries = lax.all_gather(query_embedded, ("dp", "mp"), axis=0, tiled=True)
    query_flat = all_queries.reshape(query_total * query_len, vector_width)
    segment_shard = lax.dynamic_slice_in_dim(
        doc_segments, lax.axis_index("mp") * shard_len, shard_len, 1
    )
    doc_ids = (segment_shard + (jnp.arange(row_count) * docs_per_row)[:, None]).reshape(-1)
    member = (doc_ids[:, None] == jnp.arange(doc_local)[None, :]).astype(jnp.float32)
    block_queries = min(64, query_total)
    block_count = query_total // block_queries
    block_len = block_queries * query_len

    def block_sums(block_index):
        query_block = lax.dynamic_slice_in_dim(query_flat, block_index * block_len, block_len, 0)
        inner_products = right_dot(query_block, doc_embedded)
        return jnp.dot(
            jnp.exp(sharpness * (inner_products - 1.0)), member, precision=lax.Precision.HIGHEST
        )

    local_sums = lax.map(block_sums, jnp.arange(block_count)).reshape(
        query_total, query_len, doc_local
    )
    token_sums = lax.psum(local_sums.astype(jnp.bfloat16), "mp").astype(jnp.float32)
    smooth = 1.0 + jnp.log(token_sums) / sharpness
    chosen = (query_keep[:, :, None] * retrieved).astype(jnp.float32)
    counts = jnp.sum(chosen, axis=1)
    divisor = jnp.maximum(counts, 1.0)
    local_scores = jnp.sum(chosen * smooth, axis=1) / divisor
    whole_request_ratings, all_counts = (
        lax.all_gather(local_scores.astype(jnp.bfloat16), "dp", axis=1, tiled=True).astype(
            local_scores.dtype
        ),
        lax.all_gather(counts.astype(jnp.bfloat16), "dp", axis=1, tiled=True).astype(counts.dtype),
    )
    rating_energies = whole_request_ratings / smoothing_divisor
    largest = jnp.max(rating_energies, axis=1, keepdims=True)
    powered_scores = jnp.exp(rating_energies - largest)
    pooled_sum = jnp.sum(powered_scores, axis=1, keepdims=True)
    selected_mask = jnp.arange(whole_request_ratings.shape[1])[None, :] == positives[:, None]
    log_total = largest[:, 0] + jnp.log(pooled_sum[:, 0])
    picked = jnp.sum(jnp.where(selected_mask, rating_energies, 0.0), axis=1)
    loss_value = jnp.sum(log_total - picked) / query_total
    found_rows = jnp.sum(jnp.where(selected_mask, all_counts, 0.0), axis=1) > 0.5
    found_share = jnp.mean(found_rows.astype(jnp.float32))
    logit_gradient = (
        powered_scores / pooled_sum - selected_mask.astype(jnp.float32)
    ) / smoothing_divisor
    score_grad = lax.dynamic_slice_in_dim(
        logit_gradient, lax.axis_index("dp") * doc_local, doc_local, 1
    )
    sum_grad = (score_grad[:, None, :] * chosen / divisor[:, None, :] / token_sums).reshape(
        query_total * query_len, doc_local
    )

    def body_block_back(doc_accum, block_index):
        query_block = lax.dynamic_slice_in_dim(query_flat, block_index * block_len, block_len, 0)
        grad_block = lax.dynamic_slice_in_dim(sum_grad, block_index * block_len, block_len, 0)
        inner_products = right_dot(query_block, doc_embedded)
        spread = lax.dot_general(
            grad_block, member, (((1,), (1,)), ((), ())), precision=lax.Precision.HIGHEST
        )
        product_grad = (jnp.exp(sharpness * (inner_products - 1.0)) * spread).astype(jnp.bfloat16)
        query_part = jnp.dot(product_grad, doc_embedded, preferred_element_type=jnp.float32)
        return (doc_accum + left_dot(product_grad, query_block), query_part)

    doc_vector_grad, query_parts = lax.scan(
        body_block_back,
        jnp.zeros((doc_token_count, vector_width), jnp.float32),
        jnp.arange(block_count),
    )
    query_vector_grad = lax.psum_scatter(
        query_parts.reshape(query_total, query_len, vector_width),
        ("dp", "mp"),
        scatter_dimension=0,
        tiled=True,
    )
    embedded_grad = jnp.concatenate(
        [doc_vector_grad, query_vector_grad.reshape(-1, vector_width)], axis=0
    )
    projected_grad = (
        proj_scale
        * (
            embedded_grad
            - unit_vectors * jnp.sum(embedded_grad * unit_vectors, axis=-1, keepdims=True)
        )
    ).astype(jnp.bfloat16)
    proj_weight_grad = left_dot(final_normed, projected_grad)
    final_grad = right_dot(projected_grad, proj_weight)
    doc_final_grad, query_final_grad = parted(final_grad, local_doc_shape, local_query_shape)
    doc_out_grad, doc_final_gain = rms_back(doc_out, doc_scale_final, gain_final, doc_final_grad)
    query_out_grad, query_final_gain = rms_back(
        query_out, query_scale_final, gain_final, query_final_grad
    )
    final_gain_grad = doc_final_gain + query_final_gain
    doc_ffn_grad, query_ffn_grad = (
        lax.all_gather(doc_out_grad.astype(jnp.bfloat16), "mp", axis=1, tiled=True),
        lax.all_gather(query_out_grad.astype(jnp.bfloat16), "mp", axis=0, tiled=True),
    )
    ffn_out_grad = joined(doc_ffn_grad, query_ffn_grad)
    hidden_grad = right_dot(ffn_out_grad, down_weight)
    down_weight_grad = left_dot(hidden, ffn_out_grad)
    gate_grad, up_grad = gated_pullback(hidden_grad)
    gate_up_grad = jnp.concatenate([gate_grad, up_grad], axis=1).astype(jnp.bfloat16)
    gate_up_weight_grad = left_dot(normed_ffn, gate_up_grad)
    switch_matrix_derivative = gate_up_weight_grad[:, :hidden_local]
    up_weight_grad = gate_up_weight_grad[:, hidden_local:]
    normed_ffn_grad = right_dot(gate_up_grad, gate_up_weight)
    doc_nf_part, query_nf_part = parted(normed_ffn_grad, doc_shape, query_shape)
    doc_nf_grad, query_nf_grad = (
        lax.psum_scatter(
            doc_nf_part.astype(jnp.bfloat16), "mp", scatter_dimension=1, tiled=True
        ).astype(jnp.float32),
        lax.psum_scatter(
            query_nf_part.astype(jnp.bfloat16), "mp", scatter_dimension=0, tiled=True
        ).astype(jnp.float32),
    )
    doc_back_ffn, doc_ffn_gain = rms_back(doc_mid, doc_scale_ffn, gain_ffn, doc_nf_grad)
    query_back_ffn, query_ffn_gain = rms_back(query_mid, query_scale_ffn, gain_ffn, query_nf_grad)
    doc_mid_grad = doc_out_grad + doc_back_ffn
    query_mid_grad = query_out_grad + query_back_ffn
    ffn_gain_grad = doc_ffn_gain + query_ffn_gain
    doc_ao_grad, query_ao_grad = (
        lax.all_gather(doc_mid_grad.astype(jnp.bfloat16), "mp", axis=1, tiled=True),
        lax.all_gather(query_mid_grad.astype(jnp.bfloat16), "mp", axis=0, tiled=True),
    )
    attn_out_grad = joined(doc_ao_grad, query_ao_grad)
    output_weight_grad = left_dot(context, attn_out_grad)
    context_grad = right_dot(attn_out_grad, output_weight).astype(jnp.bfloat16)
    doc_context_grad, query_context_grad = parted(context_grad, doc_shape, query_shape)
    head_shape = (head_count, inner_width // head_count)
    doc_q_grad, doc_k_grad, doc_v_grad, doc_bias_grad = doc_attention_back(
        doc_queries,
        doc_keys,
        doc_values,
        doc_segments,
        bias_table,
        doc_line,
        block_rows,
        doc_log_totals,
        doc_context_grad.reshape(doc_shape + head_shape),
    )
    group_q_grad, group_k_grad, group_v_grad, group_bias_grad = query_attention_back(
        group_queries,
        group_keys,
        group_values,
        group_keep,
        bias_table,
        query_line,
        query_log_totals,
        query_context_grad.reshape(query_shape + head_shape),
    )
    position_bias_grad = doc_bias_grad + group_bias_grad
    doc_heads_grad = jnp.concatenate(
        [
            doc_q_grad.reshape(-1, inner_width),
            doc_k_grad.reshape(-1, inner_width),
            doc_v_grad.reshape(-1, inner_width),
        ],
        axis=1,
    )
    group_heads_grad = jnp.concatenate(
        [
            group_q_grad.reshape(-1, inner_width),
            group_k_grad.reshape(-1, inner_width),
            group_v_grad.reshape(-1, inner_width),
        ],
        axis=1,
    )
    heads_grad = jnp.concatenate([doc_heads_grad, group_heads_grad], axis=0).astype(jnp.bfloat16)
    projection_grad = left_dot(normed_attn, heads_grad)
    query_weight_grad = projection_grad[:, :inner_width]
    key_weight_grad = projection_grad[:, inner_width : 2 * inner_width]
    value_weight_grad = projection_grad[:, 2 * inner_width :]
    normed_attn_grad = right_dot(heads_grad, projection_weight)
    doc_na_part, query_na_part = parted(normed_attn_grad, doc_shape, query_shape)
    doc_na_grad, query_na_grad = (
        lax.psum_scatter(
            doc_na_part.astype(jnp.bfloat16), "mp", scatter_dimension=1, tiled=True
        ).astype(jnp.float32),
        lax.psum_scatter(
            query_na_part.astype(jnp.bfloat16), "mp", scatter_dimension=0, tiled=True
        ).astype(jnp.float32),
    )
    doc_back_attn, doc_attn_gain = rms_back(doc_input, doc_scale_attn, gain_attn, doc_na_grad)
    query_back_attn, query_attn_gain = rms_back(
        query_input, query_scale_attn, gain_attn, query_na_grad
    )
    doc_grad = doc_mid_grad + doc_back_attn
    query_grad = query_mid_grad + query_back_attn
    attn_gain_grad = doc_attn_gain + query_attn_gain
    (
        query_weight_grad,
        key_weight_grad,
        value_weight_grad,
        output_weight_grad,
        position_bias_grad,
        switch_matrix_derivative,
        up_weight_grad,
        down_weight_grad,
    ) = lax.psum(
        (
            query_weight_grad,
            key_weight_grad,
            value_weight_grad,
            output_weight_grad,
            position_bias_grad,
            switch_matrix_derivative,
            up_weight_grad,
            down_weight_grad,
        ),
        "dp",
    )
    attn_gain_grad, ffn_gain_grad, final_gain_grad, proj_weight_grad = lax.psum(
        (attn_gain_grad, ffn_gain_grad, final_gain_grad, proj_weight_grad), ("dp", "mp")
    )
    return (
        loss_value,
        found_share,
        doc_grad,
        query_grad,
        attn_gain_grad,
        query_weight_grad,
        key_weight_grad,
        value_weight_grad,
        output_weight_grad,
        position_bias_grad,
        ffn_gain_grad,
        switch_matrix_derivative,
        up_weight_grad,
        down_weight_grad,
        final_gain_grad,
        proj_weight_grad,
    )


def solution(mesh):
    placed = (
        P("dp", "mp", None),
        P(("dp", "mp"), None, None),
        P("dp", None),
        P(),
        P(None, None, "dp"),
        P(),
        P(),
        P(None, "mp"),
        P(None, "mp"),
        P(None, "mp"),
        P("mp", None),
        P(None, "mp"),
        P(),
        P(None, "mp"),
        P(None, "mp"),
        P("mp", None),
        P(),
        P(),
    )
    return jax.shard_map(
        shards,
        mesh=mesh,
        in_specs=placed,
        out_specs=(
            P(),
            P(),
            P("dp", "mp", None),
            P(("dp", "mp"), None, None),
            P(),
            P(None, "mp"),
            P(None, "mp"),
            P(None, "mp"),
            P("mp", None),
            P(None, "mp"),
            P(),
            P(None, "mp"),
            P(None, "mp"),
            P("mp", None),
            P(),
            P(),
        ),
        check_vma=False,
    )
```

profile of v0, /device:TPU:0, one launch (start us, length us, event | category | flops | bytes accessed | tf_op | source)
XLA Modules:
  0.0 1583.0 jit_solution(16501098510128393461)
XLA Ops:
  17.8 15.9 %reshape.598 = f32[2360832]{0:T(1024)} reshape(f32[3,512,1537]{2,1,0:T(8,128)} %broadcast_in_dim.128) | data formatting | bytes 18886656
  74.3 16.0 %reshape.600 = f32[2360832]{0:T(1024)} reshape(f32[3,512,1537]{2,1,0:T(8,128)} %broadcast_in_dim.127) | data formatting | bytes 18886656
  184.1 50.0 %while.43 = (s32[]{:T(128)}, bf16[4,512,3,64]{1,3,2,0:T(8,128)(2,1)}, f32[4,3,512]{2,1,0:T(4,128)}, s32[4]{0:T(128)S(1)}, bf16[2,1024,3,64]{1,3,2,0:T(8,128)(2,1...) while((s32[]{:T(128)}, ...), condition=%wide.region_5.6_spmd, body=%wide.region_2.5_spmd.sunk | while | flops 415857184 | bytes 27468304 | solution.py:153
  243.6 37.1 %reduce-scatter.10.cloned.1.call-done = bf16[2,256,768]{2,1,0:T(8,128)(2,1)} async-done(((bf16[2,1024,768]{2,1,0:T(8,128)(2,1)}), bf16[2,256,768]{2,1,0:T(8,128)(2,1)}) %reduce-scatter.10.cloned.1.call-update) | async-done | bytes 786448 | tf_op jit(solution)/shard_map/reduce_scatter | solution.py:403
  287.1 17.7 %reduce-scatter.12.cloned.1.call-done = bf16[2,32,768]{2,1,0:T(8,128)(2,1)} async-done(((bf16[8,32,768]{2,1,0:T(8,128)(2,1)}), bf16[2,32,768]{2,1,0:T(8,128)(2,1)}) %reduce-scatter.12.cloned.1.call-update) | async-done | bytes 98320 | tf_op jit(solution)/shard_map/reduce_scatter | solution.py:406
  314.0 21.5 %all-gather.7.cloned.1.call-done = bf16[2,1024,768]{2,1,0:T(8,128)(2,1)} async-done(((bf16[2,256,768]{2,1,0:T(8,128)(2,1)}), bf16[2,1024,768]{2,1,0:T(8,128)(2,1)}) %all-gather.7.cloned.1.call-update) | async-done | bytes 3145744 | tf_op jit(solution)/shard_map/all_gather | solution.py:415
  355.3 16.0 %reduce-scatter.16.cloned.1.call-done = bf16[2,32,768]{2,1,0:T(8,128)(2,1)} async-done(((bf16[8,32,768]{2,1,0:T(8,128)(2,1)}), bf16[2,32,768]{2,1,0:T(8,128)(2,1)}) %reduce-scatter.16.cloned.1.call-update) | async-done | bytes 98320 | tf_op jit(solution)/shard_map/reduce_scatter | solution.py:435
  373.9 38.0 %reduce-scatter.14.cloned.1.call-done = bf16[2,256,768]{2,1,0:T(8,128)(2,1)} async-done(((bf16[2,1024,768]{2,1,0:T(8,128)(2,1)}), bf16[2,256,768]{2,1,0:T(8,128)(2,1)}) %reduce-scatter.14.cloned.1.call-update) | async-done | bytes 786448 | tf_op jit(solution)/shard_map/reduce_scatter | solution.py:432
  416.3 42.1 %all_gather.37 = bf16[64,32,128]{2,1,0:T(8,128)(2,1)S(1)} all-gather(bf16[2,32,128]{2,1,0:T(8,128)(2,1)S(1)} %bitcast.368), channel_id=1, replica_groups=mesh['dp'=8,'mp'=4] {'dp','mp'}, dimensions={0}, use_global_device_ids=true | all-gather | bytes 540672 | tf_op jit(solution)/shard_map/all_gather | solution.py:454
  475.9 26.0 %all_gather.38 = bf16[64,64]{0,1:T(8,128)(2,1)S(1)} all-gather(bf16[64,8]{0,1:T(8,128)(2,1)S(1)} %get-tuple-element.584), channel_id=1, replica_groups=mesh['dp'=8,'mp'=4] {'dp'}, dimensions={1}, use_global_device_ids=true | all-gather | bytes 9216 | tf_op jit(solution)/shard_map/all_gather | solution.py:482
  501.9 26.0 %all_gather.39 = bf16[64,64]{0,1:T(8,128)(2,1)S(1)} all-gather(bf16[64,8]{0,1:T(8,128)(2,1)S(1)} %get-tuple-element.585), channel_id=1, replica_groups=mesh['dp'=8,'mp'=4] {'dp'}, dimensions={1}, use_global_device_ids=true | all-gather | bytes 9216 | tf_op jit(solution)/shard_map/all_gather | solution.py:485
  538.9 129.9 %reduce-scatter.18.cloned.1.call-done = f32[2,32,128]{2,1,0:T(8,128)} async-done(((f32[64,32,128]{2,1,0:T(8,128)}), f32[2,32,128]{2,1,0:T(8,128)}) %reduce-scatter.18.cloned.1.call-update) | async-done | bytes 32784 | tf_op jit(solution)/shard_map/reduce_scatter | solution.py:523
  722.2 35.1 %reduce-scatter.20.cloned.1.call-done = bf16[2,256,768]{2,1,0:T(8,128)(2,1)} async-done(((bf16[2,1024,768]{2,1,0:T(8,128)(2,1)}), bf16[2,256,768]{2,1,0:T(8,128)(2,1)}) %reduce-scatter.20.cloned.1.call-update) | async-done | bytes 786448 | tf_op jit(solution)/shard_map/reduce_scatter | solution.py:562
  764.7 16.4 %reduce-scatter.22.cloned.1.call-done = bf16[2,32,768]{2,1,0:T(8,128)(2,1)} async-done(((bf16[8,32,768]{2,1,0:T(8,128)(2,1)}), bf16[2,32,768]{2,1,0:T(8,128)(2,1)}) %reduce-scatter.22.cloned.1.call-update) | async-done | bytes 98320 | tf_op jit(solution)/shard_map/reduce_scatter | solution.py:565
  790.0 21.8 %all-gather.11.cloned.1.call-done = bf16[2,1024,768]{2,1,0:T(8,128)(2,1)} async-done(((bf16[2,256,768]{2,1,0:T(8,128)(2,1)}), bf16[2,1024,768]{2,1,0:T(8,128)(2,1)}) %all-gather.11.cloned.1.call-update) | async-done | bytes 3145744 | tf_op jit(solution)/shard_map/all_gather | solution.py:575
  822.9 282.9 %while.44 = (s32[]{:T(128)}, f32[2,1024,3,64]{1,3,2,0:T(8,128)}, f32[2,1024,3,64]{1,3,2,0:T(8,128)}, f32[2,3,1537]{2,1,0:T(4,128)S(1)}, bf16[4,512,3,64]{1,3,2,0...) while((s32[]{:T(128)}, f32[2,1024,3,64]{1,3,2,0:T(8,128)}, ...), condition=%wide.region_37.38_spmd, body=%wide.region_34.37_spmd.sunk | while | flops 1026426368 | bytes 170316624 | solution.py:239
  872.7 16.4 %reshape.607 = f32[3,512,1537]{2,1,0:T(8,128)} reshape(f32[2360832]{0:T(1024)} %reshape.606) | data formatting | bytes 18886656 | tf_op jit(solution)/shard_map/while/body/eval_jaxpr/reshape | solution.py:56
  943.3 16.4 %reshape.607 = f32[3,512,1537]{2,1,0:T(8,128)} reshape(f32[2360832]{0:T(1024)} %reshape.606) | data formatting | bytes 18886656 | tf_op jit(solution)/shard_map/while/body/eval_jaxpr/reshape | solution.py:56
  1013.9 16.4 %reshape.607 = f32[3,512,1537]{2,1,0:T(8,128)} reshape(f32[2360832]{0:T(1024)} %reshape.606) | data formatting | bytes 18886656 | tf_op jit(solution)/shard_map/while/body/eval_jaxpr/reshape | solution.py:56
  1084.4 16.4 %reshape.607 = f32[3,512,1537]{2,1,0:T(8,128)} reshape(f32[2360832]{0:T(1024)} %reshape.606) | data formatting | bytes 18886656 | tf_op jit(solution)/shard_map/while/body/eval_jaxpr/reshape | solution.py:56
  1169.4 22.1 %psum.97 = f32[32,3]{0,1:T(4,128)} all-reduce(f32[32,3]{0,1:T(4,128)} %convolution_add_fusion.1), channel_id=1, replica_groups=mesh['dp'=8,'mp'=4] {'dp'}, use_global_device_ids=true, to_apply=%region_52.53 | all-reduce | flops 96 | bytes 768 | tf_op jit(solution)/shard_map/psum | solution.py:652
  1197.5 37.2 %all-reduce.6 = (f32[768]{0:T(1024)}, f32[768]{0:T(1024)}, f32[768]{0:T(1024)}) all-reduce(f32[768]{0:T(1024)S(1)} %add.473, f32[768]{0:T(1024)} %add.475, f32[768]{0:T(1024)} %add.476), channel_id=1, replica_groups=mesh['dp'=8,'mp'=4] {'dp','mp'}, use_global_device_ids=true, to_apply=%region_45.46 | all-reduce | flops 2304 | bytes 18432 | tf_op jit(solution)/shard_map/psum | solution.py:665
  1238.3 81.2 %all-reduce.11.cloned.1.call-done = f32[768,128]{1,0:T(8,128)} async-done(((f32[768,128]{1,0:T(8,128)}), f32[768,128]{1,0:T(8,128)}) %all-reduce.11.cloned.1.call-update) | async-done | bytes 393232 | tf_op jit(solution)/shard_map/psum | solution.py:665
  1319.5 243.6 %all-reduce.13.cloned.1.call-done = (f32[768,192]{0,1:T(8,128)}, f32[768,192]{0,1:T(8,128)}, f32[768,192]{0,1:T(8,128)}, f32[192,768]{1,0:T(8,128)}, f32[768,512...) async-done(((f32[768,192]{0,1:T(8,128)}, f32[768,192]{0,1:T(8,128)}, f32[768,192]{0,1:T(8,128)}, f32[192,768]{1,0:T(8,128)}, f32[768,512]{1,0:T(8,128)}, ...) | async-done | bytes 7077904 | tf_op jit(solution)/shard_map/psum | solution.py:652
  (628 shorter events, 627.5 us)
Async XLA Ops:
  7.2 338.5 %copy-start = (bf16[512,768]{1,0:T(8,128)(2,1)S(1)}, bf16[512,768]{1,0:T(8,128)(2,1)}, u32[]{:S(2)}) copy-start(bf16[512,768]{1,0:T(8,128)(2,1)} %param.39) | copy-start | bytes 2359300
  7.2 151.7 %all-gather.5.cloned.1.call-start = ((), (), s32[]{:S(2)}) async-start(), calls=%async_computation.9 | async-start | bytes 3932160 | tf_op jit(solution)/shard_map/all_gather | solution.py:371
  10.0 116.8 %copy-start.81 = (f32[768]{0:T(1024)}, f32[768]{0:T(1024)S(1)}, u32[]{:S(2)}) copy-start(f32[768]{0:T(1024)S(1)} %convert_element_type.240) | copy-start | bytes 9220
  12.3 268.5 %reduce-scatter.10.cloned.1.call-start = ((), (), s32[]{:S(2)}) async-start(), calls=%async_computation.10 | async-start | bytes 3932160 | tf_op jit(solution)/shard_map/reduce_scatter | solution.py:403
  241.6 63.2 %reduce-scatter.12.cloned.1.call-start = ((), (), s32[]{:S(2)}) async-start(), calls=%async_computation.12 | async-start | bytes 491520 | tf_op jit(solution)/shard_map/reduce_scatter | solution.py:406
  243.5 91.9 %all-gather.7.cloned.1.call-start = ((), (), s32[]{:S(2)}) async-start(), calls=%async_computation.11 | async-start | bytes 3932160 | tf_op jit(solution)/shard_map/all_gather | solution.py:415
  243.6 539.1 %copy-start.74 = (f32[768]{0:T(1024)}, f32[768]{0:T(1024)S(1)}, u32[]{:S(2)}) copy-start(f32[768]{0:T(1024)S(1)} %convert_element_type.250) | copy-start | bytes 9220
  285.2 86.1 %reduce-scatter.16.cloned.1.call-start = ((), (), s32[]{:S(2)}) async-start(), calls=%async_computation.14 | async-start | bytes 491520 | tf_op jit(solution)/shard_map/reduce_scatter | solution.py:435
  350.3 61.5 %reduce-scatter.14.cloned.1.call-start = ((), (), s32[]{:S(2)}) async-start(), calls=%async_computation.13 | async-start | bytes 3932160 | tf_op jit(solution)/shard_map/reduce_scatter | solution.py:432
  354.2 57.6 %copy-start.6 = (bf16[2,256,768]{2,1,0:T(8,128)(2,1)S(1)}, bf16[2,256,768]{2,1,0:T(8,128)(2,1)}, u32[]{:S(2)}) copy-start(bf16[2,256,768]{2,1,0:T(8,128)(2,1)} %reduce-scatter.10.cloned.1.call-done) | copy-start | bytes 2359300
  354.2 314.6 %reduce-scatter.18.cloned.1.call-start = ((), (), s32[]{:S(2)}) async-start(), calls=%async_computation.15 | async-start | bytes 1081344 | tf_op jit(solution)/shard_map/reduce_scatter | solution.py:523
  355.1 427.6 %copy-start.64 = (f32[768]{0:T(1024)}, f32[768]{0:T(1024)S(1)}, u32[]{:S(2)}) copy-start(f32[768]{0:T(1024)S(1)} %convert_element_type.258) | copy-start | bytes 9220
  355.3 60.3 %copy-start.83 = (bf16[768,128]{1,0:T(8,128)(2,1)S(1)}, bf16[768,128]{1,0:T(8,128)(2,1)}, u32[]{:S(2)}) copy-start(bf16[768,128]{1,0:T(8,128)(2,1)} %param.41) | copy-start | bytes 589828
  536.5 165.6 %all-gather.9.cloned.1.call-start = ((), (), s32[]{:S(2)}) async-start(), calls=%async_computation.16 | async-start | bytes 3932160 | tf_op jit(solution)/shard_map/all_gather | solution.py:548
  672.9 109.8 %copy-start.4 = (f32[576,768]{1,0:T(8,128)}, f32[576,768]{1,0:T(8,128)S(1)}, u32[]{:S(2)}) copy-start(f32[576,768]{1,0:T(8,128)S(1)} %fusion.173) | copy-start | bytes 5308420
  676.4 80.9 %reduce-scatter.20.cloned.1.call-start = ((), (), s32[]{:S(2)}) async-start(), calls=%async_computation.17 | async-start | bytes 3932160 | tf_op jit(solution)/shard_map/reduce_scatter | solution.py:562
  720.2 60.8 %reduce-scatter.22.cloned.1.call-start = ((), (), s32[]{:S(2)}) async-start(), calls=%async_computation.19 | async-start | bytes 491520 | tf_op jit(solution)/shard_map/reduce_scatter | solution.py:565
  722.1 89.6 %all-gather.11.cloned.1.call-start = ((), (), s32[]{:S(2)}) async-start(), calls=%async_computation.18 | async-start | bytes 3932160 | tf_op jit(solution)/shard_map/all_gather | solution.py:575
  763.3 428.2 %reduce-scatter.26.cloned.1.call-start = ((), (), s32[]{:S(2)}) async-start(), calls=%async_computation.21 | async-start | bytes 491520 | tf_op jit(solution)/shard_map/reduce_scatter | solution.py:632
  1124.4 70.6 %reduce-scatter.24.cloned.1.call-start = ((), (), s32[]{:S(2)}) async-start(), calls=%async_computation.20 | async-start | bytes 3932160 | tf_op jit(solution)/shard_map/reduce_scatter | solution.py:629
  1128.3 191.2 %all-reduce.11.cloned.1.call-start = ((), (), s32[]{:S(2)}) async-start(), calls=%async_computation.22 | async-start | bytes 786432 | tf_op jit(solution)/shard_map/psum | solution.py:665
  1130.7 432.4 %all-reduce.13.cloned.1.call-start = ((), (), s32[]{:S(2)}) async-start(), calls=%async_computation.23 | async-start | bytes 14155776 | tf_op jit(solution)/shard_map/psum | solution.py:652
  1150.2 84.5 %copy-start.9 = (bf16[2,256,768]{2,1,0:T(8,128)(2,1)S(1)}, bf16[2,256,768]{2,1,0:T(8,128)(2,1)}, u32[]{:S(2)}) copy-start(bf16[2,256,768]{2,1,0:T(8,128)(2,1)} %reduce-scatter.10.cloned.1.call-done) | copy-start | bytes 2359300
  1150.2 84.5 %copy-start.95 = (f32[2,256]{1,0:T(2,128)S(1)}, f32[2,256]{1,0:T(2,128)}, u32[]{:S(2)}) copy-start(f32[2,256]{1,0:T(2,128)} %copy-done.93) | copy-start | bytes 6148
  (137 other events, 1247.6 us)
Sparse Core Ops, SparseCore 0:
  12.4 31.2 all-gather.4
  241.7 39.0 reduce-scatter.9
  284.0 20.7 reduce-scatter.11
  306.9 28.5 all-gather.6
  350.4 20.8 reduce-scatter.15
  373.8 37.9 reduce-scatter.13
  536.6 132.1 reduce-scatter.17
  676.6 25.4 all-gather.8
  720.4 36.9 reduce-scatter.19
  760.2 20.7 reduce-scatter.21
  783.2 28.5 all-gather.10
  1124.5 20.7 reduce-scatter.25
  1147.9 37.9 reduce-scatter.23
  1191.9 127.5 all-reduce.10
  1325.8 237.1 all-reduce.12
where the time goes:
time: 1600 us; the launch traced here: 1580 us
  waiting for transfers between devices  672 us (42%)
  local copies, waits for them, and re-layouts  388 us (24%)
  blocking collectives  195 us (12%)
  matrix products  158 us (10%)
  other arithmetic  123 us (8%)
  loops' own time  27 us (2%)
  between operations  19.1 us (1%)
    psum x1, waiting for transfers between devices, shards(): lax.psum((query_weight_grad, key_weight_grad, value_weight_grad, output_w...  244 us
    reduce_scatter x1, waiting for transfers between devices, shards(): lax.psum_scatter(query_parts.reshape(query_total, query_len, vector_width...  130 us
    while x68, local copies, waits for them, and re-layouts  92.3 us
    unnamed x260, local copies, waits for them, and re-layouts  87.6 us
    psum x1, waiting for transfers between devices, shards(): lax.psum((attn_gain_grad, ffn_gain_grad, final_gain_grad, proj_weight_gra...  81.2 us
    reshape x5, local copies, waits for them, and re-layouts, diagonal_sums(): jnp.pad(padded, ((0, 0), (0, block_rows)))  67.2 us
    all_gather x1, blocking collectives, shards(): lax.all_gather(query_embedded, ('dp', 'mp'), axis=0, tiled=True)  42.1 us
    reduce_scatter x1, waiting for transfers between devices, shards(): lax.psum_scatter(doc_ffn_part.astype(jnp.bfloat16), 'mp', scatter_dimensi...  38 us
  transfers between devices with their start and end apart: 15, of which 12 were waited for; matrix products, arithmetic and copies ran while one was open for 14% of the time, Pallas kernels for 0%

commit v1 on v0

v1 whole, which is shorter than its diff:
```python
from functools import partial

import jax
import jax.numpy as jnp
import numpy as np
from jax import lax
from jax.experimental import pallas as pl
from jax.experimental.pallas import tpu as pltpu
from jax.sharding import PartitionSpec as P

epsilon = 1e-06
sharpness = 16.0
smoothing_divisor = 0.05
masked_score = -1e30
BLOCK = 128
PAIR = 2 * BLOCK
bf16 = jnp.bfloat16
f32 = jnp.float32


def bucket_starts(buckets):
    half = buckets // 2
    exact = half // 2
    distance = np.arange(0, 2048)
    scaled = (
        np.log(np.maximum(distance, 1) / exact) / np.log(128.0 / exact) * (half - exact)
    )
    far = np.minimum(exact + np.floor(np.maximum(scaled, 0.0)), half - 1)
    bucket = np.where(distance < exact, distance, far)
    return [int(np.argmax(bucket >= b)) for b in range(half)]


def dot_nn(a, b):
    return lax.dot_general(a, b, (((1,), (0,)), ((), ())), preferred_element_type=f32)


def dot_nt(a, b):
    return lax.dot_general(a, b, (((1,), (1,)), ((), ())), preferred_element_type=f32)


def dot_tn(a, b):
    return lax.dot_general(a, b, (((0,), (0,)), ((), ())), preferred_element_type=f32)


def dot_exact(a, b):
    return lax.dot_general(
        a, b, (((1,), (0,)), ((), ())), precision=lax.Precision.HIGHEST, preferred_element_type=f32
    )


def params(limit_mib=40):
    return pltpu.CompilerParams(vmem_limit_bytes=limit_mib << 20)


def bias_kernel(starts, heads, tab_ref, t_ref, tt_ref):
    half = len(starts)
    sub = lax.broadcasted_iota(jnp.int32, (BLOCK, BLOCK), 0)
    lane = lax.broadcasted_iota(jnp.int32, (BLOCK, BLOCK), 1)
    for ref, base in ((t_ref, lane - sub), (tt_ref, sub - lane)):
        for d in (-1, 0, 1):
            offset = base + BLOCK * d
            n = jnp.abs(offset)
            for h in range(heads):
                low = high = None
                if d <= 0:
                    low = jnp.full((BLOCK, BLOCK), tab_ref[0, h], f32)
                    for b in range(1, half):
                        low = jnp.where(n >= starts[b], tab_ref[b, h], low)
                if d >= 0:
                    high = jnp.full((BLOCK, BLOCK), tab_ref[half, h], f32)
                    for b in range(1, half):
                        high = jnp.where(n >= starts[b], tab_ref[half + b, h], high)
                if d < 0:
                    tile = low
                elif d > 0:
                    tile = high
                else:
                    tile = jnp.where(offset > 0, high, low)
                ref[h, d + 2] = tile
        for h in range(heads):
            ref[h, 0] = jnp.full((BLOCK, BLOCK), tab_ref[half - 1, h], f32)
            ref[h, 4] = jnp.full((BLOCK, BLOCK), tab_ref[2 * half - 1, h], f32)


def bias_tiles(table):
    buckets, heads = table.shape
    starts = bucket_starts(buckets)
    shape = jax.ShapeDtypeStruct((heads, 5, BLOCK, BLOCK), f32)
    return pl.pallas_call(
        partial(bias_kernel, starts, heads),
        in_specs=[pl.BlockSpec(memory_space=pltpu.SMEM)],
        out_shape=(shape, shape),
        compiler_params=params(),
        name="bias_tiles",
    )(table)


def clipped(d):
    return jnp.minimum(jnp.maximum(d, -2), 2) + 2


def attend_kernel(heads, size, lo_ref, cnt_ref, qkv_ref, segq_ref, segk_ref, t_ref, ctx_ref, lse_ref, k_s, v_s, s_s):
    b = pl.program_id(0)
    inner = heads * size

    @pl.when(b == 0)
    def _():
        for h in range(heads):
            k_s[h] = qkv_ref[:, inner + h * size : inner + (h + 1) * size]
            v_s[h] = qkv_ref[:, 2 * inner + h * size : 2 * inner + (h + 1) * size]

    rows = pl.multiple_of(b * BLOCK, BLOCK)
    block = qkv_ref[pl.ds(rows, BLOCK), :inner]
    queries = [block[:, h * size : (h + 1) * size] for h in range(heads)]
    seg_col = segq_ref[...]
    lo = lo_ref[b]
    cnt = cnt_ref[b]

    def first(i, tops):
        at = lo + 2 * i
        start = pl.multiple_of(at * BLOCK, BLOCK)
        allowed = seg_col == segk_ref[:, pl.ds(start, PAIR)]
        i0 = clipped(at - b)
        i1 = clipped(at + 1 - b)
        out = []
        for h in range(heads):
            s = dot_nt(queries[h], k_s[h, pl.ds(start, PAIR), :])
            s0 = jnp.where(allowed[:, :BLOCK], s[:, :BLOCK] + t_ref[h, i0], masked_score)
            s1 = jnp.where(allowed[:, BLOCK:], s[:, BLOCK:] + t_ref[h, i1], masked_score)
            s_s[h, i, :, :BLOCK] = s0
            s_s[h, i, :, BLOCK:] = s1
            out.append(jnp.maximum(tops[h], jnp.maximum(s0, s1)))
        return tuple(out)

    tops = lax.fori_loop(
        0, cnt, first, tuple(jnp.full((BLOCK, BLOCK), masked_score, f32) for _ in range(heads))
    )
    largest = [
        jnp.broadcast_to(jnp.max(top, axis=1, keepdims=True), (BLOCK, BLOCK)) for top in tops
    ]

    def second(i, carry):
        at = lo + 2 * i
        start = pl.multiple_of(at * BLOCK, BLOCK)
        sums, accs = carry
        new_sums, new_accs = [], []
        for h in range(heads):
            p0 = jnp.exp(s_s[h, i, :, :BLOCK] - largest[h])
            p1 = jnp.exp(s_s[h, i, :, BLOCK:] - largest[h])
            new_sums.append(sums[h] + (p0 + p1))
            p = jnp.concatenate([p0.astype(bf16), p1.astype(bf16)], axis=1)
            new_accs.append(accs[h] + dot_nn(p, v_s[h, pl.ds(start, PAIR), :]))
        return (tuple(new_sums), tuple(new_accs))

    sums, accs = lax.fori_loop(
        0,
        cnt,
        second,
        (
            tuple(jnp.zeros((BLOCK, BLOCK), f32) for _ in range(heads)),
            tuple(jnp.zeros((BLOCK, size), f32) for _ in range(heads)),
        ),
    )
    outs = []
    for h in range(heads):
        total = jnp.sum(sums[h], axis=1, keepdims=True)
        outs.append((accs[h] / total).astype(bf16))
        lse = largest[h] + jnp.log(jnp.broadcast_to(total, (BLOCK, BLOCK)))
        lse_ref[h : h + 1, :] = jnp.transpose(lse)[0:1, :]
    ctx_ref[...] = jnp.concatenate(outs, axis=1)


def attend(qkv, ranges, segs, tiles):
    lo, cnt = ranges
    segq_col, segq_row, segk_col, segk_row = segs
    total, wide = qkv.shape
    heads = tiles.shape[0]
    inner = wide // 3
    size = inner // heads
    blocks = total // BLOCK
    flops = 4 * total * total * inner // 2
    return pl.pallas_call(
        partial(attend_kernel, heads, size),
        grid_spec=pltpu.PrefetchScalarGridSpec(
            num_scalar_prefetch=2,
            grid=(blocks,),
            in_specs=[
                pl.BlockSpec((total, wide), lambda b, *_: (0, 0)),
                pl.BlockSpec((BLOCK, 1), lambda b, *_: (b, 0)),
                pl.BlockSpec((1, total), lambda b, *_: (0, 0)),
                pl.BlockSpec((heads, 5, BLOCK, BLOCK), lambda b, *_: (0, 0, 0, 0)),
            ],
            out_specs=[
                pl.BlockSpec((BLOCK, inner), lambda b, *_: (b, 0)),
                pl.BlockSpec((8, BLOCK), lambda b, *_: (0, b)),
            ],
            scratch_shapes=[
                pltpu.VMEM((heads, total, size), bf16),
                pltpu.VMEM((heads, total, size), bf16),
                pltpu.VMEM((heads, blocks // 2 + 1, BLOCK, PAIR), f32),
            ],
        ),
        out_shape=(
            jax.ShapeDtypeStruct((total, inner), bf16),
            jax.ShapeDtypeStruct((8, total), f32),
        ),
        compiler_params=params(),
        cost_estimate=pl.CostEstimate(
            flops=flops, transcendentals=total * total * heads // 2, bytes_accessed=4 << 20
        ),
        name="attend",
    )(lo, cnt, qkv, segq_col, segk_row, tiles)


def attend_back_kernel(
    starts,
    heads,
    size,
    lo_ref,
    cnt_ref,
    qkv_ref,
    do_ref,
    ctx_ref,
    lse_ref,
    segk_ref,
    segq_ref,
    tt_ref,
    grad_ref,
    bias_ref,
    q_s,
    do_s,
    dq_s,
    delta_s,
    d_s,
):
    b = pl.program_id(0)
    inner = heads * size
    total = qkv_ref.shape[0]
    half = len(starts)

    @pl.when(b == 0)
    def _():
        prod = do_ref[...].astype(f32) * ctx_ref[...].astype(f32)
        high = prod.astype(bf16)
        low = (prod - high.astype(f32)).astype(bf16)
        row = lax.broadcasted_iota(jnp.int32, (8, inner), 0)
        col = lax.broadcasted_iota(jnp.int32, (8, inner), 1)
        pick = ((col >= row * size) & (col < (row + 1) * size)).astype(f32).astype(bf16)
        delta_s[...] = dot_nt(pick, high) + dot_nt(pick, low)
        for h in range(heads):
            q_s[h] = qkv_ref[:, h * size : (h + 1) * size]
            do_s[h] = do_ref[:, h * size : (h + 1) * size]
        dq_s[...] = jnp.zeros(dq_s.shape, f32)
        d_s[...] = jnp.zeros(d_s.shape, f32)

    rows = pl.multiple_of(b * BLOCK, BLOCK)
    block = qkv_ref[pl.ds(rows, BLOCK), :]
    keys = [block[:, inner + h * size : inner + (h + 1) * size] for h in range(heads)]
    values = [block[:, 2 * inner + h * size : 2 * inner + (h + 1) * size] for h in range(heads)]
    seg_col = segk_ref[...]
    lo = lo_ref[b]
    cnt = cnt_ref[b]

    def step(i, carry):
        dks, dvs = carry
        at = lo + 2 * i
        start = pl.multiple_of(at * BLOCK, BLOCK)
        allowed = seg_col == segq_ref[:, pl.ds(start, PAIR)]
        i0 = clipped(b - at)
        i1 = clipped(b - at - 1)
        new_k, new_v = [], []
        for h in range(heads):
            q = q_s[h, pl.ds(start, PAIR), :]
            do = do_s[h, pl.ds(start, PAIR), :]
            s = dot_nt(keys[h], q)
            dp = dot_nt(values[h], do)
            bias = jnp.concatenate([tt_ref[h, i0], tt_ref[h, i1]], axis=1)
            lse = lse_ref[h : h + 1, pl.ds(start, PAIR)]
            delta = delta_s[h : h + 1, pl.ds(start, PAIR)]
            p = jnp.where(allowed, jnp.exp(s + bias - lse), 0.0)
            ds = p * (dp - delta)
            d_s[h, i0] += ds[:, :BLOCK]
            d_s[h, i1] += ds[:, BLOCK:]
            ds16 = ds.astype(bf16)
            new_v.append(dvs[h] + dot_nn(p.astype(bf16), do))
            new_k.append(dks[h] + dot_nn(ds16, q))
            dq_s[h, pl.ds(start, PAIR), :] += dot_tn(ds16, keys[h])
        return (tuple(new_k), tuple(new_v))

    zero = tuple(jnp.zeros((BLOCK, size), f32) for _ in range(heads))
    dks, dvs = lax.fori_loop(0, cnt, step, (zero, zero))
    grad_ref[pl.ds(rows, BLOCK), inner : 2 * inner] = jnp.concatenate(dks, axis=1).astype(bf16)
    grad_ref[pl.ds(rows, BLOCK), 2 * inner :] = jnp.concatenate(dvs, axis=1).astype(bf16)

    @pl.when(b == pl.num_programs(0) - 1)
    def _():
        grad_ref[:, :inner] = jnp.concatenate([dq_s[h] for h in range(heads)], axis=1).astype(bf16)
        sub = lax.broadcasted_iota(jnp.int32, (BLOCK, BLOCK), 0)
        lane = lax.broadcasted_iota(jnp.int32, (BLOCK, BLOCK), 1)
        ids = {}
        for d in (-1, 0, 1):
            offset = sub - lane + BLOCK * d
            n = jnp.abs(offset)
            bucket = jnp.zeros((BLOCK, BLOCK), jnp.int32)
            for e in range(1, half):
                bucket = jnp.where(n >= starts[e], e, bucket)
            ids[d] = jnp.where(offset > 0, bucket + half, bucket)
        for h in range(heads):
            for e in range(2 * half):
                parts = []
                for d in (-1, 0, 1):
                    if (d < 0 and e >= half) or (d > 0 and e < half):
                        continue
                    parts.append(jnp.where(ids[d] == e, d_s[h, d + 2], 0.0))
                if e == half - 1:
                    parts.append(d_s[h, 0])
                if e == 2 * half - 1:
                    parts.append(d_s[h, 4])
                whole = parts[0]
                for part in parts[1:]:
                    whole = whole + part
                bias_ref[h, e : e + 1, :] = jnp.sum(whole, axis=0, keepdims=True)


def attend_back(qkv, context_grad, context, lse, ranges, segs, tiles, buckets):
    lo, cnt = ranges
    segq_col, segq_row, segk_col, segk_row = segs
    total, wide = qkv.shape
    heads = tiles.shape[0]
    inner = wide // 3
    size = inner // heads
    blocks = total // BLOCK
    starts = bucket_starts(buckets)
    whole = lambda b, *_: (0, 0)
    return pl.pallas_call(
        partial(attend_back_kernel, starts, heads, size),
        grid_spec=pltpu.PrefetchScalarGridSpec(
            num_scalar_prefetch=2,
            grid=(blocks,),
            in_specs=[
                pl.BlockSpec((total, wide), whole),
                pl.BlockSpec((total, inner), whole),
                pl.BlockSpec((total, inner), whole),
                pl.BlockSpec((8, total), whole),
                pl.BlockSpec((BLOCK, 1), lambda b, *_: (b, 0)),
                pl.BlockSpec((1, total), whole),
                pl.BlockSpec((heads, 5, BLOCK, BLOCK), lambda b, *_: (0, 0, 0, 0)),
            ],
            out_specs=[
                pl.BlockSpec((total, wide), whole),
                pl.BlockSpec((heads, buckets, BLOCK), lambda b, *_: (0, 0, 0)),
            ],
            scratch_shapes=[
                pltpu.VMEM((heads, total, size), bf16),
                pltpu.VMEM((heads, total, size), bf16),
                pltpu.VMEM((heads, total, size), f32),
                pltpu.VMEM((8, total), f32),
                pltpu.VMEM((heads, 5, BLOCK, BLOCK), f32),
            ],
        ),
        out_shape=(
            jax.ShapeDtypeStruct((total, wide), bf16),
            jax.ShapeDtypeStruct((heads, buckets, BLOCK), f32),
        ),
        compiler_params=params(),
        cost_estimate=pl.CostEstimate(
            flops=10 * total * total * inner // 2,
            transcendentals=total * total * heads // 2,
            bytes_accessed=6 << 20,
        ),
        name="attend_back",
    )(lo, cnt, qkv, context_grad, context, lse, segk_col, segq_row, tiles)


def pool_matrix(shape, axis, me, query_len, query_local):
    token = lax.broadcasted_iota(jnp.int32, shape, axis)
    query = lax.broadcasted_iota(jnp.int32, shape, 1 - axis)
    span = query_len * query_local
    holder = jnp.bitwise_xor(token // span, me)
    return (holder * query_local + token % span // query_len == query).astype(f32)


def score_kernel(query_len, query_local, docs, first_ref, emb_ref, qe_ref, seg_ref, chosen_ref, pos_ref, sums_ref, logit_ref, stat_ref, acc_s):
    b = pl.program_id(0)
    count = qe_ref.shape[0]

    @pl.when(b == 0)
    def _():
        acc_s[...] = jnp.zeros(acc_s.shape, f32)

    near = jnp.exp(sharpness * (dot_nt(emb_ref[...], qe_ref[...]) - 1.0))
    seg = seg_ref[...]
    for d in range(docs):
        acc_s[d : d + 1, :] += jnp.sum(jnp.where(seg == d, near, 0.0), axis=0, keepdims=True)

    @pl.when(b == pl.num_programs(0) - 1)
    def _():
        sums = acc_s[:docs, :]
        sums_ref[...] = acc_s[...]
        chosen = chosen_ref[:docs, :]
        smooth = 1.0 + jnp.log(sums) / sharpness
        pool = pool_matrix((count, pos_ref.shape[1]), 0, first_ref[1], query_len, query_local)
        picked = dot_exact(chosen * smooth, pool)
        counts = dot_exact(chosen, pool)
        logits = picked / jnp.maximum(counts, 1.0) / smoothing_divisor
        top = jnp.max(logits, axis=0, keepdims=True)
        spread = jnp.sum(jnp.exp(logits - top), axis=0, keepdims=True)
        doc = lax.broadcasted_iota(jnp.int32, logits.shape, 0) + first_ref[0]
        mine = doc == pos_ref[0:1, :]
        stat_ref[0:1, :] = top
        stat_ref[1:2, :] = spread
        stat_ref[2:3, :] = jnp.sum(jnp.where(mine, logits, 0.0), axis=0, keepdims=True)
        stat_ref[3:4, :] = jnp.sum(jnp.where(mine, counts, 0.0), axis=0, keepdims=True)
        stat_ref[4:8, :] = jnp.zeros((4, pos_ref.shape[1]), f32)
        logit_ref[0:docs, :] = logits
        logit_ref[docs : 2 * docs, :] = counts


def score(first, emb, query_emb, seg_col, chosen, positives, query_len, query_local, docs):
    count, width = query_emb.shape
    lanes = positives.shape[1]
    length = emb.shape[0]
    blocks = length // BLOCK
    whole = lambda b, *_: (0, 0)
    return pl.pallas_call(
        partial(score_kernel, query_len, query_local, docs),
        grid_spec=pltpu.PrefetchScalarGridSpec(
            num_scalar_prefetch=1,
            grid=(blocks,),
            in_specs=[
                pl.BlockSpec((BLOCK, width), lambda b, *_: (b, 0)),
                pl.BlockSpec((count, width), whole),
                pl.BlockSpec((BLOCK, 1), lambda b, *_: (b, 0)),
                pl.BlockSpec((8, count), whole),
                pl.BlockSpec((8, lanes), whole),
            ],
            out_specs=[
                pl.BlockSpec((8, count), whole),
                pl.BlockSpec((8, lanes), whole),
                pl.BlockSpec((8, lanes), whole),
            ],
            scratch_shapes=[pltpu.VMEM((8, count), f32)],
        ),
        out_shape=(
            jax.ShapeDtypeStruct((8, count), f32),
            jax.ShapeDtypeStruct((8, lanes), f32),
            jax.ShapeDtypeStruct((8, lanes), f32),
        ),
        compiler_params=params(),
        name="score",
    )(first, emb, query_emb, seg_col, chosen, positives)


def score_back_kernel(query_len, query_local, docs, first_ref, emb_ref, qe_ref, seg_ref, chosen_ref, pos_ref, sums_ref, logit_ref, stat_ref, demb_ref, dqe_ref, grad_s, dq_s):
    b = pl.program_id(0)
    count = qe_ref.shape[0]

    @pl.when(b == 0)
    def _():
        logits = logit_ref[0:docs, :]
        counts = logit_ref[docs : 2 * docs, :]
        doc = lax.broadcasted_iota(jnp.int32, logits.shape, 0) + first_ref[0]
        mine = (doc == pos_ref[0:1, :]).astype(f32)
        share = jnp.exp(logits - stat_ref[0:1, :]) / stat_ref[1:2, :]
        grad = (share - mine) / smoothing_divisor / jnp.maximum(counts, 1.0)
        spread = pool_matrix((logits.shape[1], count), 1, first_ref[1], query_len, query_local)
        grad_s[0:docs, :] = dot_exact(grad, spread) * chosen_ref[:docs, :] / sums_ref[:docs, :]
        dq_s[...] = jnp.zeros(dq_s.shape, f32)

    emb = emb_ref[...]
    near = jnp.exp(sharpness * (dot_nt(emb, qe_ref[...]) - 1.0))
    seg = seg_ref[...]
    weight = jnp.broadcast_to(grad_s[0:1, :], near.shape)
    for d in range(1, docs):
        weight = jnp.where(seg == d, grad_s[d : d + 1, :], weight)
    grad = (near * weight).astype(bf16)
    demb_ref[...] = dot_nn(grad, qe_ref[...])
    dq_s[...] += dot_tn(emb, grad)

    @pl.when(b == pl.num_programs(0) - 1)
    def _():
        dqe_ref[...] = jnp.transpose(dq_s[...]).astype(bf16)


def score_back(first, emb, query_emb, seg_col, chosen, positives, sums, logits, stats, query_len, query_local, docs):
    count, width = query_emb.shape
    lanes = positives.shape[1]
    length = emb.shape[0]
    blocks = length // BLOCK
    whole = lambda b, *_: (0, 0)
    return pl.pallas_call(
        partial(score_back_kernel, query_len, query_local, docs),
        grid_spec=pltpu.PrefetchScalarGridSpec(
            num_scalar_prefetch=1,
            grid=(blocks,),
            in_specs=[
                pl.BlockSpec((BLOCK, width), lambda b, *_: (b, 0)),
                pl.BlockSpec((count, width), whole),
                pl.BlockSpec((BLOCK, 1), lambda b, *_: (b, 0)),
                pl.BlockSpec((8, count), whole),
                pl.BlockSpec((8, lanes), whole),
                pl.BlockSpec((8, count), whole),
                pl.BlockSpec((8, lanes), whole),
                pl.BlockSpec((8, lanes), whole),
            ],
            out_specs=[
                pl.BlockSpec((BLOCK, width), lambda b, *_: (b, 0)),
                pl.BlockSpec((count, width), whole),
            ],
            scratch_shapes=[pltpu.VMEM((8, count), f32), pltpu.VMEM((width, count), f32)],
        ),
        out_shape=(
            jax.ShapeDtypeStruct((length, width), f32),
            jax.ShapeDtypeStruct((count, width), bf16),
        ),
        compiler_params=params(),
        name="score_back",
    )(first, emb, query_emb, seg_col, chosen, positives, sums, logits, stats)


def rms_scale(values):
    return lax.rsqrt(jnp.mean(values * values, axis=-1, keepdims=True) + epsilon)


def rms_back(values, scale_values, gain_values, gradient):
    weighted = gradient * gain_values
    average = jnp.mean(weighted * values, axis=-1, keepdims=True)
    input_grad = (
        scale_values * weighted - values * (scale_values * scale_values * scale_values) * average
    )
    gain_grad = jnp.sum(gradient * values * scale_values, axis=0)
    return (input_grad, gain_grad)


def gated_unit(gate_values, up_values):
    return jax.nn.gelu(gate_values, approximate=True) * up_values


def swapped(bit, mine, theirs, axis=0):
    first = jnp.where(bit == 0, mine, theirs)
    second = jnp.where(bit == 0, theirs, mine)
    return jnp.concatenate([first, second], axis=axis)


def part(values, index, parts, axis=0):
    size = values.shape[axis] // parts
    return lax.dynamic_slice_in_dim(values, index * size, size, axis)


def shards(
    doc_tokens,
    query_tokens,
    doc_segments,
    query_keep,
    retrieved,
    positives,
    attn_gain,
    query_weight,
    key_weight,
    value_weight,
    output_weight,
    position_bias,
    ffn_gain,
    gate_weight,
    up_weight,
    down_weight,
    final_gain,
    proj_weight,
):
    groups = lax.axis_size("dp")
    tensor_size = lax.axis_size("mp")
    bits = groups.bit_length() - 1
    dp = lax.axis_index("dp")
    mp = lax.axis_index("mp")
    x = mp // 2
    core = mp % 2
    row_count, shard_len, width = doc_tokens.shape
    length = shard_len * tensor_size
    query_local, query_len, _ = query_tokens.shape
    chip_queries = query_local * 2
    buckets = position_bias.shape[0]
    hidden_local = gate_weight.shape[1]
    doc_local = retrieved.shape[2]
    docs_row = doc_local // row_count
    query_total = query_keep.shape[0]
    vector_width = proj_weight.shape[1]
    inner = query_weight.shape[1]

    def over(axis, size, mask):
        pairs = [(i, i ^ mask) for i in range(size)]
        return lambda values: lax.ppermute(values, axis, pairs)

    to_x = over("mp", tensor_size, 2)
    to_core = over("mp", tensor_size, 1)
    to_dp = [over("dp", groups, 1 << b) for b in range(bits)]
    dp_bit = [(dp >> b) & 1 for b in range(bits)]

    kept_rows = lax.dynamic_index_in_dim(doc_tokens, x, 0, keepdims=False)
    sent_rows = lax.dynamic_index_in_dim(doc_tokens, 1 - x, 0, keepdims=False)
    far_rows = to_x(sent_rows)
    near_rows = to_core(kept_rows)
    far_core_rows = to_core(far_rows)
    flat_queries = query_tokens.reshape(query_local * query_len, width)
    near_queries = to_core(flat_queries)

    def from_x(weight):
        if bits == 0:
            return to_x(weight)
        got = to_x(part(weight, dp_bit[0], 2))
        return swapped(dp_bit[0], got, to_dp[0](got))

    own_qkv = jnp.concatenate([query_weight, key_weight, value_weight], axis=1)
    far_qkv = from_x(own_qkv)
    far_output = from_x(output_weight)
    own_gate_up = jnp.concatenate([gate_weight, up_weight], axis=1)
    far_gate_up = from_x(own_gate_up)
    far_down = from_x(down_weight)
    far_bias = to_x(position_bias)
    qkv_weights = (own_qkv, far_qkv)
    output_weights = (output_weight, far_output)
    gate_up_weights = (own_gate_up, far_gate_up)
    down_weights = (down_weight, far_down)
    tiles = [bias_tiles(table.astype(f32)) for table in (position_bias, far_bias)]

    row_segments = lax.dynamic_index_in_dim(doc_segments, x, 0, keepdims=False)
    chip_keep = lax.dynamic_slice_in_dim(
        query_keep, (dp * tensor_size + x * 2) * query_local, chip_queries, 0
    ).reshape(-1)
    query_ids = jnp.arange(chip_queries * query_len, dtype=jnp.int32) // query_len + docs_row
    seg_q = jnp.concatenate([row_segments, query_ids])
    seg_k = jnp.concatenate([row_segments, jnp.where(chip_keep > 0, query_ids, -1)])
    segs = (seg_q[:, None], seg_q[None, :], seg_k[:, None], seg_k[None, :])
    blocked = row_segments.reshape(-1, BLOCK)
    low = jnp.sum((row_segments[None, :] < blocked[:, :1]).astype(jnp.int32), axis=1)
    high = jnp.sum((row_segments[None, :] <= blocked[:, -1:]).astype(jnp.int32), axis=1)
    low_block = low // BLOCK
    high_block = (high + BLOCK - 1) // BLOCK
    doc_blocks = length // BLOCK
    query_blocks = chip_queries * query_len // BLOCK
    lo = jnp.concatenate([low_block, jnp.full((query_blocks,), doc_blocks - 1, jnp.int32)])
    cnt = jnp.concatenate(
        [(high_block - low_block + 1) // 2, jnp.full((query_blocks,), 1, jnp.int32)]
    )
    ranges = (lo, cnt)

    order = [("dp", b) for b in reversed(range(bits))] + [("x", 0)]
    blocks = groups * 2

    def my_queries(values, moved=True):
        lead = values.shape[0]
        split = values.reshape(lead, blocks, 2, -1)
        mine = lax.dynamic_index_in_dim(split, core, 2, keepdims=False)
        mine = mine.reshape((lead,) + (2,) * (bits + 1) + (-1,))
        for s, (axis, b) in enumerate(order if moved else []):
            bit = x if axis == "x" else dp_bit[b]
            mine = jnp.where(bit == 0, mine, jnp.flip(mine, 1 + s))
        mine = jnp.transpose(mine, (0,) + tuple(range(bits + 1, 0, -1)) + (bits + 2,))
        return mine.reshape(lead, -1)

    row_retrieved = lax.dynamic_slice_in_dim(retrieved, x * docs_row, docs_row, 2)
    chosen = (query_keep[:, :, None] * row_retrieved).reshape(query_total * query_len, docs_row)
    chosen = my_queries(jnp.transpose(chosen.astype(f32)))
    chosen = jnp.pad(chosen, ((0, 8 - docs_row), (0, 0)))
    my_positives = my_queries(positives.reshape(1, -1), moved=False)
    half_queries = my_positives.shape[1]
    query_lanes = -(-half_queries // BLOCK) * BLOCK
    pos_rows = jnp.pad(my_positives, ((0, 7), (0, query_lanes - half_queries)), constant_values=-1)

    near_first = jnp.where(core == 0, kept_rows, near_rows)
    near_second = jnp.where(core == 0, near_rows, kept_rows)
    far_first = jnp.where(core == 0, far_rows, far_core_rows)
    far_second = jnp.where(core == 0, far_core_rows, far_rows)
    tokens = jnp.concatenate(
        [
            jnp.where(x == 0, near_first, far_first),
            jnp.where(x == 0, near_second, far_second),
            jnp.where(x == 0, far_first, near_first),
            jnp.where(x == 0, far_second, near_second),
            jnp.where(core == 0, flat_queries, near_queries),
            jnp.where(core == 0, near_queries, flat_queries),
        ],
        axis=0,
    )
    inputs = tokens.astype(f32)
    gain_attn = attn_gain.astype(f32)
    gain_ffn = ffn_gain.astype(f32)
    gain_final = final_gain.astype(f32)
    scale_attn = rms_scale(inputs)
    normed_attn = (inputs * scale_attn * gain_attn).astype(bf16)
    heads = [dot_nn(normed_attn, w).astype(bf16) for w in qkv_weights]
    attended = [attend(h, ranges, segs, t[0]) for h, t in zip(heads, tiles)]
    contexts = [a[0] for a in attended]
    logs = [a[1] for a in attended]
    attn_part = sum(dot_nn(c, w) for c, w in zip(contexts, output_weights)).astype(bf16)
    mid = inputs + (attn_part.astype(f32) + to_core(attn_part).astype(f32))
    scale_ffn = rms_scale(mid)
    normed_ffn = (mid * scale_ffn * gain_ffn).astype(bf16)
    hiddens, pulls = [], []
    for w in gate_up_weights:
        gate_up = dot_nn(normed_ffn, w)
        hidden, pull = jax.vjp(gated_unit, gate_up[:, :hidden_local], gate_up[:, hidden_local:])
        hiddens.append(hidden.astype(bf16))
        pulls.append(pull)
    ffn_part = sum(dot_nn(h, w) for h, w in zip(hiddens, down_weights)).astype(bf16)
    layer_out = mid + (ffn_part.astype(f32) + to_core(ffn_part).astype(f32))
    scale_final = rms_scale(layer_out)
    final_normed = (layer_out * scale_final * gain_final).astype(bf16)
    projected = dot_nn(final_normed, proj_weight)
    proj_scale = lax.rsqrt(jnp.sum(projected * projected, axis=-1, keepdims=True) + epsilon)
    unit_vectors = projected * proj_scale
    embedded = unit_vectors.astype(bf16)

    doc_embedded = embedded[:length]
    query_emb = part(embedded[length:], core, 2)
    for axis, b in order:
        moved = to_x(query_emb) if axis == "x" else to_dp[b](query_emb)
        query_emb = jnp.concatenate([query_emb, moved], axis=0)
    place = sum((x if axis == "x" else dp_bit[b]) << s for s, (axis, b) in enumerate(order))
    first_doc = jnp.stack([dp * doc_local + x * docs_row, place])
    seg_col = row_segments[:, None]
    sums, logits, stats = score(
        first_doc, doc_embedded, query_emb, seg_col, chosen, pos_rows, query_len, query_local, docs_row
    )
    for move in [to_x] + to_dp:
        moved = move(stats)
        top = jnp.maximum(stats[0:1], moved[0:1])
        total = stats[1:2] * jnp.exp(stats[0:1] - top) + moved[1:2] * jnp.exp(moved[0:1] - top)
        stats = jnp.concatenate([top, total, stats[2:] + moved[2:]], axis=0)
    valid = jnp.arange(query_lanes) < half_queries
    loss_sum = jnp.sum(jnp.where(valid, stats[0] + jnp.log(stats[1]) - stats[2], 0.0))
    found_sum = jnp.sum(jnp.where(valid & (stats[3] > 0.5), 1.0, 0.0))
    ends = jnp.broadcast_to(jnp.stack([loss_sum, found_sum])[:, None], (2, BLOCK))
    ends = (ends + to_core(ends)) / query_total
    loss_value = ends[0, 0]
    found_share = ends[1, 0]

    demb, dqe = score_back(
        first_doc,
        doc_embedded,
        query_emb,
        seg_col,
        chosen,
        pos_rows,
        sums,
        logits,
        stats,
        query_len,
        query_local,
        docs_row,
    )
    demb16 = demb.astype(bf16)
    doc_vector_grad = demb16.astype(f32) + to_core(demb16).astype(f32)
    for axis, b in reversed(order):
        half = dqe.shape[0] // 2
        moved = to_x(dqe[half:]) if axis == "x" else to_dp[b](dqe[half:])
        dqe = (dqe[:half].astype(f32) + moved.astype(f32)).astype(bf16)
    query_vector_grad = swapped(core, dqe, to_core(dqe)).astype(f32)
    embedded_grad = jnp.concatenate([doc_vector_grad, query_vector_grad], axis=0)

    def reduced(own, far, first=False):
        own16 = own.astype(bf16)
        acc = own16.astype(f32) + to_x(far.astype(bf16)).astype(f32)
        for b in range(bits - 1):
            acc = acc.astype(bf16)
            acc = part(acc, dp_bit[b], 2).astype(f32) + to_dp[b](
                part(acc, 1 - dp_bit[b], 2)
            ).astype(f32)
        acc = acc.astype(bf16)
        acc = (acc.astype(f32) + to_dp[bits - 1](acc).astype(f32)).astype(bf16)
        for b in reversed(range(bits - 1)):
            acc = swapped(dp_bit[b], acc, to_dp[b](acc))
        return acc.astype(f32)

    projected_grad = (
        proj_scale
        * (
            embedded_grad
            - unit_vectors * jnp.sum(embedded_grad * unit_vectors, axis=-1, keepdims=True)
        )
    ).astype(bf16)
    proj_part = part(dot_tn(final_normed, projected_grad), core, 2).astype(bf16)
    for move in [to_x] + to_dp:
        proj_part = (proj_part.astype(f32) + move(proj_part).astype(f32)).astype(bf16)
    proj_weight_grad = swapped(core, proj_part, to_core(proj_part)).astype(f32)
    final_grad = dot_nt(projected_grad, proj_weight)
    layer_out_grad, final_gain_part = rms_back(layer_out, scale_final, gain_final, final_grad)
    ffn_out_grad = layer_out_grad.astype(bf16)
    down_grads = [dot_tn(h, ffn_out_grad) for h in hiddens]
    down_weight_grad = reduced(*down_grads)
    gate_up_grads = []
    for w, pull in zip(down_weights, pulls):
        gate_grad, up_grad = pull(dot_nt(ffn_out_grad, w))
        gate_up_grads.append(jnp.concatenate([gate_grad, up_grad], axis=1).astype(bf16))
    gate_up_weight_grad = reduced(*[dot_tn(normed_ffn, g) for g in gate_up_grads])
    nf_part = sum(dot_nt(g, w) for g, w in zip(gate_up_grads, gate_up_weights)).astype(bf16)
    normed_ffn_grad = nf_part.astype(f32) + to_core(nf_part).astype(f32)
    back_ffn, ffn_gain_part = rms_back(mid, scale_ffn, gain_ffn, normed_ffn_grad)
    mid_grad = layer_out_grad + back_ffn
    attn_out_grad = mid_grad.astype(bf16)
    output_weight_grad = reduced(*[dot_tn(c, attn_out_grad) for c in contexts])
    heads_grads, bias_grads = [], []
    for k in range(2):
        context_grad = dot_nt(attn_out_grad, output_weights[k]).astype(bf16)
        heads_grad, bias_grad = attend_back(
            heads[k], context_grad, contexts[k], logs[k], ranges, segs, tiles[k][1], buckets
        )
        heads_grads.append(heads_grad)
        bias_grads.append(jnp.sum(bias_grad, axis=-1))
    projection_grad = reduced(*[dot_tn(normed_attn, g) for g in heads_grads])
    na_part = sum(dot_nt(g, w) for g, w in zip(heads_grads, qkv_weights))
    attn_gain_part = jnp.sum(na_part * inputs * scale_attn, axis=0)

    def my_tokens(values, which):
        doc_mine = jnp.concatenate(
            [
                lax.dynamic_slice_in_dim(values, which * shard_len, shard_len, 0),
                lax.dynamic_slice_in_dim(values, (which + 2) * shard_len, shard_len, 0),
                lax.dynamic_slice_in_dim(
                    values, length + which * query_local * query_len, query_local * query_len, 0
                ),
            ],
            axis=0,
        )
        return doc_mine

    na_half = my_tokens(na_part.astype(bf16), core).astype(f32) + to_core(
        my_tokens(na_part.astype(bf16), 1 - core)
    ).astype(f32)
    inputs_half = my_tokens(inputs, core)
    scale_half = my_tokens(scale_attn, core)
    weighted = na_half * gain_attn
    average = jnp.mean(weighted * inputs_half, axis=-1, keepdims=True)
    input_grad = (
        my_tokens(mid_grad, core)
        + scale_half * weighted
        - inputs_half * (scale_half * scale_half * scale_half) * average
    )
    first_half = input_grad[:shard_len]
    second_half = input_grad[shard_len : 2 * shard_len]
    stay = jnp.where(x == 0, first_half, second_half)
    leave = jnp.where(x == 0, second_half, first_half).astype(bf16)
    back = to_x(leave).astype(f32)
    doc_grad = jnp.stack([jnp.where(x == 0, stay, back), jnp.where(x == 0, back, stay)], axis=0)
    query_grad = input_grad[2 * shard_len :].reshape(query_local, query_len, width)

    lanes = BLOCK
    gains = jnp.concatenate(
        [
            (0.5 * final_gain_part).reshape(-1, lanes),
            (0.5 * ffn_gain_part).reshape(-1, lanes),
            attn_gain_part.reshape(-1, lanes),
        ],
        axis=0,
    )
    gain_rows = gains.shape[0]
    bias_rows = [jnp.pad(g, ((0, 0), (0, lanes - buckets))) for g in bias_grads]
    packet = jnp.concatenate([gains, bias_rows[0]], axis=0) + to_x(
        jnp.concatenate([gains, bias_rows[1]], axis=0)
    )
    for move in to_dp:
        packet = packet + move(packet)
    position_bias_grad = jnp.transpose(packet[gain_rows:, :buckets])
    gains = packet[:gain_rows]
    gains = (gains + to_core(gains)).reshape(3, width)

    return (
        loss_value,
        found_share,
        doc_grad,
        query_grad,
        gains[2],
        projection_grad[:, :inner],
        projection_grad[:, inner : 2 * inner],
        projection_grad[:, 2 * inner :],
        output_weight_grad,
        position_bias_grad,
        gains[1],
        gate_up_weight_grad[:, :hidden_local],
        gate_up_weight_grad[:, hidden_local:],
        down_weight_grad,
        gains[0],
        proj_weight_grad,
    )


def solution(mesh):
    placed = (
        P("dp", "mp", None),
        P(("dp", "mp"), None, None),
        P("dp", None),
        P(),
        P(None, None, "dp"),
        P(),
        P(),
        P(None, "mp"),
        P(None, "mp"),
        P(None, "mp"),
        P("mp", None),
        P(None, "mp"),
        P(),
        P(None, "mp"),
        P(None, "mp"),
        P("mp", None),
        P(),
        P(),
    )
    return jax.shard_map(
        shards,
        mesh=mesh,
        in_specs=placed,
        out_specs=(
            P(),
            P(),
            P("dp", "mp", None),
            P(("dp", "mp"), None, None),
            P(),
            P(None, "mp"),
            P(None, "mp"),
            P(None, "mp"),
            P("mp", None),
            P(None, "mp"),
            P(),
            P(None, "mp"),
            P(None, "mp"),
            P("mp", None),
            P(),
            P(),
        ),
        check_vma=False,
    )
```

time: 1600 us -> 518 us (0.32)
  waiting for transfers between devices: 672 us -> 187 us
  local copies, waits for them, and re-layouts: 388 us -> 48.5 us
  blocking collectives: 195 us -> 0 us
  matrix products: 158 us -> 50.7 us
  Pallas kernels: 0 us -> 100 us
  starting transfers between devices: 0.8 us -> 70.9 us
  other arithmetic: 123 us -> 53.1 us
  loops' own time: 27 us -> 0 us
  between operations: 19.1 us -> 2.96 us
    psum x2 -> x0, waiting for transfers between devices: 325 us -> none  [the longest x1 244 us: shards(): lax.psum((query_weight_grad, key_weight_grad, value_weight_grad, output_w...]
    reduce_scatter x9 -> x0, waiting for transfers between devices: 290 us -> none  [the longest x1 130 us: shards(): lax.psum_scatter(query_parts.reshape(query_total, query_len, vector_width...]
    ppermute x0 -> x67, waiting for transfers between devices: none -> 187 us  [over(): return lambda values: lax.ppermute(values, axis, pairs)]
    all_gather x7 -> x0, blocking collectives: 124 us -> none  [the longest x1 42.1 us: shards(): lax.all_gather(query_embedded, ('dp', 'mp'), axis=0, tiled=True)]
    dot_general x59 -> x27, matrix products: 158 us -> 50.7 us  [the longest x9 20.3 us: dot_nt(): lax.dot_general(a, b, (((1,), (1,)), ((), ())), preferred_element_type=f32)]
    reshape x21 -> x4, local copies, waits for them, and re-layouts: 105 us -> 0.44 us  [the longest x2 0.19 us: my_queries(): return mine.reshape(lead, -1)]
    pallas_call x0 -> x8, Pallas kernels: none -> 100 us  [the longest x2 53.9 us: attend_back(): pl.pallas_call(partial(attend_back_kernel, starts, heads, size), grid_spe...]
    while x70 -> x0, local copies, waits for them, and re-layouts: 94.9 us -> none
  transfers between devices with their start and end apart: 15 -> 67, of which waited for: 12 -> 39; matrix products, arithmetic and copies ran while one was open for 14% -> 16% of each run, Pallas kernels for 0% -> 18%
where the time goes in v1:
time: 518 us; the launch traced here: 513 us
  waiting for transfers between devices  187 us (36%)
  Pallas kernels  100 us (19%)
  starting transfers between devices  70.9 us (14%)
  other arithmetic  53.1 us (10%)
  matrix products  50.7 us (10%)
  local copies, waits for them, and re-layouts  48.5 us (9%)
    ppermute x67, waiting for transfers between devices, over(): return lambda values: lax.ppermute(values, axis, pairs)  187 us
    ppermute x67, starting transfers between devices, over(): return lambda values: lax.ppermute(values, axis, pairs)  70.9 us
    pallas_call x2, Pallas kernels, attend_back(): pl.pallas_call(partial(attend_back_kernel, starts, heads, size), grid_spe...  53.9 us
    pallas_call x2, Pallas kernels, attend(): pl.pallas_call(partial(attend_kernel, heads, size), grid_spec=pltpu.Prefe...  32.8 us
    unnamed x195, local copies, waits for them, and re-layouts  20.9 us
    dot_general x9, matrix products, dot_nt(): lax.dot_general(a, b, (((1,), (1,)), ((), ())), preferred_element_type=f32)  20.3 us
    reduce_sum x3, other arithmetic, rms_scale(): jnp.mean(values * values, axis=-1, keepdims=True) + epsilon  16.6 us
    dot_general x9, matrix products, dot_tn(): lax.dot_general(a, b, (((0,), (0,)), ((), ())), preferred_element_type=f32)  15.7 us
  transfers between devices with their start and end apart: 67, of which 39 were waited for; matrix products, arithmetic and copies ran while one was open for 16% of the time, Pallas kernels for 18%

profile of v1, /device:TPU:0, one launch (start us, length us, event | category | flops | bytes accessed | tf_op | source)
XLA Modules:
  0.0 513.4 jit_solution(11331223968738422090)
XLA Ops:
  17.1 11.6 %collective-permute-done.7 = bf16[96,768]{1,0:T(8,128)(2,1)S(1)} collective-permute-done((bf16[96,768]{1,0:T(8,128)(2,1)S(1)}, bf16[96,768]{1,0:T(8,128)(2,1)S(1)}, u32[]{:S(2)}, u32[]{:S(2)}) %collective-permute-start.7) | collective-permute-done | bytes 147488 | tf_op jit(solution)/shard_map/ppermute | solution.py:591
  44.8 16.3 %attend.2 = (bf16[1152,192]{1,0:T(8,128)(2,1)S(1)}, f32[8,1152]{1,0:T(8,128)S(1)}) custom-call(s32[9]{0:T(128)S(1)} %get-tuple-element.150.lo_ref, s32[9]{0:T(128)S(1)} %get-tuple-element.151.cnt_ref, bf16[1152,576]{1,0:T(8,128)(2,1)S(1)} %convolution_convert_fusion.1.qkv_ref, s32[1152,1]{1,0:T(8,128)S(1)} %broadcast_in_dim.32.segq_ref, ...), custom_call_target="tpu_custom_call" | custom-call | flops 509607936 | bytes 4194304 | tf_op jit(solution)/shard_map/attend/pallas_call | solution.py:182
  64.6 16.5 %attend.3 = (bf16[1152,192]{1,0:T(8,128)(2,1)S(1)}, f32[8,1152]{1,0:T(8,128)S(1)}) custom-call(s32[9]{0:T(128)S(1)} %get-tuple-element.150.lo_ref, s32[9]{0:T(128)S(1)} %get-tuple-element.151.cnt_ref, bf16[1152,576]{1,0:T(8,128)(2,1)S(1)} %convolution_convert_fusion.qkv_ref, s32[1152,1]{1,0:T(8,128)S(1)} %broadcast_in_dim.32.segq_ref, ...), custom_call_target="tpu_custom_call" | custom-call | flops 509607936 | bytes 4194304 | tf_op jit(solution)/shard_map/attend/pallas_call | solution.py:182
  83.7 10.9 %collective-permute-done.12 = bf16[256,768]{1,0:T(8,128)(2,1)S(1)} collective-permute-done((bf16[256,768]{1,0:T(8,128)(2,1)S(1)}, bf16[256,768]{1,0:T(8,128)(2,1)S(1)}, u32[]{:S(2)}, u32[]{:S(2)}) %collective-permute-start.12) | collective-permute-done | bytes 393248 | tf_op jit(solution)/shard_map/ppermute | solution.py:591
  95.2 16.6 %collective-permute-done.13 = bf16[256,768]{1,0:T(8,128)(2,1)S(1)} collective-permute-done((bf16[256,768]{1,0:T(8,128)(2,1)S(1)}, bf16[256,768]{1,0:T(8,128)(2,1)S(1)}, u32[]{:S(2)}, u32[]{:S(2)}) %collective-permute-start.13) | collective-permute-done | bytes 393248 | tf_op jit(solution)/shard_map/ppermute | solution.py:591
  135.7 13.2 %multiply_reduce_fusion.5 = (f32[1152]{0:T(1024)S(1)}, f32[1152,768]{1,0:T(8,128)S(1)}) fusion(f32[1152,768]{1,0:T(8,128)} %copy-done.11, bf16[1152,768]{1,0:T(8,128)(2,1)} %collective-permute-done.14, bf16[1152,768]{1,0:T(8,128)(2,1)} %fusion), kind=kLoop, calls=%fused_computation.13 | loop fusion | flops 5307264 | bytes 10621440 | tf_op jit(solution)/shard_map/reduce_sum | solution.py:522
  170.9 4.7 score.1
  192.0 5.0 score_back.1
  247.7 10.2 %collective-permute-done.56 = bf16[512,768]{1,0:T(8,128)(2,1)S(1)} collective-permute-done((bf16[512,768]{1,0:T(8,128)(2,1)S(1)}, bf16[512,768]{1,0:T(8,128)(2,1)S(1)}, u32[]{:S(2)}, u32[]{:S(2)}) %collective-permute-start.56) | collective-permute-done | bytes 786464 | tf_op jit(solution)/shard_map/ppermute | solution.py:591
  262.1 5.8 %collective-permute-done.57 = bf16[256,768]{1,0:T(8,128)(2,1)S(1)} collective-permute-done((bf16[256,768]{1,0:T(8,128)(2,1)S(1)}, bf16[256,768]{1,0:T(8,128)(2,1)S(1)}, u32[]{:S(2)}, u32[]{:S(2)}) %collective-permute-start.57) | collective-permute-done | bytes 393248 | tf_op jit(solution)/shard_map/ppermute | solution.py:591
  269.9 3.8 collective-permute-done.58
  277.4 5.5 %collective-permute-done.59 = bf16[128,768]{1,0:T(8,128)(2,1)S(1)} collective-permute-done((bf16[128,768]{1,0:T(8,128)(2,1)S(1)}, bf16[128,768]{1,0:T(8,128)(2,1)S(1)}, u32[]{:S(2)}, u32[]{:S(2)}) %collective-permute-start.59) | collective-permute-done | bytes 196640 | tf_op jit(solution)/shard_map/ppermute | solution.py:591
  283.7 7.1 %collective-permute-done.50 = bf16[768,1024]{1,0:T(8,128)(2,1)S(1)} collective-permute-done((bf16[768,1024]{1,0:T(8,128)(2,1)S(1)}, bf16[768,1024]{1,0:T(8,128)(2,1)S(1)}, u32[]{:S(2)}, u32[]{:S(2)}) %collective-permute-start.50) | collective-permute-done | bytes 1572896 | tf_op jit(solution)/shard_map/ppermute | solution.py:591
  295.1 3.9 fusion.44
  305.7 26.9 %attend_back.2 = (bf16[1152,576]{1,0:T(8,128)(2,1)S(1)}, f32[3,32,128]{2,1,0:T(8,128)S(1)}) custom-call(s32[9]{0:T(128)S(1)} %get-tuple-element.150.lo_ref, s32[9]{0:T(128)S(1)} %get-tuple-element.151.cnt_ref, bf16[1152,576]{1,0:T(8,128)(2,1)S(1)} %copy-done.10, bf16[1152,192]{1,0:T(8,128)(2,1)S(1)} %copy.112.do_ref, ...), custom_call_target="tpu_custom_call" | custom-call | flops 1274019840 | bytes 6291456 | tf_op jit(solution)/shard_map/attend_back/pallas_call | solution.py:335
  345.6 27.0 %attend_back.3 = (bf16[1152,576]{1,0:T(8,128)(2,1)S(1)}, f32[3,32,128]{2,1,0:T(8,128)S(1)}) custom-call(s32[9]{0:T(128)S(1)} %get-tuple-element.150.lo_ref, s32[9]{0:T(128)S(1)} %get-tuple-element.151.cnt_ref, bf16[1152,576]{1,0:T(8,128)(2,1)S(1)} %copy-done.8, bf16[1152,192]{1,0:T(8,128)(2,1)S(1)} %copy.114.do_ref, ...), custom_call_target="tpu_custom_call" | custom-call | flops 1274019840 | bytes 6291456 | tf_op jit(solution)/shard_map/attend_back/pallas_call | solution.py:335
  383.2 13.0 %collective-permute-done.33 = f32[21,128]{1,0:T(8,128)S(1)} collective-permute-done((f32[21,128]{1,0:T(8,128)S(1)}, f32[21,128]{1,0:T(8,128)S(1)}, u32[]{:S(2)}, u32[]{:S(2)}) %collective-permute-start.33) | collective-permute-done | bytes 10784 | tf_op jit(solution)/shard_map/ppermute | solution.py:591
  412.4 5.0 collective-permute-done.45
  449.1 9.1 %collective-permute-done.40 = bf16[192,576]{0,1:T(8,128)(2,1)S(1)} collective-permute-done((bf16[192,576]{0,1:T(8,128)(2,1)S(1)}, bf16[192,576]{0,1:T(8,128)(2,1)S(1)}, u32[]{:S(2)}, u32[]{:S(2)}) %collective-permute-start.40) | collective-permute-done | bytes 221216 | tf_op jit(solution)/shard_map/ppermute | solution.py:591
  458.4 4.9 collective-permute-start.41
  466.0 6.7 %collective-permute-done.41 = bf16[192,576]{0,1:T(8,128)(2,1)S(1)} collective-permute-done((bf16[192,576]{0,1:T(8,128)(2,1)S(1)}, bf16[192,576]{0,1:T(8,128)(2,1)S(1)}, u32[]{:S(2)}, u32[]{:S(2)}) %collective-permute-start.41) | collective-permute-done | bytes 221216 | tf_op jit(solution)/shard_map/ppermute | solution.py:591
  473.0 11.1 %collective-permute-done.42 = bf16[192,576]{0,1:T(8,128)(2,1)S(1)} collective-permute-done((bf16[192,576]{0,1:T(8,128)(2,1)S(1)}, bf16[192,576]{0,1:T(8,128)(2,1)S(1)}, u32[]{:S(2)}, u32[]{:S(2)}) %collective-permute-start.42) | collective-permute-done | bytes 221216 | tf_op jit(solution)/shard_map/ppermute | solution.py:591
  487.9 9.6 %collective-permute-done.43 = bf16[384,576]{0,1:T(8,128)(2,1)S(1)} collective-permute-done((bf16[384,576]{0,1:T(8,128)(2,1)S(1)}, bf16[384,576]{0,1:T(8,128)(2,1)S(1)}, u32[]{:S(2)}, u32[]{:S(2)}) %collective-permute-start.43) | collective-permute-done | bytes 442400 | tf_op jit(solution)/shard_map/ppermute | solution.py:591
  499.1 11.3 %collective-permute-done.55 = bf16[384,1024]{1,0:T(8,128)(2,1)S(1)} collective-permute-done((bf16[384,1024]{1,0:T(8,128)(2,1)S(1)}, bf16[384,1024]{1,0:T(8,128)(2,1)S(1)}, u32[]{:S(2)}, u32[]{:S(2)}) %collective-permute-start.55) | collective-permute-done | bytes 786464 | tf_op jit(solution)/shard_map/ppermute | solution.py:591
  (534 shorter events, 254.9 us)
Async XLA Ops:
  2.7 27.5 %collective-permute-start.1 = (bf16[256,768]{1,0:T(8,128)(2,1)}, bf16[256,768]{1,0:T(8,128)(2,1)S(1)}, u32[]{:S(2)}, u32[]{:S(2)}) collective-permute-start(bf16[256,768]{1,0:T(8,128)(2,1)} %get-tuple-element.115), channel_id=1, source_target_pairs={{0,2},{1,3},{2,0},{3,1},{4,6},{5,7},{6,4},{7,5},{8,10},{9,11},{10,... | collective-permute-start | bytes 1179656 | tf_op jit(solution)/shard_map/ppermute | solution.py:591
  5.7 35.7 %collective-permute-start = (bf16[256,768]{1,0:T(8,128)(2,1)S(1)}, bf16[256,768]{1,0:T(8,128)(2,1)S(1)}, u32[]{:S(2)}, u32[]{:S(2)}) collective-permute-start(bf16[256,768]{1,0:T(8,128)(2,1)S(1)} %get-tuple-element.116), channel_id=1, source_target_pairs={{0,1},{1,0},{2,3},{3,2},{4,5},{5,4},{6,7},{7,6},{8,9},{9,8},{10,11... | collective-permute-start | bytes 1179656 | tf_op jit(solution)/shard_map/ppermute | solution.py:591
  12.6 28.2 %collective-permute-start.4 = (bf16[384,576]{0,1:T(8,128)(2,1)}, bf16[384,576]{0,1:T(8,128)(2,1)}, u32[]{:S(2)}, u32[]{:S(2)}) collective-permute-start(bf16[384,576]{0,1:T(8,128)(2,1)} %constant_dynamic-slice_fusion.26), channel_id=1, source_target_pairs={{0,2},{1,3},{2,0},{3,1},{4,6},{5,7},{6,4},{7,5},{8,10},{9,11},{10,... | collective-permute-start | bytes 1327112 | tf_op jit(solution)/shard_map/ppermute | solution.py:591
  12.8 22.9 %collective-permute-start.6 = (bf16[32,3]{1,0:T(8,128)(2,1)S(1)}, bf16[32,3]{1,0:T(8,128)(2,1)S(1)}, u32[]{:S(2)}, u32[]{:S(2)}) collective-permute-start(bf16[32,3]{1,0:T(8,128)(2,1)S(1)} %copy.103), channel_id=1, source_target_pairs={{0,2},{1,3},{2,0},{3,1},{4,6},{5,7},{6,4},{7,5},{8,10},{9,11},{10,... | collective-permute-start | bytes 584 | tf_op jit(solution)/shard_map/ppermute | solution.py:591
  39.0 44.1 %collective-permute-start.10 = (bf16[384,1024]{1,0:T(8,128)(2,1)}, bf16[384,1024]{1,0:T(8,128)(2,1)}, u32[]{:S(2)}, u32[]{:S(2)}) collective-permute-start(bf16[384,1024]{1,0:T(8,128)(2,1)} %constant_dynamic-slice_fusion.24), channel_id=1, source_target_pairs={{0,2},{1,3},{2,0},{3,1},{4,6},{5,7},{6,4},{7,5},{8,10},{9,11},{10,... | collective-permute-start | bytes 2359304 | tf_op jit(solution)/shard_map/ppermute | solution.py:591
  40.8 20.9 %collective-permute-start.5 = (bf16[384,576]{0,1:T(8,128)(2,1)}, bf16[384,576]{0,1:T(8,128)(2,1)S(1)}, u32[]{:S(2)}, u32[]{:S(2)}) collective-permute-start(bf16[384,576]{0,1:T(8,128)(2,1)} %collective-permute-done.4), channel_id=1, source_target_pairs={{0,4},{4,0},{8,12},{12,8},{16,20},{20,16},{24,28},{28,24},{1,5},{5... | collective-permute-start | bytes 1327112 | tf_op jit(solution)/shard_map/ppermute | solution.py:591
  82.9 30.4 %collective-permute-start.9 = (bf16[1152,768]{1,0:T(8,128)(2,1)}, bf16[1152,768]{1,0:T(8,128)(2,1)}, u32[]{:S(2)}, u32[]{:S(2)}) collective-permute-start(bf16[1152,768]{1,0:T(8,128)(2,1)} %fusion.2), channel_id=1, source_target_pairs={{0,1},{1,0},{2,3},{3,2},{4,5},{5,4},{6,7},{7,6},{8,9},{9,8},{10,11... | collective-permute-start | bytes 5308424 | tf_op jit(solution)/shard_map/ppermute | solution.py:591
  83.1 28.8 %collective-permute-start.11 = (bf16[384,1024]{1,0:T(8,128)(2,1)}, bf16[384,1024]{1,0:T(8,128)(2,1)S(1)}, u32[]{:S(2)}, u32[]{:S(2)}) collective-permute-start(bf16[384,1024]{1,0:T(8,128)(2,1)} %collective-permute-done.10), channel_id=1, source_target_pairs={{0,4},{4,0},{8,12},{12,8},{16,20},{20,16},{24,28},{28,24},{1,5},{5... | collective-permute-start | bytes 2359304 | tf_op jit(solution)/shard_map/ppermute | solution.py:591
  94.6 17.2 %collective-permute-start.13 = (bf16[256,768]{1,0:T(8,128)(2,1)S(1)}, bf16[256,768]{1,0:T(8,128)(2,1)S(1)}, u32[]{:S(2)}, u32[]{:S(2)}) collective-permute-start(bf16[256,768]{1,0:T(8,128)(2,1)S(1)} %collective-permute-done.12), channel_id=1, source_target_pairs={{0,4},{4,0},{8,12},{12,8},{16,20},{20,16},{24,28},{28,24},{1,5},{5... | collective-permute-start | bytes 1179656 | tf_op jit(solution)/shard_map/ppermute | solution.py:591
  237.1 20.8 %collective-permute-start.56 = (bf16[512,768]{1,0:T(8,128)(2,1)S(1)}, bf16[512,768]{1,0:T(8,128)(2,1)S(1)}, u32[]{:S(2)}, u32[]{:S(2)}) collective-permute-start(bf16[512,768]{1,0:T(8,128)(2,1)S(1)} %convolution_convert_fusion.8), channel_id=1, source_target_pairs={{0,2},{1,3},{2,0},{3,1},{4,6},{5,7},{6,4},{7,5},{8,10},{9,11},{10,... | collective-permute-start | bytes 2359304 | tf_op jit(solution)/shard_map/ppermute | solution.py:591
  239.7 51.1 %collective-permute-start.50 = (bf16[768,1024]{1,0:T(8,128)(2,1)S(1)}, bf16[768,1024]{1,0:T(8,128)(2,1)S(1)}, u32[]{:S(2)}, u32[]{:S(2)}) collective-permute-start(bf16[768,1024]{1,0:T(8,128)(2,1)S(1)} %convolution_convert_fusion.4), channel_id=1, source_target_pairs={{0,2},{1,3},{2,0},{3,1},{4,6},{5,7},{6,4},{7,5},{8,10},{9,11},{10,... | collective-permute-start | bytes 4718600 | tf_op jit(solution)/shard_map/ppermute | solution.py:591
  244.8 48.9 %collective-permute-start.30 = (bf16[1152,768]{1,0:T(8,128)(2,1)S(1)}, bf16[1152,768]{1,0:T(8,128)(2,1)S(1)}, u32[]{:S(2)}, u32[]{:S(2)}) collective-permute-start(bf16[1152,768]{1,0:T(8,128)(2,1)S(1)} %fusion.1), channel_id=1, source_target_pairs={{0,1},{1,0},{2,3},{3,2},{4,5},{5,4},{6,7},{7,6},{8,9},{9,8},{10,11... | collective-permute-start | bytes 5308424 | tf_op jit(solution)/shard_map/ppermute | solution.py:591
  283.0 56.9 %collective-permute-start.60 = (bf16[128,768]{1,0:T(8,128)(2,1)S(1)}, bf16[128,768]{1,0:T(8,128)(2,1)}, u32[]{:S(2)}, u32[]{:S(2)}) collective-permute-start(bf16[128,768]{1,0:T(8,128)(2,1)S(1)} %add_convert_fusion.10), channel_id=1, source_target_pairs={{0,8},{4,12},{8,0},{12,4},{16,24},{20,28},{24,16},{28,20},{1,9},{5... | collective-permute-start | bytes 589832 | tf_op jit(solution)/shard_map/ppermute | solution.py:591
  292.5 140.3 %collective-permute-start.51 = (bf16[384,1024]{1,0:T(8,128)(2,1)}, bf16[384,1024]{1,0:T(8,128)(2,1)}, u32[]{:S(2)}, u32[]{:S(2)}) collective-permute-start(bf16[384,1024]{1,0:T(8,128)(2,1)} %constant_dynamic-slice_fusion.3), channel_id=1, source_target_pairs={{0,4},{4,0},{8,12},{12,8},{16,20},{20,16},{24,28},{28,24},{1,5},{5... | collective-permute-start | bytes 2359304 | tf_op jit(solution)/shard_map/ppermute | solution.py:591
  341.6 83.8 %collective-permute-start.61 = (bf16[256,768]{1,0:T(8,128)(2,1)}, bf16[256,768]{1,0:T(8,128)(2,1)}, u32[]{:S(2)}, u32[]{:S(2)}) collective-permute-start(bf16[256,768]{1,0:T(8,128)(2,1)} %pad_maximum_fusion.22), channel_id=1, source_target_pairs={{0,4},{4,0},{8,12},{12,8},{16,20},{20,16},{24,28},{28,24},{1,5},{5... | collective-permute-start | bytes 1179656 | tf_op jit(solution)/shard_map/ppermute | solution.py:591
  341.8 67.2 %collective-permute-start.44 = (bf16[192,768]{1,0:T(8,128)(2,1)}, bf16[192,768]{1,0:T(8,128)(2,1)}, u32[]{:S(2)}, u32[]{:S(2)}) collective-permute-start(bf16[192,768]{1,0:T(8,128)(2,1)} %convolution_convert_fusion.10), channel_id=1, source_target_pairs={{0,2},{1,3},{2,0},{3,1},{4,6},{5,7},{6,4},{7,5},{8,10},{9,11},{10,... | collective-permute-start | bytes 884744 | tf_op jit(solution)/shard_map/ppermute | solution.py:591
  375.1 63.3 %collective-permute-start.38 = (bf16[768,576]{0,1:T(8,128)(2,1)}, bf16[768,576]{0,1:T(8,128)(2,1)}, u32[]{:S(2)}, u32[]{:S(2)}) collective-permute-start(bf16[768,576]{0,1:T(8,128)(2,1)} %convolution_convert_fusion.6), channel_id=1, source_target_pairs={{0,2},{1,3},{2,0},{3,1},{4,6},{5,7},{6,4},{7,5},{8,10},{9,11},{10,... | collective-permute-start | bytes 2654216 | tf_op jit(solution)/shard_map/ppermute | solution.py:591
  378.3 18.0 %collective-permute-start.33 = (f32[21,128]{1,0:T(8,128)S(1)}, f32[21,128]{1,0:T(8,128)S(1)}, u32[]{:S(2)}, u32[]{:S(2)}) collective-permute-start(f32[21,128]{1,0:T(8,128)S(1)} %select_maximum_fusion), channel_id=1, source_target_pairs={{0,2},{1,3},{2,0},{3,1},{4,6},{5,7},{6,4},{7,5},{8,10},{9,11},{10,... | collective-permute-start | bytes 32264 | tf_op jit(solution)/shard_map/ppermute | solution.py:591
  408.3 32.2 %collective-permute-start.31 = (bf16[576,768]{1,0:T(8,128)(2,1)S(1)}, bf16[576,768]{1,0:T(8,128)(2,1)S(1)}, u32[]{:S(2)}, u32[]{:S(2)}) collective-permute-start(bf16[576,768]{1,0:T(8,128)(2,1)S(1)} %pad_maximum_fusion.13), channel_id=1, source_target_pairs={{0,1},{1,0},{2,3},{3,2},{4,5},{5,4},{6,7},{7,6},{8,9},{9,8},{10,11... | collective-permute-start | bytes 2654216 | tf_op jit(solution)/shard_map/ppermute | solution.py:591
  444.7 21.0 %collective-permute-start.53 = (bf16[192,1024]{1,0:T(8,128)(2,1)S(1)}, bf16[192,1024]{1,0:T(8,128)(2,1)S(1)}, u32[]{:S(2)}, u32[]{:S(2)}) collective-permute-start(bf16[192,1024]{1,0:T(8,128)(2,1)S(1)} %add_convert_fusion.7), channel_id=1, source_target_pairs={{0,16},{4,20},{8,24},{12,28},{16,0},{20,4},{24,8},{28,12},{1,17},{... | collective-permute-start | bytes 1179656 | tf_op jit(solution)/shard_map/ppermute | solution.py:591
  448.8 24.0 %collective-permute-start.32 = (bf16[256,768]{1,0:T(8,128)(2,1)S(1)}, bf16[256,768]{1,0:T(8,128)(2,1)S(1)}, u32[]{:S(2)}, u32[]{:S(2)}) collective-permute-start(bf16[256,768]{1,0:T(8,128)(2,1)S(1)} %select_convert_fusion), channel_id=1, source_target_pairs={{0,2},{1,3},{2,0},{3,1},{4,6},{5,7},{6,4},{7,5},{8,10},{9,11},{10,... | collective-permute-start | bytes 1179656 | tf_op jit(solution)/shard_map/ppermute | solution.py:591
  458.4 14.3 %collective-permute-start.41 = (bf16[192,576]{0,1:T(8,128)(2,1)S(1)}, bf16[192,576]{0,1:T(8,128)(2,1)S(1)}, u32[]{:S(2)}, u32[]{:S(2)}) collective-permute-start(bf16[192,576]{0,1:T(8,128)(2,1)S(1)} %add_convert_fusion.9), channel_id=1, source_target_pairs={{0,16},{4,20},{8,24},{12,28},{16,0},{20,4},{24,8},{28,12},{1,17},{... | collective-permute-start | bytes 663560 | tf_op jit(solution)/shard_map/ppermute | solution.py:591
  465.9 19.2 %collective-permute-start.54 = (bf16[192,1024]{1,0:T(8,128)(2,1)S(1)}, bf16[192,1024]{1,0:T(8,128)(2,1)S(1)}, u32[]{:S(2)}, u32[]{:S(2)}) collective-permute-start(bf16[192,1024]{1,0:T(8,128)(2,1)S(1)} %add_convert_fusion.6), channel_id=1, source_target_pairs={{0,8},{4,12},{8,0},{12,4},{16,24},{20,28},{24,16},{28,20},{1,9},{5... | collective-permute-start | bytes 1179656 | tf_op jit(solution)/shard_map/ppermute | solution.py:591
  485.2 25.2 %collective-permute-start.55 = (bf16[384,1024]{1,0:T(8,128)(2,1)S(1)}, bf16[384,1024]{1,0:T(8,128)(2,1)S(1)}, u32[]{:S(2)}, u32[]{:S(2)}) collective-permute-start(bf16[384,1024]{1,0:T(8,128)(2,1)S(1)} %pad_maximum_fusion.15), channel_id=1, source_target_pairs={{0,4},{4,0},{8,12},{12,8},{16,20},{20,16},{24,28},{28,24},{1,5},{5... | collective-permute-start | bytes 2359304 | tf_op jit(solution)/shard_map/ppermute | solution.py:591
  (136 other events, 1050.1 us)

commit v2 on v1

v2 whole, which is shorter than its diff:
```python
from functools import partial

import jax
import jax.numpy as jnp
import numpy as np
from jax import lax
from jax.experimental import pallas as pl
from jax.experimental.pallas import tpu as pltpu
from jax.sharding import PartitionSpec as P

epsilon = 1e-06
sharpness = 16.0
smoothing_divisor = 0.05
masked_score = -1e30
BLOCK = 128
PAIR = 2 * BLOCK
bf16 = jnp.bfloat16
f32 = jnp.float32


def bucket_starts(buckets):
    half = buckets // 2
    exact = half // 2
    distance = np.arange(0, 2048)
    scaled = (
        np.log(np.maximum(distance, 1) / exact) / np.log(128.0 / exact) * (half - exact)
    )
    far = np.minimum(exact + np.floor(np.maximum(scaled, 0.0)), half - 1)
    bucket = np.where(distance < exact, distance, far)
    return [int(np.argmax(bucket >= b)) for b in range(half)]


def dot_nn(a, b):
    return lax.dot_general(a, b, (((1,), (0,)), ((), ())), preferred_element_type=f32)


def dot_nt(a, b):
    return lax.dot_general(a, b, (((1,), (1,)), ((), ())), preferred_element_type=f32)


def dot_tn(a, b):
    return lax.dot_general(a, b, (((0,), (0,)), ((), ())), preferred_element_type=f32)


def dot_exact(a, b):
    return lax.dot_general(
        a, b, (((1,), (0,)), ((), ())), precision=lax.Precision.HIGHEST, preferred_element_type=f32
    )


def params(limit_mib=40):
    return pltpu.CompilerParams(vmem_limit_bytes=limit_mib << 20)


def cost(micros):
    return pl.CostEstimate(flops=int(micros * 3e9), transcendentals=0, bytes_accessed=1 << 10)


def bias_kernel(starts, heads, tab_ref, t_ref, tt_ref):
    half = len(starts)
    sub = lax.broadcasted_iota(jnp.int32, (BLOCK, BLOCK), 0)
    lane = lax.broadcasted_iota(jnp.int32, (BLOCK, BLOCK), 1)
    for ref, base in ((t_ref, lane - sub), (tt_ref, sub - lane)):
        for d in (-1, 0, 1):
            offset = base + BLOCK * d
            n = jnp.abs(offset)
            for h in range(heads):
                low = high = None
                if d <= 0:
                    low = jnp.full((BLOCK, BLOCK), tab_ref[0, h], f32)
                    for b in range(1, half):
                        low = jnp.where(n >= starts[b], tab_ref[b, h], low)
                if d >= 0:
                    high = jnp.full((BLOCK, BLOCK), tab_ref[half, h], f32)
                    for b in range(1, half):
                        high = jnp.where(n >= starts[b], tab_ref[half + b, h], high)
                if d < 0:
                    tile = low
                elif d > 0:
                    tile = high
                else:
                    tile = jnp.where(offset > 0, high, low)
                ref[h, d + 2] = tile
        for h in range(heads):
            ref[h, 0] = jnp.full((BLOCK, BLOCK), tab_ref[half - 1, h], f32)
            ref[h, 4] = jnp.full((BLOCK, BLOCK), tab_ref[2 * half - 1, h], f32)


def bias_tiles(table):
    buckets, heads = table.shape
    starts = bucket_starts(buckets)
    shape = jax.ShapeDtypeStruct((heads, 5, BLOCK, BLOCK), f32)
    return pl.pallas_call(
        partial(bias_kernel, starts, heads),
        in_specs=[pl.BlockSpec(memory_space=pltpu.SMEM)],
        out_shape=(shape, shape),
        compiler_params=params(6),
        cost_estimate=cost(2),
        name="bias_tiles",
    )(table)


def clipped(d):
    return jnp.minimum(jnp.maximum(d, -2), 2) + 2


def attend_kernel(heads, size, most, lo_ref, cnt_ref, qkv_ref, segq_ref, segk_ref, t_ref, ctx_ref, lse_ref, k_s, v_s):
    b = pl.program_id(0)
    inner = heads * size
    last = pl.num_programs(0) - 1

    @pl.when(b == 0)
    def _():
        for h in range(heads):
            k_s[h] = qkv_ref[:, inner + h * size : inner + (h + 1) * size]
            v_s[h] = qkv_ref[:, 2 * inner + h * size : 2 * inner + (h + 1) * size]

    def window(first, count, lo, pairs):
        rows = pl.ds(pl.multiple_of(first * BLOCK, BLOCK), count * BLOCK)
        block = qkv_ref[rows, :inner]
        seg_col = segq_ref[rows, :]
        spans = [pl.ds(pl.multiple_of((lo + 2 * i) * BLOCK, BLOCK), PAIR) for i in range(pairs)]
        allowed = [seg_col == segk_ref[:, span] for span in spans]
        outs, logs = [], []
        for h in range(heads):
            query = block[:, h * size : (h + 1) * size]
            scores = []
            for i, span in enumerate(spans):
                s = dot_nt(query, k_s[h, span, :])
                bias = jnp.concatenate(
                    [
                        jnp.concatenate(
                            [t_ref[h, clipped(lo + 2 * i + c - first - r)] for c in range(2)], axis=1
                        )
                        for r in range(count)
                    ],
                    axis=0,
                )
                scores.append(jnp.where(allowed[i], s + bias, masked_score))
            top = scores[0]
            for s in scores[1:]:
                top = jnp.maximum(top, s)
            largest = jnp.max(top, axis=1, keepdims=True)
            total = acc = None
            for i, span in enumerate(spans):
                p = jnp.exp(scores[i] - largest)
                total = p if total is None else total + p
                more = dot_nn(p.astype(bf16), v_s[h, span, :])
                acc = more if acc is None else acc + more
            total = jnp.sum(total, axis=1, keepdims=True)
            outs.append((acc / total).astype(bf16))
            lse = jnp.broadcast_to(largest + jnp.log(total), (count * BLOCK, BLOCK))
            lse_ref[h : h + 1, rows] = jnp.transpose(lse)[0:1, :]
        ctx_ref[rows, :] = jnp.concatenate(outs, axis=1)

    for pairs in range(1, most + 1):
        pl.when((b < last) & (cnt_ref[b] == pairs))(partial(window, 2 * b, 2, lo_ref[b], pairs))
    pl.when(b == last)(partial(window, 2 * b, 1, lo_ref[b], 1))


def attend(qkv, ranges, segs, tiles):
    lo, cnt = ranges
    segq_col, segq_row, segk_col, segk_row = segs
    total, wide = qkv.shape
    heads = tiles.shape[0]
    inner = wide // 3
    size = inner // heads
    steps = lo.shape[0]
    whole = lambda b, *_: (0, 0)
    return pl.pallas_call(
        partial(attend_kernel, heads, size, steps - 1),
        grid_spec=pltpu.PrefetchScalarGridSpec(
            num_scalar_prefetch=2,
            grid=(steps,),
            in_specs=[
                pl.BlockSpec((total, wide), whole, pipeline_mode=pl.Buffered(1)),
                pl.BlockSpec((total, 1), whole, pipeline_mode=pl.Buffered(1)),
                pl.BlockSpec((1, total), whole, pipeline_mode=pl.Buffered(1)),
                pl.BlockSpec((heads, 5, BLOCK, BLOCK), lambda b, *_: (0, 0, 0, 0), pipeline_mode=pl.Buffered(1)),
            ],
            out_specs=[
                pl.BlockSpec((total, inner), whole),
                pl.BlockSpec((8, total), whole),
            ],
            scratch_shapes=[
                pltpu.VMEM((heads, total, size), bf16),
                pltpu.VMEM((heads, total, size), bf16),
            ],
        ),
        out_shape=(
            jax.ShapeDtypeStruct((total, inner), bf16),
            jax.ShapeDtypeStruct((8, total), f32),
        ),
        compiler_params=params(12),
        cost_estimate=cost(9),
        name="attend",
    )(lo, cnt, qkv, segq_col, segk_row, tiles)


def attend_back_kernel(
    starts,
    heads,
    size,
    most,
    lo_ref,
    cnt_ref,
    qkv_ref,
    do_ref,
    ctx_ref,
    lse_ref,
    segk_ref,
    segq_ref,
    tt_ref,
    grad_ref,
    bias_ref,
    q_s,
    do_s,
    dq_s,
    delta_s,
    d_s,
):
    b = pl.program_id(0)
    last = pl.num_programs(0) - 1
    inner = heads * size
    half = len(starts)

    @pl.when(b == 0)
    def _():
        prod = do_ref[...].astype(f32) * ctx_ref[...].astype(f32)
        high = prod.astype(bf16)
        low = (prod - high.astype(f32)).astype(bf16)
        row = lax.broadcasted_iota(jnp.int32, (8, inner), 0)
        col = lax.broadcasted_iota(jnp.int32, (8, inner), 1)
        pick = ((col >= row * size) & (col < (row + 1) * size)).astype(f32).astype(bf16)
        delta_s[...] = dot_nt(pick, high) + dot_nt(pick, low)
        for h in range(heads):
            q_s[h] = qkv_ref[:, h * size : (h + 1) * size]
            do_s[h] = do_ref[:, h * size : (h + 1) * size]
        dq_s[...] = jnp.zeros(dq_s.shape, f32)
        d_s[...] = jnp.zeros(d_s.shape, f32)

    def window(first, count, lo, pairs):
        rows = pl.ds(pl.multiple_of(first * BLOCK, BLOCK), count * BLOCK)
        block = qkv_ref[rows, inner:]
        seg_col = segk_ref[rows, :]
        spans = [pl.ds(pl.multiple_of((lo + 2 * i) * BLOCK, BLOCK), PAIR) for i in range(pairs)]
        allowed = [seg_col == segq_ref[:, span] for span in spans]
        dks, dvs = [], []
        for h in range(heads):
            key = block[:, h * size : (h + 1) * size]
            value = block[:, inner + h * size : inner + (h + 1) * size]
            dk = dv = None
            for i, span in enumerate(spans):
                q = q_s[h, span, :]
                do = do_s[h, span, :]
                s = dot_nt(key, q)
                dp = dot_nt(value, do)
                at = [[clipped(first + r - lo - 2 * i - c) for c in range(2)] for r in range(count)]
                bias = jnp.concatenate(
                    [
                        jnp.concatenate([tt_ref[h, at[r][c]] for c in range(2)], axis=1)
                        for r in range(count)
                    ],
                    axis=0,
                )
                p = jnp.where(allowed[i], jnp.exp(s + bias - lse_ref[h : h + 1, span]), 0.0)
                ds = p * (dp - delta_s[h : h + 1, span])
                for r in range(count):
                    for c in range(2):
                        d_s[h, at[r][c]] += ds[
                            r * BLOCK : (r + 1) * BLOCK, c * BLOCK : (c + 1) * BLOCK
                        ]
                ds16 = ds.astype(bf16)
                dv_more = dot_nn(p.astype(bf16), do)
                dk_more = dot_nn(ds16, q)
                dv = dv_more if dv is None else dv + dv_more
                dk = dk_more if dk is None else dk + dk_more
                dq_s[h, :, span] += dot_tn(key, ds16)
            dks.append(dk)
            dvs.append(dv)
        grad_ref[rows, inner:] = jnp.concatenate(dks + dvs, axis=1).astype(bf16)

    for pairs in range(1, most + 1):
        pl.when((b < last) & (cnt_ref[b] == pairs))(partial(window, 2 * b, 2, lo_ref[b], pairs))
    pl.when(b == last)(partial(window, 2 * b, 1, lo_ref[b], 1))

    @pl.when(b == last)
    def _():
        grad_ref[:, :inner] = jnp.concatenate([jnp.transpose(dq_s[h]) for h in range(heads)], axis=1).astype(bf16)
        sub = lax.broadcasted_iota(jnp.int32, (BLOCK, BLOCK), 0)
        lane = lax.broadcasted_iota(jnp.int32, (BLOCK, BLOCK), 1)
        below = lane + sub > BLOCK - 1
        reverse = (lane + sub == BLOCK - 1).astype(f32)
        bucket_row = lax.broadcasted_iota(jnp.int32, (2 * half, BLOCK), 0)
        line_lane = lax.broadcasted_iota(jnp.int32, (2 * half, BLOCK), 1)
        picks = {}
        for d in (-1, 0, 1):
            for low in (False, True):
                offset = line_lane + (1 if low else 1 - BLOCK) + BLOCK * d
                n = jnp.abs(offset)
                bucket = jnp.where(offset > 0, half, 0)
                for e in range(1, half):
                    bucket = bucket + (n >= starts[e]).astype(jnp.int32)
                picks[d, low] = bucket == bucket_row
        for h in range(heads):
            whole = jnp.zeros((2 * half, BLOCK), f32)
            for d in (-1, 0, 1):
                tile = dot_exact(d_s[h, d + 2], reverse)
                for low in (False, True):
                    kept = jnp.where(below == low, tile, 0.0)
                    line = jnp.sum(
                        pltpu.roll(kept, 0, 1, stride=1, stride_axis=0), axis=0, keepdims=True
                    )
                    whole = whole + jnp.where(picks[d, low], line, 0.0)
            for e, d in ((half - 1, 0), (2 * half - 1, 4)):
                far = jnp.sum(d_s[h, d], axis=0, keepdims=True)
                whole = whole + jnp.where(bucket_row == e, far, 0.0)
            bias_ref[h] = whole


def attend_back(qkv, context_grad, context, lse, ranges, segs, tiles, buckets):
    lo, cnt = ranges
    segq_col, segq_row, segk_col, segk_row = segs
    total, wide = qkv.shape
    heads = tiles.shape[0]
    inner = wide // 3
    size = inner // heads
    steps = lo.shape[0]
    starts = bucket_starts(buckets)
    whole = lambda b, *_: (0, 0)
    return pl.pallas_call(
        partial(attend_back_kernel, starts, heads, size, steps - 1),
        grid_spec=pltpu.PrefetchScalarGridSpec(
            num_scalar_prefetch=2,
            grid=(steps,),
            in_specs=[
                pl.BlockSpec((total, wide), whole, pipeline_mode=pl.Buffered(1)),
                pl.BlockSpec((total, inner), whole, pipeline_mode=pl.Buffered(1)),
                pl.BlockSpec((total, inner), whole, pipeline_mode=pl.Buffered(1)),
                pl.BlockSpec((8, total), whole, pipeline_mode=pl.Buffered(1)),
                pl.BlockSpec((total, 1), whole, pipeline_mode=pl.Buffered(1)),
                pl.BlockSpec((1, total), whole, pipeline_mode=pl.Buffered(1)),
                pl.BlockSpec((heads, 5, BLOCK, BLOCK), lambda b, *_: (0, 0, 0, 0), pipeline_mode=pl.Buffered(1)),
            ],
            out_specs=[
                pl.BlockSpec((total, wide), whole),
                pl.BlockSpec((heads, buckets, BLOCK), lambda b, *_: (0, 0, 0)),
            ],
            scratch_shapes=[
                pltpu.VMEM((heads, total, size), bf16),
                pltpu.VMEM((heads, total, size), bf16),
                pltpu.VMEM((heads, size, total), f32),
                pltpu.VMEM((8, total), f32),
                pltpu.VMEM((heads, 5, BLOCK, BLOCK), f32),
            ],
        ),
        out_shape=(
            jax.ShapeDtypeStruct((total, wide), bf16),
            jax.ShapeDtypeStruct((heads, buckets, BLOCK), f32),
        ),
        compiler_params=params(16),
        cost_estimate=cost(15),
        name="attend_back",
    )(lo, cnt, qkv, context_grad, context, lse, segk_col, segq_row, tiles)


def pool_matrix(shape, axis, me, query_len, query_local):
    token = lax.broadcasted_iota(jnp.int32, shape, axis)
    query = lax.broadcasted_iota(jnp.int32, shape, 1 - axis)
    span = query_len * query_local
    holder = jnp.bitwise_xor(token // span, me)
    return (holder * query_local + token % span // query_len == query).astype(f32)


def score_kernel(query_len, query_local, docs, first_ref, emb_ref, qe_ref, seg_ref, chosen_ref, pos_ref, sums_ref, logit_ref, stat_ref, acc_s):
    b = pl.program_id(0)
    count = qe_ref.shape[0]

    @pl.when(b == 0)
    def _():
        acc_s[...] = jnp.zeros(acc_s.shape, f32)

    near = jnp.exp(sharpness * (dot_nt(emb_ref[...], qe_ref[...]) - 1.0))
    seg = seg_ref[...]
    for d in range(docs):
        acc_s[d : d + 1, :] += jnp.sum(jnp.where(seg == d, near, 0.0), axis=0, keepdims=True)

    @pl.when(b == pl.num_programs(0) - 1)
    def _():
        sums = acc_s[:docs, :]
        sums_ref[...] = acc_s[...]
        chosen = chosen_ref[:docs, :]
        smooth = 1.0 + jnp.log(sums) / sharpness
        pool = pool_matrix((count, pos_ref.shape[1]), 0, first_ref[1], query_len, query_local)
        picked = dot_exact(chosen * smooth, pool)
        counts = dot_exact(chosen, pool)
        logits = picked / jnp.maximum(counts, 1.0) / smoothing_divisor
        top = jnp.max(logits, axis=0, keepdims=True)
        spread = jnp.sum(jnp.exp(logits - top), axis=0, keepdims=True)
        doc = lax.broadcasted_iota(jnp.int32, logits.shape, 0) + first_ref[0]
        mine = doc == pos_ref[0:1, :]
        stat_ref[0:1, :] = top
        stat_ref[1:2, :] = spread
        stat_ref[2:3, :] = jnp.sum(jnp.where(mine, logits, 0.0), axis=0, keepdims=True)
        stat_ref[3:4, :] = jnp.sum(jnp.where(mine, counts, 0.0), axis=0, keepdims=True)
        stat_ref[4:8, :] = jnp.zeros((4, pos_ref.shape[1]), f32)
        logit_ref[0:docs, :] = logits
        logit_ref[docs : 2 * docs, :] = counts


def score(first, emb, query_emb, seg_col, chosen, positives, query_len, query_local, docs):
    count, width = query_emb.shape
    lanes = positives.shape[1]
    length = emb.shape[0]
    blocks = length // BLOCK
    whole = lambda b, *_: (0, 0)
    return pl.pallas_call(
        partial(score_kernel, query_len, query_local, docs),
        grid_spec=pltpu.PrefetchScalarGridSpec(
            num_scalar_prefetch=1,
            grid=(blocks,),
            in_specs=[
                pl.BlockSpec((BLOCK, width), lambda b, *_: (b, 0)),
                pl.BlockSpec((count, width), whole, pipeline_mode=pl.Buffered(1)),
                pl.BlockSpec((BLOCK, 1), lambda b, *_: (b, 0)),
                pl.BlockSpec((8, count), whole, pipeline_mode=pl.Buffered(1)),
                pl.BlockSpec((8, lanes), whole, pipeline_mode=pl.Buffered(1)),
            ],
            out_specs=[
                pl.BlockSpec((8, count), whole),
                pl.BlockSpec((8, lanes), whole),
                pl.BlockSpec((8, lanes), whole),
            ],
            scratch_shapes=[pltpu.VMEM((8, count), f32)],
        ),
        out_shape=(
            jax.ShapeDtypeStruct((8, count), f32),
            jax.ShapeDtypeStruct((8, lanes), f32),
            jax.ShapeDtypeStruct((8, lanes), f32),
        ),
        compiler_params=params(10),
        cost_estimate=cost(5),
        name="score",
    )(first, emb, query_emb, seg_col, chosen, positives)


def score_back_kernel(query_len, query_local, docs, first_ref, emb_ref, qe_ref, seg_ref, chosen_ref, pos_ref, sums_ref, logit_ref, stat_ref, demb_ref, dqe_ref, grad_s, dq_s):
    b = pl.program_id(0)
    count = qe_ref.shape[0]

    @pl.when(b == 0)
    def _():
        logits = logit_ref[0:docs, :]
        counts = logit_ref[docs : 2 * docs, :]
        doc = lax.broadcasted_iota(jnp.int32, logits.shape, 0) + first_ref[0]
        mine = (doc == pos_ref[0:1, :]).astype(f32)
        share = jnp.exp(logits - stat_ref[0:1, :]) / stat_ref[1:2, :]
        grad = (share - mine) / smoothing_divisor / jnp.maximum(counts, 1.0)
        spread = pool_matrix((logits.shape[1], count), 1, first_ref[1], query_len, query_local)
        grad_s[0:docs, :] = dot_exact(grad, spread) * chosen_ref[:docs, :] / sums_ref[:docs, :]
        dq_s[...] = jnp.zeros(dq_s.shape, f32)

    emb = emb_ref[...]
    near = jnp.exp(sharpness * (dot_nt(emb, qe_ref[...]) - 1.0))
    seg = seg_ref[...]
    weight = jnp.broadcast_to(grad_s[0:1, :], near.shape)
    for d in range(1, docs):
        weight = jnp.where(seg == d, grad_s[d : d + 1, :], weight)
    grad = (near * weight).astype(bf16)
    demb_ref[...] = dot_nn(grad, qe_ref[...])
    dq_s[...] += dot_tn(emb, grad)

    @pl.when(b == pl.num_programs(0) - 1)
    def _():
        dqe_ref[...] = jnp.transpose(dq_s[...]).astype(bf16)


def score_back(first, emb, query_emb, seg_col, chosen, positives, sums, logits, stats, query_len, query_local, docs):
    count, width = query_emb.shape
    lanes = positives.shape[1]
    length = emb.shape[0]
    blocks = length // BLOCK
    whole = lambda b, *_: (0, 0)
    return pl.pallas_call(
        partial(score_back_kernel, query_len, query_local, docs),
        grid_spec=pltpu.PrefetchScalarGridSpec(
            num_scalar_prefetch=1,
            grid=(blocks,),
            in_specs=[
                pl.BlockSpec((BLOCK, width), lambda b, *_: (b, 0)),
                pl.BlockSpec((count, width), whole, pipeline_mode=pl.Buffered(1)),
                pl.BlockSpec((BLOCK, 1), lambda b, *_: (b, 0)),
                pl.BlockSpec((8, count), whole, pipeline_mode=pl.Buffered(1)),
                pl.BlockSpec((8, lanes), whole, pipeline_mode=pl.Buffered(1)),
                pl.BlockSpec((8, count), whole, pipeline_mode=pl.Buffered(1)),
                pl.BlockSpec((8, lanes), whole, pipeline_mode=pl.Buffered(1)),
                pl.BlockSpec((8, lanes), whole, pipeline_mode=pl.Buffered(1)),
            ],
            out_specs=[
                pl.BlockSpec((BLOCK, width), lambda b, *_: (b, 0)),
                pl.BlockSpec((count, width), whole),
            ],
            scratch_shapes=[pltpu.VMEM((8, count), f32), pltpu.VMEM((width, count), f32)],
        ),
        out_shape=(
            jax.ShapeDtypeStruct((length, width), f32),
            jax.ShapeDtypeStruct((count, width), bf16),
        ),
        compiler_params=params(12),
        cost_estimate=cost(5),
        name="score_back",
    )(first, emb, query_emb, seg_col, chosen, positives, sums, logits, stats)


def full(*shape):
    return pl.BlockSpec(shape, lambda *_: (0,) * len(shape), pipeline_mode=pl.Buffered(1))


def kept(*shape):
    return pl.BlockSpec(shape, lambda *_: (0,) * len(shape))


def rows_of(count, width):
    return pl.BlockSpec((count, width), lambda b, *_: (b, 0))


SCALARS = pl.BlockSpec(memory_space=pltpu.SMEM)


def like(shape, dtype):
    return jax.ShapeDtypeStruct(shape, dtype)


def rms(values):
    return lax.rsqrt(jnp.mean(values * values, axis=-1, keepdims=True) + epsilon)


def choose_kernel(query_local, query_len, steps, place_ref, pos_ref, ret_ref, segq_ref, segk_ref, chosen_ref, rows_ref, colq_ref, colk_ref, ret_s):
    core, me = place_ref[0], place_ref[1]
    span = query_local * query_len
    blocks = ret_s.shape[0] // span

    def holder(p):
        return sum(((p >> s) & 1) << (steps - 1 - s) for s in range(steps))

    def held(p):
        return holder(jnp.bitwise_xor(me, p)) * 2 + core

    for p in range(blocks):
        start = pl.multiple_of(held(p) * span, span)
        ret_s[p * span : (p + 1) * span, :] = ret_ref[pl.ds(start, span), :].astype(f32)
    docs = ret_s.shape[1]
    row = lax.broadcasted_iota(jnp.int32, (docs, docs), 0)
    col = lax.broadcasted_iota(jnp.int32, (docs, docs), 1)
    shift = jnp.where(row < docs // 2, row + place_ref[2], -1)
    chosen_ref[...] = dot_nt((shift == col).astype(f32), ret_s[...])
    lane = lax.broadcasted_iota(jnp.int32, rows_ref.shape, 1)
    rows = jnp.full(rows_ref.shape, -1, jnp.int32)
    for p in range(blocks):
        for i in range(query_local):
            query = (holder(p) * 2 + core) * query_local + i
            rows = jnp.where(lane == p * query_local + i, pos_ref[query], rows)
    rows_ref[...] = rows
    for row_ref, col_ref in ((segq_ref, colq_ref), (segk_ref, colk_ref)):
        whole = jnp.broadcast_to(row_ref[...], (8, row_ref.shape[1]))
        col_ref[...] = jnp.transpose(whole)[:, 0:1]


def choose(place, positives, retrieved, seg_q, seg_k, query_local, query_len, steps):
    total, docs = retrieved.shape
    lanes = -(-(total // 2 // query_len) // BLOCK) * BLOCK
    tokens = seg_q.shape[1]
    return pl.pallas_call(
        partial(choose_kernel, query_local, query_len, steps),
        in_specs=[SCALARS, SCALARS] + [pl.BlockSpec(memory_space=pltpu.VMEM)] * 3,
        out_shape=(
            like((8, total // 2), f32),
            like((8, lanes), jnp.int32),
            like((tokens, 1), jnp.int32),
            like((tokens, 1), jnp.int32),
        ),
        scratch_shapes=[pltpu.VMEM((total // 2, docs), f32)],
        compiler_params=params(10),
        cost_estimate=cost(1),
        name="choose",
    )(place, positives, retrieved, seg_q, seg_k)


def pack_kernel(bit_ref, q_ref, k_ref, v_ref, o_ref, g_ref, u_ref, d_ref, b_ref, qkv_ref, half_qkv, half_o, half_gu, half_d):
    inner = q_ref.shape[1]
    hidden = g_ref.shape[1]
    for i, ref in enumerate((q_ref, k_ref, v_ref)):
        qkv_ref[:, i * inner : (i + 1) * inner] = ref[...]
    bit = bit_ref[0]
    rows = half_qkv.shape[0]
    span = pl.ds(pl.multiple_of(bit * rows, rows), rows)
    half_qkv[...] = qkv_ref[span, :]
    half_gu[:, :hidden] = g_ref[span, :]
    other = pl.ds(pl.multiple_of(bit_ref[1] * rows, rows), rows)
    half_gu[:, hidden:] = u_ref[other, :]
    rows = o_ref.shape[0] // 2
    half_o[:rows, :] = o_ref[pl.ds(pl.multiple_of(bit * rows, rows), rows), :]
    half_o[rows:, :] = jnp.zeros((half_o.shape[0] - rows, half_o.shape[1]), bf16)
    half_o[rows:, : b_ref.shape[1]] = b_ref[...]
    rows = half_d.shape[0]
    half_d[...] = d_ref[pl.ds(pl.multiple_of(bit * rows, rows), rows), :]


def pack(bit, q, k, v, o, gate, up, down, bias):
    depth, inner = q.shape
    hidden = gate.shape[1]
    return pl.pallas_call(
        pack_kernel,
        in_specs=[SCALARS] + [pl.BlockSpec(memory_space=pltpu.VMEM)] * 8,
        out_shape=(
            like((depth, 3 * inner), bf16),
            like((depth // 2, 3 * inner), bf16),
            like((inner // 2 + bias.shape[0], depth), bf16),
            like((depth // 2, 2 * hidden), bf16),
            like((hidden // 2, depth), bf16),
        ),
        compiler_params=params(12),
        cost_estimate=cost(1),
        name="pack",
    )(bit, q, k, v, o, gate, up, down, bias)


def enter_kernel(place_ref, kept_ref, near_ref, far_ref, cross_ref, gain_ref, w_ref, tok_ref, norm_ref, heads_ref):
    gain = gain_ref[...].astype(f32)
    mp = place_ref[0]
    shard = far_ref.shape[0]
    query = kept_ref.shape[0] - shard
    pieces = [(kept_ref, 0), (near_ref, 1), (far_ref, 2), (cross_ref, 3)]
    spans = [(ref, 0, shard, jnp.bitwise_xor(mp, i) * shard) for ref, i in pieces]
    spans += [
        (ref, shard, query, 4 * shard + jnp.bitwise_xor(mp % 2, i) * query) for ref, i in pieces[:2]
    ]
    for ref, first, count, start in spans:
        rows = pl.ds(pl.multiple_of(start, count), count)
        piece = ref[first : first + count, :]
        values = piece.astype(f32)
        normed = (values * rms(values) * gain).astype(bf16)
        tok_ref[rows, :] = piece
        norm_ref[rows, :] = normed
        heads_ref[rows, :] = dot_nn(normed, w_ref[...]).astype(bf16)


def enter(place, pieces, gain, weight):
    total = sum(piece.shape[0] for piece in pieces)
    depth, wide = weight.shape
    return pl.pallas_call(
        enter_kernel,
        in_specs=[SCALARS] + [pl.BlockSpec(memory_space=pltpu.VMEM)] * 6,
        out_shape=(like((total, depth), bf16), like((total, depth), bf16), like((total, wide), bf16)),
        compiler_params=params(12),
        cost_estimate=cost(3),
        name="enter",
    )(place, *pieces, gain, weight)


def gelu_parts(gate):
    inner = 0.7978845608028654 * (gate + 0.044715 * gate * gate * gate)
    return 0.5 * (1.0 + jnp.tanh(inner))


def ffn_own_kernel(tok_ref, near_ref, moved_ref, gain_ref, g_ref, u_ref, d_ref, mid_ref, norm_ref, gu_ref, part_ref):
    hidden = g_ref.shape[1]
    mid = tok_ref[...].astype(f32) + (near_ref[...].astype(f32) + moved_ref[...].astype(f32))
    mid_ref[...] = mid
    normed = (mid * rms(mid) * gain_ref[...].astype(f32)).astype(bf16)
    norm_ref[...] = normed
    gate = dot_nn(normed, g_ref[...])
    up = dot_nn(normed, u_ref[...])
    gu_ref[:, :hidden] = gate.astype(bf16)
    gu_ref[:, hidden:] = up.astype(bf16)
    part_ref[...] = dot_nn((gate * gelu_parts(gate) * up).astype(bf16), d_ref[...])


def ffn_own(tokens, near, moved, gain, gate, up, down, count):
    total, depth = tokens.shape
    hidden = gate.shape[1]
    return pl.pallas_call(
        ffn_own_kernel,
        grid=(total // count,),
        in_specs=[rows_of(count, depth)] * 3
        + [full(1, depth), full(depth, hidden), full(depth, hidden), full(hidden, depth)],
        out_specs=[
            rows_of(count, depth),
            rows_of(count, depth),
            rows_of(count, 2 * hidden),
            rows_of(count, depth),
        ],
        out_shape=(
            like((total, depth), f32),
            like((total, depth), bf16),
            like((total, 2 * hidden), bf16),
            like((total, depth), f32),
        ),
        compiler_params=params(16),
        cost_estimate=cost(5),
        name="ffn_own",
    )(tokens, near, moved, gain, gate, up, down)


def ffn_far_kernel(norm_ref, g_ref, u_ref, d_ref, part_ref, gu_ref, out_ref):
    hidden = d_ref.shape[0]
    normed = norm_ref[...]
    gate = dot_nn(normed, g_ref[...])
    up = dot_nn(normed, u_ref[...])
    gu_ref[:, :hidden] = gate.astype(bf16)
    gu_ref[:, hidden:] = up.astype(bf16)
    more = dot_nn((gate * gelu_parts(gate) * up).astype(bf16), d_ref[...])
    out_ref[...] = (part_ref[...] + more).astype(bf16)


def ffn_far(normed, gate, up, down, partial_sum, count):
    total, depth = normed.shape
    hidden = down.shape[0]
    return pl.pallas_call(
        ffn_far_kernel,
        grid=(total // count,),
        in_specs=[
            rows_of(count, depth),
            full(depth, hidden),
            full(depth, hidden),
            full(hidden, depth),
            rows_of(count, depth),
        ],
        out_specs=[rows_of(count, 2 * hidden), rows_of(count, depth)],
        out_shape=(like((total, 2 * hidden), bf16), like((total, depth), bf16)),
        compiler_params=params(14),
        cost_estimate=cost(5),
        name="ffn_far",
    )(normed, gate, up, down, partial_sum)


def leave_kernel(mid_ref, near_ref, moved_ref, gain_ref, w_ref, out_ref, proj_ref, emb_ref):
    out = mid_ref[...] + (near_ref[...].astype(f32) + moved_ref[...].astype(f32))
    out_ref[...] = out
    normed = (out * rms(out) * gain_ref[...].astype(f32)).astype(bf16)
    projected = dot_nn(normed, w_ref[...])
    proj_ref[...] = projected
    scale = lax.rsqrt(jnp.sum(projected * projected, axis=-1, keepdims=True) + epsilon)
    emb_ref[...] = (projected * scale).astype(bf16)


def leave(mid, near, moved, gain, weight, count):
    total, depth = mid.shape
    wide = weight.shape[1]
    return pl.pallas_call(
        leave_kernel,
        grid=(total // count,),
        in_specs=[rows_of(count, depth)] * 3 + [full(1, depth), full(depth, wide)],
        out_specs=[rows_of(count, depth), rows_of(count, wide), rows_of(count, wide)],
        out_shape=(like((total, depth), f32), like((total, wide), f32), like((total, wide), bf16)),
        compiler_params=params(10),
        cost_estimate=cost(4),
        name="leave",
    )(mid, near, moved, gain, weight)


def norm_back(values, gain, gradient):
    scale = rms(values)
    weighted = gradient * gain
    average = jnp.mean(weighted * values, axis=-1, keepdims=True)
    back = scale * weighted - values * (scale * scale * scale) * average
    return back, gradient * values * scale


def leave_back_kernel(core_ref, out_ref, proj_ref, near_ref, moved_ref, qn_ref, qm_ref, gain_ref, w_ref, grad_ref, wg_ref, gg_ref, emb_s):
    b = pl.program_id(0)
    last = pl.num_programs(0) - 1

    @pl.when(b == 0)
    def _():
        wg_ref[...] = jnp.zeros(wg_ref.shape, f32)
        gg_ref[...] = jnp.zeros(gg_ref.shape, f32)

    @pl.when(b < last)
    def _():
        emb_s[...] = near_ref[...] + moved_ref[...].astype(f32)

    @pl.when(b == last)
    def _():
        half = qn_ref.shape[0]
        core = core_ref[0]
        emb_s[pl.ds(pl.multiple_of(core * half, half), half), :] = qn_ref[...].astype(f32)
        emb_s[pl.ds(pl.multiple_of((1 - core) * half, half), half), :] = qm_ref[...].astype(f32)

    projected = proj_ref[...]
    scale = lax.rsqrt(jnp.sum(projected * projected, axis=-1, keepdims=True) + epsilon)
    unit = projected * scale
    grad = emb_s[...]
    grad = (scale * (grad - unit * jnp.sum(grad * unit, axis=-1, keepdims=True))).astype(bf16)
    out = out_ref[...]
    gain = gain_ref[...].astype(f32)
    normed = (out * rms(out) * gain).astype(bf16)
    wg_ref[...] += dot_tn(normed, grad)
    back, addends = norm_back(out, gain, dot_nt(grad, w_ref[...]))
    grad_ref[...] = back
    gg_ref[0:1, :] += jnp.sum(addends, axis=0, keepdims=True)


def leave_back(core, layer_out, projected, near, moved, query_near, query_moved, gain, weight):
    total, depth = layer_out.shape
    wide = weight.shape[1]
    count = total - near.shape[0]
    steps = total // count
    clamp = pl.BlockSpec((count, wide), lambda b, *_: (jnp.minimum(b, steps - 2), 0))
    return pl.pallas_call(
        leave_back_kernel,
        grid=(steps,),
        in_specs=[
            SCALARS,
            rows_of(count, depth),
            rows_of(count, wide),
            clamp,
            clamp,
            full(count // 2, wide),
            full(count // 2, wide),
            full(1, depth),
            full(depth, wide),
        ],
        out_specs=[rows_of(count, depth), kept(depth, wide), kept(8, depth)],
        out_shape=(like((total, depth), f32), like((depth, wide), f32), like((8, depth), f32)),
        scratch_shapes=[pltpu.VMEM((count, wide), f32)],
        compiler_params=params(8),
        cost_estimate=cost(5),
        name="leave_back",
    )(core, layer_out, projected, near, moved, query_near, query_moved, gain, weight)


def ffn_back_kernel(hidden, own, *refs):
    gate_s, up_s, down_s = refs[-3:]
    if own:
        index_ref, grad_ref, norm_ref, gu_ref, d_ref, g_ref, u_ref, part_in, down_in = refs[:9]
        nf_ref, a_ref, b_ref, *downs = refs[9:-3]
    else:
        grad_ref, norm_ref, gu_ref, d_ref, g_ref, u_ref, nf_ref, a_ref, b_ref, down_ref = refs[:-3]
    b = pl.program_id(0)

    @pl.when(b == 0)
    def _():
        gate_s[...] = jnp.zeros(gate_s.shape, f32)
        up_s[...] = jnp.zeros(up_s.shape, f32)
        down_s[...] = jnp.zeros(down_s.shape, f32)

    grad = grad_ref[...].astype(bf16)
    gate = gu_ref[:, :hidden].astype(f32)
    up = gu_ref[:, hidden:].astype(f32)
    hidden_grad = dot_nt(grad, d_ref[...])
    half = gelu_parts(gate)
    curve = 0.7978845608028654 * (1.0 + 0.134145 * gate * gate)
    slope = half + 2.0 * gate * half * (1.0 - half) * curve
    act = gate * half
    gate_grad = (hidden_grad * up * slope).astype(bf16)
    up_grad = (hidden_grad * act).astype(bf16)
    normed = norm_ref[...]
    gate_s[...] += dot_tn(normed, gate_grad)
    up_s[...] += dot_tn(normed, up_grad)
    down_s[...] += dot_tn(grad, (act * up).astype(bf16))
    back = dot_nt(gate_grad, g_ref[...]) + dot_nt(up_grad, u_ref[...])
    nf_ref[...] = (part_in[...] + back).astype(bf16) if own else back

    @pl.when(b == pl.num_programs(0) - 1)
    def _():
        cut = a_ref.shape[1]
        a_ref[...] = gate_s[:, :cut].astype(bf16)
        b_ref[:, : hidden - cut] = gate_s[:, cut:].astype(bf16)
        b_ref[:, hidden - cut :] = up_s[...].astype(bf16)
        if not own:
            down_ref[...] = down_s[...].astype(bf16)
        else:
            for k, ref in enumerate(downs):
                size = ref.shape[0]
                rows = pl.ds(pl.multiple_of(jnp.bitwise_xor(index_ref[0], k) * size, size), size)
                ref[:, :hidden] = down_in[rows, :]
                ref[:, hidden:] = down_s[rows, :].astype(bf16)


def ffn_back(grad, normed, gate_up, down, gate, up, count, index=None, part_sum=None, far_down=None):
    total, depth = normed.shape
    hidden = down.shape[0]
    own = index is not None
    quarter = depth // 4
    downs = [(quarter, 2 * hidden)] * 4 if own else [(depth, hidden)]
    shapes = [(depth, hidden // 2), (depth, hidden + hidden // 2)] + downs
    return pl.pallas_call(
        partial(ffn_back_kernel, hidden, own),
        grid=(total // count,),
        in_specs=([SCALARS] if own else [])
        + [
            rows_of(count, depth),
            rows_of(count, depth),
            rows_of(count, 2 * hidden),
            full(hidden, depth),
            full(depth, hidden),
            full(depth, hidden),
        ]
        + ([rows_of(count, depth), full(depth, hidden)] if own else []),
        out_specs=[rows_of(count, depth)] + [kept(*shape) for shape in shapes],
        out_shape=(like((total, depth), bf16 if own else f32),) + tuple(like(shape, bf16) for shape in shapes),
        scratch_shapes=[pltpu.VMEM((depth, hidden), f32)] * 3,
        compiler_params=params(28),
        cost_estimate=cost(10),
        name="ffn_back",
    )(*([index] if own else []), grad, normed, gate_up, down, gate, up, *([part_sum, far_down] if own else []))


def mid_back_kernel(near_ref, moved_ref, mid_ref, grad_ref, gain_ref, c0_ref, c1_ref, w0_ref, w1_ref, out_ref, dc0_ref, dc1_ref, ow0_ref, ow1_ref, gg_ref, o0_s, o1_s):
    b = pl.program_id(0)

    @pl.when(b == 0)
    def _():
        o0_s[...] = jnp.zeros(o0_s.shape, f32)
        o1_s[...] = jnp.zeros(o1_s.shape, f32)
        gg_ref[...] = jnp.zeros(gg_ref.shape, f32)

    gradient = near_ref[...].astype(f32) + moved_ref[...].astype(f32)
    back, addends = norm_back(mid_ref[...], gain_ref[...].astype(f32), gradient)
    mid_grad = grad_ref[...] + back
    out_ref[...] = mid_grad
    gg_ref[0:1, :] += jnp.sum(addends, axis=0, keepdims=True)
    rounded = mid_grad.astype(bf16)
    dc0_ref[...] = dot_nt(rounded, w0_ref[...]).astype(bf16)
    dc1_ref[...] = dot_nt(rounded, w1_ref[...]).astype(bf16)
    o0_s[...] += dot_tn(rounded, c0_ref[...])
    o1_s[...] += dot_tn(rounded, c1_ref[...])

    @pl.when(b == pl.num_programs(0) - 1)
    def _():
        ow0_ref[...] = o0_s[...].astype(bf16)
        ow1_ref[...] = o1_s[...].astype(bf16)


def mid_back(near, moved, mid, grad, gain, contexts, weights, count):
    total, depth = mid.shape
    inner = weights[0].shape[0]
    return pl.pallas_call(
        mid_back_kernel,
        grid=(total // count,),
        in_specs=[rows_of(count, depth)] * 4
        + [full(1, depth)]
        + [rows_of(count, inner)] * 2
        + [full(inner, depth)] * 2,
        out_specs=[
            rows_of(count, depth),
            rows_of(count, inner),
            rows_of(count, inner),
            kept(depth, inner),
            kept(depth, inner),
            kept(8, depth),
        ],
        out_shape=(
            like((total, depth), f32),
            like((total, inner), bf16),
            like((total, inner), bf16),
            like((depth, inner), bf16),
            like((depth, inner), bf16),
            like((8, depth), f32),
        ),
        scratch_shapes=[pltpu.VMEM((depth, inner), f32)] * 2,
        compiler_params=params(16),
        cost_estimate=cost(6),
        name="mid_back",
    )(near, moved, mid, grad, gain, *contexts, *weights)


def heads_far_kernel(norm_ref, grad_ref, ow_ref, out_ref):
    wide = grad_ref.shape[1]
    out_ref[:, :wide] = dot_tn(norm_ref[...], grad_ref[...]).astype(bf16)
    out_ref[:, wide:] = ow_ref[...]


def heads_far(normed, grads, output_grad):
    total, depth = normed.shape
    wide = grads.shape[1] + output_grad.shape[1]
    return pl.pallas_call(
        heads_far_kernel,
        in_specs=[pl.BlockSpec(memory_space=pltpu.VMEM)] * 3,
        out_shape=like((depth, wide), bf16),
        compiler_params=params(10),
        cost_estimate=cost(3),
        name="heads_far",
    )(normed, grads, output_grad)


def heads_own_kernel(index_ref, norm_ref, grad_ref, ow_ref, moved_ref, *refs):
    outs, sum_s = refs[:4], refs[4]
    wide = grad_ref.shape[1]
    sum_s[:, :wide] = dot_tn(norm_ref[...], grad_ref[...]) + moved_ref[:, :wide].astype(f32)
    sum_s[:, wide:] = ow_ref[...].astype(f32) + moved_ref[:, wide:].astype(f32)
    for k, ref in enumerate(outs):
        count = ref.shape[0]
        start = pl.multiple_of(jnp.bitwise_xor(index_ref[0], k) * count, count)
        ref[...] = sum_s[pl.ds(start, count), :].astype(bf16)


def heads_own(index, normed, grads, output_grad, moved):
    total, depth = normed.shape
    wide = moved.shape[1]
    return pl.pallas_call(
        heads_own_kernel,
        in_specs=[SCALARS] + [pl.BlockSpec(memory_space=pltpu.VMEM)] * 4,
        out_shape=(like((depth // 4, wide), bf16),) * 4,
        scratch_shapes=[pltpu.VMEM((depth, wide), f32)],
        compiler_params=params(12),
        cost_estimate=cost(3),
        name="heads_own",
    )(index, normed, grads, output_grad, moved)


def quarter_kernel(index_ref, near_ref, moved_ref, *outs):
    for k, ref in enumerate(outs):
        count = ref.shape[0]
        rows = pl.ds(pl.multiple_of(jnp.bitwise_xor(index_ref[0], k) * count, count), count)
        ref[...] = (near_ref[rows, :].astype(f32) + moved_ref[rows, :].astype(f32)).astype(bf16)


def quarter_sums(index, near, moved):
    depth, wide = near.shape
    return pl.pallas_call(
        quarter_kernel,
        in_specs=[SCALARS] + [pl.BlockSpec(memory_space=pltpu.VMEM)] * 2,
        out_shape=(like((depth // 4, wide), bf16),) * 4,
        compiler_params=params(8),
        cost_estimate=cost(1),
        name="quarter_sums",
    )(index, near, moved)


def enter_back_kernel(place_ref, tok_ref, own_ref, far_ref, w0_ref, w1_ref, kept_ref, sent_ref, gg_ref, na_s):
    core = place_ref[0] % 2
    total = tok_ref.shape[0]
    own_half = kept_ref.shape[0]
    gg_ref[...] = jnp.zeros(gg_ref.shape, f32)
    count = total // 3
    for i in range(3):
        rows = slice(i * count, (i + 1) * count)
        grad = dot_nt(own_ref[rows, :], w0_ref[...]) + dot_nt(far_ref[rows, :], w1_ref[...])
        values = tok_ref[rows, :].astype(f32)
        gg_ref[0:1, :] += jnp.sum(grad * values * rms(values), axis=0, keepdims=True)
        na_s[rows, :] = grad.astype(bf16)
    shard, query = split_of(total, own_half)
    for ref, which in ((kept_ref, core), (sent_ref, 1 - core)):
        for i in range(2):
            start = pl.multiple_of((which + 2 * i) * shard, shard)
            ref[i * shard : (i + 1) * shard, :] = na_s[pl.ds(start, shard), :]
        start = pl.multiple_of(4 * shard + which * query, query)
        ref[2 * shard :, :] = na_s[pl.ds(start, query), :]


def widen_kernel(groups, cuts, index_ref, *refs):
    outs = refs[4 * groups : 4 * groups + len(cuts)]
    scratch = list(refs[4 * groups + len(cuts) :])
    for (sources, turned), out in zip(cuts, outs):
        target = scratch.pop(0) if turned else out
        at = 0
        for group, first, last in sources:
            for k, ref in enumerate(refs[4 * group : 4 * group + 4]):
                count = ref.shape[0]
                rows = pl.ds(pl.multiple_of(jnp.bitwise_xor(index_ref[0], k) * count, count), count)
                target[rows, at : at + last - first] = ref[:, first:last].astype(f32)
            at += last - first
        if turned:
            out[...] = jnp.transpose(target[...])


def widened(index, groups, cuts, name):
    depth = groups[0][0].shape[0] * 4
    widths = [sum(last - first for _, first, last in sources) for sources, _ in cuts]
    return pl.pallas_call(
        partial(widen_kernel, len(groups), cuts),
        in_specs=[SCALARS] + [pl.BlockSpec(memory_space=pltpu.VMEM)] * (4 * len(groups)),
        out_shape=tuple(
            like((wide, depth) if turned else (depth, wide), f32) for wide, (_, turned) in zip(widths, cuts)
        ),
        scratch_shapes=[pltpu.VMEM((depth, wide), f32) for wide, (_, turned) in zip(widths, cuts) if turned],
        compiler_params=params(20),
        cost_estimate=cost(3),
        name=name,
    )(index, *[piece for group in groups for piece in group])


def split_of(total, half):
    query = half - (half // BLOCK) * BLOCK
    return (half - query) // 2, query


def enter_back(place, tokens, own, far, weights):
    total, depth = tokens.shape
    return pl.pallas_call(
        enter_back_kernel,
        in_specs=[SCALARS] + [pl.BlockSpec(memory_space=pltpu.VMEM)] * 5,
        out_shape=(like((total // 2, depth), bf16),) * 2 + (like((8, depth), f32),),
        scratch_shapes=[pltpu.VMEM((total, depth), bf16)],
        compiler_params=params(16),
        cost_estimate=cost(4),
        name="enter_back",
    )(place, tokens, own, far, *weights)


def inputs_back_kernel(place_ref, tok_ref, mid_ref, near_ref, moved_ref, gain_ref, stay_ref, leave_ref, query_ref):
    core, x = place_ref[0] % 2, place_ref[0] // 2
    total = tok_ref.shape[0]
    shard, query = split_of(total, near_ref.shape[0])
    gain = gain_ref[...].astype(f32)

    def piece(start, at, count):
        rows = pl.ds(pl.multiple_of(start, count), count)
        at = pl.ds(pl.multiple_of(at, count), count)
        gradient = near_ref[at, :].astype(f32) + moved_ref[at, :].astype(f32)
        back, _ = norm_back(tok_ref[rows, :].astype(f32), gain, gradient)
        return mid_ref[rows, :] + back

    leave_ref[...] = piece((core + 2 * (1 - x)) * shard, (1 - x) * shard, shard).astype(bf16)
    stay_ref[...] = piece((core + 2 * x) * shard, x * shard, shard)
    query_ref[...] = piece(4 * shard + core * query, 2 * shard, query)


def inputs_back(place, tokens, mid_grad, near, moved, gain):
    total, depth = tokens.shape
    shard, query = split_of(total, near.shape[0])
    return pl.pallas_call(
        inputs_back_kernel,
        in_specs=[SCALARS] + [pl.BlockSpec(memory_space=pltpu.VMEM)] * 5,
        out_shape=(like((shard, depth), f32), like((shard, depth), bf16), like((query, depth), f32)),
        compiler_params=params(12),
        cost_estimate=cost(2),
        name="inputs_back",
    )(place, tokens, mid_grad, near, moved, gain)


def swapped(bit, mine, theirs, axis=0):
    first = jnp.where(bit == 0, mine, theirs)
    second = jnp.where(bit == 0, theirs, mine)
    return jnp.concatenate([first, second], axis=axis)


def after(values, *earlier):
    return lax.optimization_barrier((values,) + earlier)[0]


def part(values, index, parts, axis=0):
    size = values.shape[axis] // parts
    return lax.dynamic_slice_in_dim(values, index * size, size, axis)


def shards(
    doc_tokens,
    query_tokens,
    doc_segments,
    query_keep,
    retrieved,
    positives,
    attn_gain,
    query_weight,
    key_weight,
    value_weight,
    output_weight,
    position_bias,
    ffn_gain,
    gate_weight,
    up_weight,
    down_weight,
    final_gain,
    proj_weight,
):
    groups = lax.axis_size("dp")
    tensor_size = lax.axis_size("mp")
    bits = groups.bit_length() - 1
    dp = lax.axis_index("dp")
    mp = lax.axis_index("mp")
    x = mp // 2
    core = mp % 2
    row_count, shard_len, width = doc_tokens.shape
    length = shard_len * tensor_size
    query_local, query_len, _ = query_tokens.shape
    chip_queries = query_local * 2
    buckets = position_bias.shape[0]
    hidden_local = gate_weight.shape[1]
    doc_local = retrieved.shape[2]
    docs_row = doc_local // row_count
    query_total = query_keep.shape[0]
    vector_width = proj_weight.shape[1]
    inner = query_weight.shape[1]

    def over(axis, size, mask):
        pairs = [(i, i ^ mask) for i in range(size)]
        return lambda values: lax.ppermute(values, axis, pairs)

    to_x = over("mp", tensor_size, 2)
    to_core = over("mp", tensor_size, 1)
    to_dp = [over("dp", groups, 1 << b) for b in range(bits)]
    dp_bit = [(dp >> b) & 1 for b in range(bits)]

    def exchange(steps):
        dp_mask = sum(1 << b for axis, b in steps if axis == "dp")
        mp_mask = 2 if any(axis == "x" for axis, b in steps) else 0
        pairs = [
            (i, ((i // tensor_size) ^ dp_mask) * tensor_size + ((i % tensor_size) ^ mp_mask))
            for i in range(groups * tensor_size)
        ]
        return lambda values: lax.ppermute(values, ("dp", "mp"), pairs)

    def rounds(order):
        out = []
        for i in range(0, len(order), 2):
            steps = order[i : i + 2]
            if len(steps) == 1:
                out.append([exchange(steps)])
            else:
                out.append([exchange(steps[:1]), exchange(steps[1:]), exchange(steps)])
        return out

    kept_rows = lax.dynamic_index_in_dim(doc_tokens, x, 0, keepdims=False)
    sent_rows = lax.dynamic_index_in_dim(doc_tokens, 1 - x, 0, keepdims=False)
    far_rows = to_x(sent_rows)
    kept_tokens = jnp.concatenate(
        [kept_rows, query_tokens.reshape(query_local * query_len, width)], axis=0
    )
    near_tokens = to_core(kept_tokens)
    cross_rows = to_core(far_rows)

    own_qkv, qkv_half, output_half, gate_up_half, down_half = pack(
        jnp.stack(dp_bit[:2]),
        after(query_weight, sent_rows),
        key_weight,
        value_weight,
        output_weight,
        gate_weight,
        up_weight,
        down_weight,
        position_bias,
    )
    qkv_half = to_x(qkv_half)
    output_half = to_x(output_half)
    gate_up_half = to_x(gate_up_half)
    down_half = to_x(down_half)
    far_bias = output_half[inner // 2 :, : position_bias.shape[1]]
    output_half = output_half[: inner // 2]

    def other_half(got, b=0):
        return swapped(dp_bit[b], got, to_dp[b](got))

    near_tiles = bias_tiles(position_bias.astype(f32))
    far_tiles = bias_tiles(far_bias.astype(f32))
    tiles = (near_tiles, far_tiles)

    row_segments = lax.dynamic_index_in_dim(doc_segments, x, 0, keepdims=False)
    chip_keep = lax.dynamic_slice_in_dim(
        query_keep, (dp * tensor_size + x * 2) * query_local, chip_queries, 0
    ).reshape(-1)
    query_ids = jnp.arange(chip_queries * query_len, dtype=jnp.int32) // query_len + docs_row
    seg_q = jnp.concatenate([row_segments, query_ids])
    seg_k = jnp.concatenate([row_segments, jnp.where(chip_keep > 0, query_ids, -1)])
    blocked = row_segments.reshape(-1, PAIR)
    low = jnp.sum((row_segments[None, :] < blocked[:, :1]).astype(jnp.int32), axis=1)
    high = jnp.sum((row_segments[None, :] <= blocked[:, -1:]).astype(jnp.int32), axis=1)
    low_block = low // BLOCK
    high_block = (high + BLOCK - 1) // BLOCK
    lo = jnp.concatenate([low_block, jnp.full((1,), length // BLOCK - 1, jnp.int32)])
    cnt = jnp.concatenate([(high_block - low_block + 1) // 2, jnp.ones((1,), jnp.int32)])
    ranges = (lo, cnt)

    order = [("dp", b) for b in reversed(range(bits))] + [("x", 0)]
    place = sum((x if axis == "x" else dp_bit[b]) << s for s, (axis, b) in enumerate(order))
    kept_retrieved = (query_keep[:, :, None] * retrieved).reshape(query_total * query_len, doc_local)
    seg_q, seg_k = seg_q[None, :], seg_k[None, :]
    chosen, pos_rows, col_q, col_k = choose(
        jnp.stack([core, place, x * docs_row]),
        positives,
        kept_retrieved,
        seg_q,
        seg_k,
        query_local,
        query_len,
        bits + 1,
    )
    segs = (col_q, seg_q, col_k, seg_k)
    half_queries = query_total // 2
    query_lanes = pos_rows.shape[1]

    place_mp = mp.reshape(1)
    gain_attn, gain_ffn, gain_final = [g.reshape(1, width) for g in (attn_gain, ffn_gain, final_gain)]
    pieces = (kept_tokens, near_tokens, far_rows, cross_rows)
    own_qkv = after(own_qkv, chosen)
    tokens, normed_attn, own_heads = enter(place_mp, pieces, gain_attn, own_qkv)
    far_qkv = other_half(after(qkv_half, own_heads))
    own_context, own_log = attend(own_heads, ranges, segs, near_tiles[0])
    far_heads = dot_nn(normed_attn, after(far_qkv, own_context)).astype(bf16)
    far_output = other_half(after(output_half, far_qkv))
    far_context, far_log = attend(far_heads, ranges, segs, far_tiles[0])
    far_output = after(far_output, far_context)
    gate_up_half = after(gate_up_half, far_output)
    far_gate = other_half(gate_up_half[:, :hidden_local])
    far_up = other_half(gate_up_half[:, hidden_local:], 1)
    heads = (own_heads, far_heads)
    contexts = (own_context, far_context)
    logs = (own_log, far_log)
    qkv_weights = (own_qkv, far_qkv)
    output_weights = (output_weight, far_output)
    attn_part = sum(dot_nn(c, w) for c, w in zip(contexts, output_weights)).astype(bf16)
    count = tokens.shape[0] // 3
    mid, normed_ffn, own_gate_up, ffn_sum = ffn_own(
        tokens, attn_part, to_core(attn_part), gain_ffn, gate_weight, up_weight, down_weight, count
    )
    far_down = other_half(after(down_half, mid))
    far_gate_up_out, ffn_part = ffn_far(
        normed_ffn, *after((far_gate, far_up), ffn_sum), far_down, ffn_sum, count
    )
    layer_out, projected, embedded = leave(
        mid, ffn_part, to_core(ffn_part), gain_final, proj_weight, count
    )

    doc_embedded = embedded[:length]
    query_emb = part(embedded[length:], core, 2)
    for moves in rounds(order):
        query_emb = jnp.concatenate([query_emb] + [move(query_emb) for move in moves], axis=0)
    first_doc = jnp.stack([dp * doc_local + x * docs_row, place])
    seg_col = col_q
    sums, logits, stats = score(
        first_doc, doc_embedded, query_emb, seg_col, chosen, pos_rows, query_len, query_local, docs_row
    )
    for moves in rounds(order[::-1]):
        every = [stats] + [move(stats) for move in moves]
        top = every[0][0:1]
        for moved in every[1:]:
            top = jnp.maximum(top, moved[0:1])
        total = sum(moved[1:2] * jnp.exp(moved[0:1] - top) for moved in every)
        stats = jnp.concatenate([top, total, sum(moved[2:] for moved in every)], axis=0)
    valid = jnp.arange(query_lanes) < half_queries
    loss_sum = jnp.sum(jnp.where(valid, stats[0] + jnp.log(stats[1]) - stats[2], 0.0))
    found_sum = jnp.sum(jnp.where(valid & (stats[3] > 0.5), 1.0, 0.0))
    ends = jnp.broadcast_to(jnp.stack([loss_sum, found_sum])[:, None], (2, BLOCK))
    ends = (ends + to_core(ends)) / query_total
    loss_value = ends[0, 0]
    found_share = ends[1, 0]

    demb, dqe = score_back(
        first_doc,
        doc_embedded,
        query_emb,
        seg_col,
        chosen,
        pos_rows,
        sums,
        logits,
        stats,
        query_len,
        query_local,
        docs_row,
    )
    demb_moved = to_core(demb.astype(bf16))
    for moves in reversed(rounds(order)):
        pieces = jnp.split(dqe, len(moves) + 1, axis=0)
        moved = [move(piece).astype(f32) for move, piece in zip(moves, pieces[1:])]
        dqe = sum(moved, pieces[0].astype(f32)).astype(bf16)
    dqe_moved = to_core(dqe)

    def widen(values):
        return values.astype(f32)

    def narrow(values):
        return values.astype(bf16)

    def added(*values):
        return narrow(sum(widen(v) for v in values[1:]) + widen(values[0]))

    four = [exchange([("dp", 0)]), exchange([("dp", 1)]), exchange([("dp", 0), ("dp", 1)])]
    four_index = (dp % 4).reshape(1)
    rest = range(2, bits)

    def scattered(pieces):
        return (pieces[0],) + tuple(move(piece) for move, piece in zip(four, pieces[1:]))

    def rest_of(values, moved):
        values = added(values, moved)
        for b in rest[1:]:
            values = added(values, to_dp[b](values))
        return values

    def gathered(values):
        return (values,) + tuple(move(values) for move in four)

    def assembled(pieces):
        low = [jnp.where(dp_bit[0] == 0, pieces[0], pieces[1]), jnp.where(dp_bit[0] == 0, pieces[1], pieces[0])]
        high = [jnp.where(dp_bit[0] == 0, pieces[2], pieces[3]), jnp.where(dp_bit[0] == 0, pieces[3], pieces[2])]
        return jnp.concatenate(
            [jnp.where(dp_bit[1] == 0, u, v) for u, v in zip(low + high, high + low)], axis=0
        )

    layer_out_grad, proj_grad, final_gain_part = leave_back(
        core.reshape(1), layer_out, projected, demb, demb_moved, dqe, dqe_moved, gain_final, proj_weight
    )
    proj_part = narrow(part(proj_grad, core, 2))
    proj_moved = to_x(proj_part)
    nf_sum, far_first, far_rest, far_down_grad = ffn_back(
        after(layer_out_grad, proj_part), normed_ffn, far_gate_up_out, far_down, far_gate, far_up, count
    )
    first_moved = to_x(far_first)
    proj_part = added(proj_part, after(proj_moved, far_first))
    proj_moves = [move(proj_part) for move in four]
    nf_part, own_first, own_rest, *down_pieces = ffn_back(
        after(layer_out_grad, proj_part),
        normed_ffn,
        own_gate_up,
        down_weight,
        gate_weight,
        up_weight,
        count,
        four_index,
        nf_sum,
        far_down_grad,
    )
    first_pieces = quarter_sums(four_index, own_first, after(first_moved, nf_part))
    first_moves = scattered(first_pieces)
    rest_moved = to_x(after(far_rest, first_pieces))
    down_moves = scattered(tuple(down_pieces))
    proj_part = added(*after((proj_part, *proj_moves), first_pieces))
    proj_moved = to_dp[rest[0]](proj_part)
    nf_part = after(nf_part, proj_part)
    mid_grad, own_context_grad, far_context_grad, own_out, far_out, ffn_gain_part = mid_back(
        nf_part, to_core(nf_part), mid, layer_out_grad, gain_ffn, contexts, output_weights, count
    )

    far_grads, far_bias_grad = attend_back(
        far_heads,
        far_context_grad,
        far_context,
        far_log,
        ranges,
        segs,
        far_tiles[1],
        buckets,
    )
    far_all = heads_far(normed_attn, far_grads, far_out)

    down = added(*after(down_moves, far_all))
    down_kept, down_moved = down[:, hidden_local:], to_x(down[:, :hidden_local])
    all_moved = to_x(after(far_all, down))
    first = added(*after(first_moves, far_all))
    first_moved = to_dp[rest[0]](first)
    rest_pieces = quarter_sums(four_index, own_rest, after(rest_moved, far_all))
    rest_moves = scattered(rest_pieces)
    proj_part = rest_of(proj_part, after(proj_moved, far_all))
    own_grads, own_bias_grad = attend_back(
        own_heads,
        after(own_context_grad, rest_pieces, first, down, proj_part),
        own_context,
        own_log,
        ranges,
        segs,
        near_tiles[1],
        buckets,
    )

    others = added(*after(rest_moves, own_grads))
    others_moved = to_dp[rest[0]](others)
    down = added(after(down_moved, own_grads), down_kept)
    down_moved = to_dp[rest[0]](down)
    first = rest_of(first, after(first_moved, own_grads))
    first_all = gathered(first)
    na_kept, na_sent, attn_gain_part = enter_back(
        place_mp, tokens, after(own_grads, others, down, first), far_grads, qkv_weights
    )
    all_pieces = heads_own(four_index, normed_attn, own_grads, own_out, after(all_moved, na_sent))
    all_moves = scattered(all_pieces)
    na_moved = to_core(after(na_sent, all_pieces))

    stay, leaving, query_grad = inputs_back(place_mp, tokens, mid_grad, na_kept, na_moved, gain_attn)
    back = to_x(leaving)
    others = rest_of(others, after(others_moved, leaving))
    down = rest_of(down, after(down_moved, leaving))
    others_all = gathered(others)
    down_all = gathered(down)
    both = added(*after(all_moves, others, down))
    both_moved = to_dp[rest[0]](both)

    lanes = BLOCK
    gains = jnp.concatenate(
        [
            (0.5 * final_gain_part[0]).reshape(-1, lanes),
            (0.5 * ffn_gain_part[0]).reshape(-1, lanes),
            attn_gain_part[0].reshape(-1, lanes),
        ],
        axis=0,
    )
    gain_rows = gains.shape[0]
    bias_rows = [
        jnp.pad(jnp.sum(g, axis=-1), ((0, 0), (0, lanes - buckets)))
        for g in (own_bias_grad, far_bias_grad)
    ]
    packet = jnp.concatenate([gains, bias_rows[0]], axis=0)
    packet_moved = to_x(after(jnp.concatenate([gains, bias_rows[1]], axis=0), all_pieces))
    packet = packet + after(packet_moved, both)
    packet_moves = [move(packet) for move in four]
    proj_moved = to_core(after(proj_part, both))

    both = rest_of(both, after(both_moved, packet))
    both_all = gathered(both)
    packet = sum(after(packet_moves, both), packet)
    for b in rest:
        packet = packet + to_dp[b](packet)
    cut = hidden_local // 2
    gate_weight_grad, up_weight_grad, down_weight_grad = widened(
        four_index,
        after((first_all, others_all, down_all), both),
        (
            (((0, 0, cut), (1, 0, cut)), False),
            (((1, cut, cut + hidden_local),), False),
            (((2, 0, hidden_local),), True),
        ),
        "widen_ffn",
    )
    packet = after(packet, up_weight_grad)
    position_bias_grad = jnp.transpose(packet[gain_rows:, :buckets])
    gains = packet[:gain_rows]
    gains = (gains + to_core(gains)).reshape(3, width)
    proj_weight_grad = widen(swapped(core, proj_part, after(proj_moved, up_weight_grad)))
    back = widen(after(back, up_weight_grad))
    doc_grad = jnp.stack([jnp.where(x == 0, stay, back), jnp.where(x == 0, back, stay)], axis=0)

    query_weight_grad, key_weight_grad, value_weight_grad, output_weight_grad = widened(
        four_index,
        (after(both_all, doc_grad),),
        tuple((((0, i * inner, (i + 1) * inner),), i == 3) for i in range(4)),
        "widen_heads",
    )

    return (
        loss_value,
        found_share,
        doc_grad,
        query_grad.reshape(query_local, query_len, width),
        gains[2],
        query_weight_grad,
        key_weight_grad,
        value_weight_grad,
        output_weight_grad,
        position_bias_grad,
        gains[1],
        gate_weight_grad,
        up_weight_grad,
        down_weight_grad,
        gains[0],
        proj_weight_grad,
    )


def solution(mesh):
    placed = (
        P("dp", "mp", None),
        P(("dp", "mp"), None, None),
        P("dp", None),
        P(),
        P(None, None, "dp"),
        P(),
        P(),
        P(None, "mp"),
        P(None, "mp"),
        P(None, "mp"),
        P("mp", None),
        P(None, "mp"),
        P(),
        P(None, "mp"),
        P(None, "mp"),
        P("mp", None),
        P(),
        P(),
    )
    return jax.shard_map(
        shards,
        mesh=mesh,
        in_specs=placed,
        out_specs=(
            P(),
            P(),
            P("dp", "mp", None),
            P(("dp", "mp"), None, None),
            P(),
            P(None, "mp"),
            P(None, "mp"),
            P(None, "mp"),
            P("mp", None),
            P(None, "mp"),
            P(),
            P(None, "mp"),
            P(None, "mp"),
            P("mp", None),
            P(),
            P(),
        ),
        check_vma=False,
    )
```

time: 518 us -> 391 us (0.75)
  waiting for transfers between devices: 187 us -> 120 us
  matrix products: 50.7 us -> 2.8 us
  other arithmetic: 53.1 us -> 11.6 us
  Pallas kernels: 100 us -> 123 us
  starting transfers between devices: 70.9 us -> 81.3 us
  local copies, waits for them, and re-layouts: 48.5 us -> 42.5 us
    ppermute x67 -> x34, waiting for transfers between devices: 187 us -> 78.3 us  [over(): return lambda values: lax.ppermute(values, axis, pairs)]
    ppermute x0 -> x48, starting transfers between devices: none -> 57.5 us  [exchange(): return lambda values: lax.ppermute(values, ('dp', 'mp'), pairs)]
    ppermute x67 -> x34, starting transfers between devices: 70.9 us -> 23.8 us  [over(): return lambda values: lax.ppermute(values, axis, pairs)]
    ppermute x0 -> x48, waiting for transfers between devices: none -> 42.1 us  [exchange(): return lambda values: lax.ppermute(values, ('dp', 'mp'), pairs)]
    dot_general x18 -> x0, matrix products: 36.1 us -> none  [the longest x9 20.3 us: dot_nt(): lax.dot_general(a, b, (((1,), (1,)), ((), ())), preferred_element_type=f32)]
    pallas_call x4 -> x22, Pallas kernels: 86.6 us -> 109 us  [the longest x2 30.1 us: attend_back(): pl.pallas_call(partial(attend_back_kernel, starts, heads, size, steps - 1...]
    reduce_sum x8 -> x2, other arithmetic: 18.9 us -> 0.18 us  [shards(): jnp.sum(g, axis=-1)]
    convert_element_type x45 -> x17, other arithmetic: 18.1 us -> 3.93 us  [the longest x12 2.38 us: narrow(): return values.astype(bf16)]
  transfers between devices with their start and end apart: 67 -> 82, of which waited for: 39 -> 32; matrix products, arithmetic and copies ran while one was open for 16% -> 5% of each run, Pallas kernels for 18% -> 25%
where the time goes in v2:
time: 391 us; the launch traced here: 384 us
  Pallas kernels  123 us (31%)
  waiting for transfers between devices  120 us (31%)
  starting transfers between devices  81.3 us (21%)
  local copies, waits for them, and re-layouts  42.5 us (11%)
  other arithmetic  11.6 us (3%)
    ppermute x34, waiting for transfers between devices, over(): return lambda values: lax.ppermute(values, axis, pairs)  78.3 us
    ppermute x48, starting transfers between devices, exchange(): return lambda values: lax.ppermute(values, ('dp', 'mp'), pairs)  57.5 us
    ppermute x48, waiting for transfers between devices, exchange(): return lambda values: lax.ppermute(values, ('dp', 'mp'), pairs)  42.1 us
    unnamed x177, local copies, waits for them, and re-layouts  33.3 us
    pallas_call x2, Pallas kernels, attend_back(): pl.pallas_call(partial(attend_back_kernel, starts, heads, size, steps - 1...  30.1 us
    ppermute x34, starting transfers between devices, over(): return lambda values: lax.ppermute(values, axis, pairs)  23.8 us
    pallas_call x2, Pallas kernels, ffn_back(): pl.pallas_call(partial(ffn_back_kernel, hidden, own), grid=(total // coun...  18.5 us
    pallas_call x2, Pallas kernels, attend(): pl.pallas_call(partial(attend_kernel, heads, size, steps - 1), grid_spec=...  18 us
  transfers between devices with their start and end apart: 82, of which 32 were waited for; matrix products, arithmetic and copies ran while one was open for 5% of the time, Pallas kernels for 25%

profile of v2, /device:TPU:0, one launch (start us, length us, event | category | flops | bytes accessed | tf_op | source)
XLA Modules:
  0.0 384.0 jit_solution(1709343101311169361)
XLA Ops:
  34.9 9.0 %attend.2 = (bf16[1152,192]{1,0:T(8,128)(2,1)S(1)}, f32[8,1152]{1,0:T(8,128)S(1)}) custom-call(s32[5]{0:T(128)S(1)} %get-tuple-element.459.lo_ref, s32[5]{0:T(128)S(1)} %get-tuple-element.460.cnt_ref, bf16[1152,576]{1,0:T(8,128)(2,1)S(1)} %get-tuple-element.177.qkv_ref, s32[1152,1]{1,0:T(8,128)S(1)} %copy-done.47, s32[1,1152]{1,0:T(1,128)S(1)} %broadcast_in_dim.28.segk_ref, ...), custom_call_target="tpu_custom_call" | custom-call | flops 27000000512 | bytes 1024 | tf_op jit(solution)/shard_map/attend/pallas_call | solution.py:170
  50.4 9.0 %attend.3 = (bf16[1152,192]{1,0:T(8,128)(2,1)S(1)}, f32[8,1152]{1,0:T(8,128)S(1)}) custom-call(s32[5]{0:T(128)S(1)} %get-tuple-element.459.lo_ref, s32[5]{0:T(128)S(1)} %get-tuple-element.460.cnt_ref, bf16[1152,576]{1,0:T(8,128)(2,1)S(1)} %convolution_convert_fusion.qkv_ref, s32[1152,1]{1,0:T(8,128)S(1)} %copy-done.47, ...), custom_call_target="tpu_custom_call" | custom-call | flops 27000000512 | bytes 1024 | tf_op jit(solution)/shard_map/attend/pallas_call | solution.py:170
  65.1 17.9 %collective-permute-done.8 = bf16[384,1024]{1,0:T(8,128)(2,1)} collective-permute-done((bf16[384,1024]{1,0:T(8,128)(2,1)}, bf16[384,1024]{1,0:T(8,128)(2,1)}, u32[]{:S(2)}, u32[]{:S(2)}) %collective-permute-start.8) | collective-permute-done | bytes 786464 | tf_op jit(solution)/shard_map/ppermute | solution.py:1190
  91.2 5.7 %ffn_own.1 = (f32[1152,768]{1,0:T(8,128)S(1)}, bf16[1152,768]{1,0:T(8,128)(2,1)S(1)}, bf16[1152,1024]{1,0:T(8,128)(2,1)S(1)}, f32[1152,768]{1,0:T(8,128)S(1)}) custom-call(bf16[1152,768]{1,0:T(8,128)(2,1)S(1)} %copy-done.41, bf16[1152,768]{1,0:T(8,128)(2,1)S(1)} %fusion.near_ref, bf16[1152,768]{1,0:T(8,128)(2,1)} %collective-permute-done.7.moved_ref, ...), custom_call_target="tpu_custom_call" | custom-call | flops 15000000512 | bytes 1024 | tf_op jit(solution)/shard_map/ffn_own/pallas_call | solution.py:682
  100.8 7.2 %collective-permute-done.12 = bf16[256,768]{1,0:T(8,128)(2,1)S(1)} collective-permute-done((bf16[256,768]{1,0:T(8,128)(2,1)S(1)}, bf16[256,768]{1,0:T(8,128)(2,1)S(1)}, u32[]{:S(2)}, u32[]{:S(2)}) %collective-permute-start.12) | collective-permute-done | bytes 393248 | tf_op jit(solution)/shard_map/ppermute | solution.py:1190
  108.2 4.5 %ffn_far.1 = (bf16[1152,1024]{1,0:T(8,128)(2,1)S(1)}, bf16[1152,768]{1,0:T(8,128)(2,1)}) custom-call(bf16[1152,768]{1,0:T(8,128)(2,1)S(1)} %get-tuple-element.191.norm_ref.refs_1_.refs_2_, bf16[768,512]{1,0:T(8,128)(2,1)S(1)} %pad_maximum_fusion.2.g_ref.refs_4_, bf16[768,512]{1,0:T(8,128)(2,1)S(1)} %pad_maximum_fusion.3.u_ref.refs_5_, ...), custom_call_target="tpu_custom_call" | custom-call | flops 15000000512 | bytes 1024 | tf_op jit(solution)/shard_map/ffn_far/pallas_call | solution.py:719
  114.2 4.0 %collective-permute-done.13.moved_ref = bf16[1152,768]{1,0:T(8,128)(2,1)} collective-permute-done((bf16[1152,768]{1,0:T(8,128)(2,1)}, bf16[1152,768]{1,0:T(8,128)(2,1)}, u32[]{:S(2)}, u32[]{:S(2)}) %collective-permute-start.13) | collective-permute-done | bytes 1769504 | tf_op jit(solution)/shard_map/ppermute | solution.py:1190
  120.2 3.8 leave.1
  138.1 4.9 %score.1 = (f32[8,1024]{1,0:T(8,128)S(1)}, f32[8,128]{1,0:T(8,128)S(1)}, f32[8,128]{1,0:T(8,128)S(1)}) custom-call(s32[2]{0:T(128)S(1)} %pad_add_fusion.2.first_ref, bf16[1024,128]{1,0:T(8,128)(2,1)S(1)} %slice.145.emb_ref, bf16[1024,128]{1,0:T(8,128)(2,1)S(1)} %constant_dynamic-update-slice_fusion.qe_ref, s32[1152,1]{1,0:T(8,128)S(1)} %copy-done.48, ...), custom_call_target="tpu_custom_call" | custom-call | flops 15000000512 | bytes 1024 | tf_op jit(solution)/shard_map/score/pallas_call | solution.py:417
  155.9 5.0 %score_back.1 = (f32[1024,128]{1,0:T(8,128)S(1)}, bf16[1024,128]{1,0:T(8,128)(2,1)S(1)}) custom-call(s32[2]{0:T(128)S(1)} %pad_add_fusion.2.first_ref, bf16[1024,128]{1,0:T(8,128)(2,1)S(1)} %slice.145.emb_ref, bf16[1024,128]{1,0:T(8,128)(2,1)S(1)} %constant_dynamic-update-slice_fusion.qe_ref, s32[1152,1]{1,0:T(8,128)S(1)} %copy-done.48, ...), custom_call_target="tpu_custom_call" | custom-call | flops 15000000512 | bytes 1024 | tf_op jit(solution)/shard_map/score_back/pallas_call | solution.py:484
  180.3 4.8 %leave_back.1 = (f32[1152,768]{1,0:T(8,128)S(1)}, f32[768,128]{1,0:T(8,128)S(1)}, f32[8,768]{1,0:T(8,128)S(1)}) custom-call(s32[1]{0:T(128)} %bitcast.8.core_ref, f32[1152,768]{1,0:T(8,128)S(1)} %copy-done.55, f32[1152,128]{1,0:T(8,128)S(1)} %copy-done.71, f32[1024,128]{1,0:T(8,128)S(1)} %get-tuple-element.207.near_ref, ...), custom_call_target="tpu_custom_call" | custom-call | flops 15000000512 | bytes 1024 | tf_op jit(solution)/shard_map/leave_back/pallas_call | solution.py:810
  186.3 9.2 %ffn_back.2 = (f32[1152,768]{1,0:T(8,128)S(1)}, bf16[768,256]{1,0:T(8,128)(2,1)S(1)}, bf16[768,768]{1,0:T(8,128)(2,1)S(1)}, bf16[768,512]{1,0:T(8,128)(2,1)S(1)}) custom-call(f32[1152,768]{1,0:T(8,128)S(1)} %get-tuple-element.215.refs_0_.refs_1_.grad_ref, bf16[1152,768]{1,0:T(8,128)(2,1)S(1)} %copy-done.69, bf16[1152,1024]{1,0:T(8,128)(2,1)S(1)} %copy-done.67, ...), custom_call_target="tpu_custom_call" | custom-call | flops 30000001024 | bytes 1024 | tf_op jit(solution)/shard_map/ffn_back/pallas_call | solution.py:888
  200.2 9.3 %ffn_back.3 = (bf16[1152,768]{1,0:T(8,128)(2,1)S(1)}, bf16[768,256]{1,0:T(8,128)(2,1)S(1)}, bf16[768,768]{1,0:T(8,128)(2,1)S(1)}, bf16[192,1024]{1,0:T(8,128)(2,...) custom-call(s32[1]{0:T(128)} %bitcast.18.refs_0_.index_ref, ...), custom_call_target="tpu_custom_call" | custom-call | flops 30000001024 | bytes 1024 | tf_op jit(solution)/shard_map/ffn_back/pallas_call | solution.py:888
  214.9 4.8 %mid_back.1 = (f32[1152,768]{1,0:T(8,128)S(1)}, bf16[1152,192]{1,0:T(8,128)(2,1)S(1)}, bf16[1152,192]{1,0:T(8,128)(2,1)S(1)}, bf16[768,192]{1,0:T(8,128)(2,1)S(1...) custom-call(bf16[1152,768]{1,0:T(8,128)(2,1)S(1)} %get-tuple-element.230.near_ref, ...), custom_call_target="tpu_custom_call" | custom-call | flops 17999998976 | bytes 1024 | tf_op jit(solution)/shard_map/mid_back/pallas_call | solution.py:939
  219.8 15.0 %attend_back.2 = (bf16[1152,576]{1,0:T(8,128)(2,1)S(1)}, f32[3,32,128]{2,1,0:T(8,128)S(1)}) custom-call(s32[5]{0:T(128)S(1)} %copy-done.15, s32[5]{0:T(128)S(1)} %copy-done.17, bf16[1152,576]{1,0:T(8,128)(2,1)S(1)} %copy-done.34, bf16[1152,192]{1,0:T(8,128)(2,1)S(1)} %get-tuple-element.236.do_ref, bf16[1152,192]{1,0:T(8,128)(2,1)S(1)} %copy-done.7, ...), custom_call_target="tpu_custom_call" | custom-call | flops 44999999488 | bytes 1024 | tf_op jit(solution)/shard_map/attend_back/pallas_call | solution.py:331
  250.6 15.1 %attend_back.3 = (bf16[1152,576]{1,0:T(8,128)(2,1)S(1)}, f32[3,32,128]{2,1,0:T(8,128)S(1)}) custom-call(s32[5]{0:T(128)S(1)} %copy-done.15, s32[5]{0:T(128)S(1)} %copy-done.17, bf16[1152,576]{1,0:T(8,128)(2,1)S(1)} %copy-done.63, bf16[1152,192]{1,0:T(8,128)(2,1)S(1)} %get-tuple-element.260.do_ref, bf16[1152,192]{1,0:T(8,128)(2,1)S(1)} %copy-done.5, ...), custom_call_target="tpu_custom_call" | custom-call | flops 44999999488 | bytes 1024 | tf_op jit(solution)/shard_map/attend_back/pallas_call | solution.py:331
  267.4 3.5 enter_back.1
  270.9 19.4 %collective-permute-done.54.moved_ref = bf16[768,768]{1,0:T(8,128)(2,1)S(1)} collective-permute-done((bf16[768,768]{1,0:T(8,128)(2,1)S(1)}, bf16[768,768]{1,0:T(8,128)(2,1)S(1)}, u32[]{:S(2)}, u32[]{:S(2)}) %collective-permute-start.54) | collective-permute-done | bytes 1179680 | tf_op jit(solution)/shard_map/ppermute | solution.py:1190
  305.7 6.5 %collective-permute-done.64 = bf16[192,512]{1,0:T(8,128)(2,1)S(1)} collective-permute-done((bf16[192,512]{1,0:T(8,128)(2,1)S(1)}, bf16[192,512]{1,0:T(8,128)(2,1)S(1)}, u32[]{:S(2)}, u32[]{:S(2)}) %collective-permute-start.64) | collective-permute-done | bytes 196640 | tf_op jit(solution)/shard_map/ppermute | solution.py:1190
  312.3 6.3 %collective-permute-done.60 = bf16[192,768]{1,0:T(8,128)(2,1)S(1)} collective-permute-done((bf16[192,768]{1,0:T(8,128)(2,1)}, bf16[192,768]{1,0:T(8,128)(2,1)S(1)}, u32[]{:S(2)}, u32[]{:S(2)}) %collective-permute-start.60) | collective-permute-done | bytes 294944 | tf_op jit(solution)/shard_map/ppermute | solution.py:1190
  322.2 4.0 %collective-permute-done.70 = bf16[192,768]{1,0:T(8,128)(2,1)S(1)} collective-permute-done((bf16[192,768]{1,0:T(8,128)(2,1)S(1)}, bf16[192,768]{1,0:T(8,128)(2,1)S(1)}, u32[]{:S(2)}, u32[]{:S(2)}) %collective-permute-start.70) | collective-permute-done | bytes 294944 | tf_op jit(solution)/shard_map/ppermute | solution.py:1204
  337.7 3.4 collective-permute-start.63
  348.0 13.5 %collective-permute-done.66.refs_10_ = bf16[192,512]{1,0:T(8,128)(2,1)S(1)} collective-permute-done((bf16[192,512]{1,0:T(8,128)(2,1)S(1)}, bf16[192,512]{1,0:T(8,128)(2,1)S(1)}, u32[]{:S(2)}, u32[]{:S(2)}) %collective-permute-start.66) | collective-permute-done | bytes 196640 | tf_op jit(solution)/shard_map/ppermute | solution.py:1204
  370.0 6.0 %collective-permute-done.76 = f32[21,128]{1,0:T(8,128)S(1)} collective-permute-done((f32[21,128]{1,0:T(8,128)S(1)}, f32[21,128]{1,0:T(8,128)S(1)}, u32[]{:S(2)}, u32[]{:S(2)}) %collective-permute-start.76) | collective-permute-done | bytes 10784 | tf_op jit(solution)/shard_map/ppermute | solution.py:1190
  (432 shorter events, 189.7 us)
Async XLA Ops:
  2.7 23.3 %collective-permute-start.1 = (bf16[256,768]{1,0:T(8,128)(2,1)}, bf16[256,768]{1,0:T(8,128)(2,1)}, u32[]{:S(2)}, u32[]{:S(2)}) collective-permute-start(bf16[256,768]{1,0:T(8,128)(2,1)} %get-tuple-element.438), channel_id=1, source_target_pairs={{0,2},{1,3},{2,0},{3,1},{4,6},{5,7},{6,4},{7,5},{8,10},{9,11},{10,... | collective-permute-start | bytes 1179656 | tf_op jit(solution)/shard_map/ppermute | solution.py:1190
  6.5 22.5 %collective-permute-start = (bf16[320,768]{1,0:T(8,128)(2,1)S(1)}, bf16[320,768]{1,0:T(8,128)(2,1)S(1)}, u32[]{:S(2)}, u32[]{:S(2)}) collective-permute-start(bf16[320,768]{1,0:T(8,128)(2,1)S(1)} %pad_maximum_fusion.5.kept_ref), channel_id=1, source_target_pairs={{0,1},{1,0},{2,3},{3,2},{4,5},{5,4},{6,7},{7,6},{8,9},{9,8},{10,11... | collective-permute-start | bytes 1474568 | tf_op jit(solution)/shard_map/ppermute | solution.py:1190
  14.3 19.1 %collective-permute-start.3 = (bf16[384,576]{1,0:T(8,128)(2,1)}, bf16[384,576]{1,0:T(8,128)(2,1)S(1)}, u32[]{:S(2)}, u32[]{:S(2)}) collective-permute-start(bf16[384,576]{1,0:T(8,128)(2,1)} %get-tuple-element.182), channel_id=1, source_target_pairs={{0,2},{1,3},{2,0},{3,1},{4,6},{5,7},{6,4},{7,5},{8,10},{9,11},{10,... | collective-permute-start | bytes 1327112 | tf_op jit(solution)/shard_map/ppermute | solution.py:1190
  62.2 24.1 %collective-permute-start.7 = (bf16[1152,768]{1,0:T(8,128)(2,1)S(1)}, bf16[1152,768]{1,0:T(8,128)(2,1)}, u32[]{:S(2)}, u32[]{:S(2)}) collective-permute-start(bf16[1152,768]{1,0:T(8,128)(2,1)S(1)} %fusion.near_ref), channel_id=1, source_target_pairs={{0,1},{1,0},{2,3},{3,2},{4,5},{5,4},{6,7},{7,6},{8,9},{9,8},{10,11... | collective-permute-start | bytes 5308424 | tf_op jit(solution)/shard_map/ppermute | solution.py:1190
  62.3 20.7 %collective-permute-start.8 = (bf16[384,1024]{1,0:T(8,128)(2,1)}, bf16[384,1024]{1,0:T(8,128)(2,1)}, u32[]{:S(2)}, u32[]{:S(2)}) collective-permute-start(bf16[384,1024]{1,0:T(8,128)(2,1)} %get-tuple-element.192), channel_id=1, source_target_pairs={{0,2},{1,3},{2,0},{3,1},{4,6},{5,7},{6,4},{7,5},{8,10},{9,11},{10,... | collective-permute-start | bytes 2359304 | tf_op jit(solution)/shard_map/ppermute | solution.py:1190
  62.6 35.8 %collective-permute-start.11 = (bf16[256,768]{1,0:T(8,128)(2,1)S(1)}, bf16[256,768]{1,0:T(8,128)(2,1)S(1)}, u32[]{:S(2)}, u32[]{:S(2)}) collective-permute-start(bf16[256,768]{1,0:T(8,128)(2,1)S(1)} %copy-done.28), channel_id=1, source_target_pairs={{0,2},{1,3},{2,0},{3,1},{4,6},{5,7},{6,4},{7,5},{8,10},{9,11},{10,... | collective-permute-start | bytes 1179656 | tf_op jit(solution)/shard_map/ppermute | solution.py:1190
  209.8 25.0 %collective-permute-start.45 = (bf16[192,1024]{1,0:T(8,128)(2,1)S(1)}, bf16[192,1024]{1,0:T(8,128)(2,1)S(1)}, u32[]{:S(2)}, u32[]{:S(2)}) collective-permute-start(bf16[192,1024]{1,0:T(8,128)(2,1)S(1)} %get-tuple-element.252), channel_id=1, source_target_pairs={{0,4},{1,5},{2,6},{3,7},{4,0},{5,1},{6,2},{7,3},{8,12},{9,13},{10,... | collective-permute-start | bytes 1179656 | tf_op jit(solution)/shard_map/ppermute | solution.py:1204
  211.5 24.7 %collective-permute-start.46 = (bf16[192,1024]{1,0:T(8,128)(2,1)S(1)}, bf16[192,1024]{1,0:T(8,128)(2,1)S(1)}, u32[]{:S(2)}, u32[]{:S(2)}) collective-permute-start(bf16[192,1024]{1,0:T(8,128)(2,1)S(1)} %get-tuple-element.253), channel_id=1, source_target_pairs={{0,8},{1,9},{2,10},{3,11},{4,12},{5,13},{6,14},{7,15},{8,0},{9,1},... | collective-permute-start | bytes 1179656 | tf_op jit(solution)/shard_map/ppermute | solution.py:1204
  211.6 28.5 %collective-permute-start.47 = (bf16[192,1024]{1,0:T(8,128)(2,1)S(1)}, bf16[192,1024]{1,0:T(8,128)(2,1)S(1)}, u32[]{:S(2)}, u32[]{:S(2)}) collective-permute-start(bf16[192,1024]{1,0:T(8,128)(2,1)S(1)} %get-tuple-element.254), channel_id=1, source_target_pairs={{0,12},{1,13},{2,14},{3,15},{4,8},{5,9},{6,10},{7,11},{8,4},{9,5},... | collective-permute-start | bytes 1179656 | tf_op jit(solution)/shard_map/ppermute | solution.py:1204
  213.4 24.8 %collective-permute-start.48 = (bf16[384,128]{1,0:T(8,128)(2,1)S(1)}, bf16[384,128]{1,0:T(8,128)(2,1)S(1)}, u32[]{:S(2)}, u32[]{:S(2)}) collective-permute-start(bf16[384,128]{1,0:T(8,128)(2,1)S(1)} %add_convert_fusion.10), channel_id=1, source_target_pairs={{0,16},{4,20},{8,24},{12,28},{16,0},{20,4},{24,8},{28,12},{1,17},{... | collective-permute-start | bytes 294920 | tf_op jit(solution)/shard_map/ppermute | solution.py:1190
  213.9 30.5 %collective-permute-start.41 = (bf16[768,768]{1,0:T(8,128)(2,1)S(1)}, bf16[768,768]{1,0:T(8,128)(2,1)S(1)}, u32[]{:S(2)}, u32[]{:S(2)}) collective-permute-start(bf16[768,768]{1,0:T(8,128)(2,1)S(1)} %get-tuple-element.235), channel_id=1, source_target_pairs={{0,2},{1,3},{2,0},{3,1},{4,6},{5,7},{6,4},{7,5},{8,10},{9,11},{10,... | collective-permute-start | bytes 3538952 | tf_op jit(solution)/shard_map/ppermute | solution.py:1190
  244.5 21.3 %collective-permute-start.53 = (bf16[192,256]{1,0:T(8,128)(2,1)S(1)}, bf16[192,256]{1,0:T(8,128)(2,1)S(1)}, u32[]{:S(2)}, u32[]{:S(2)}) collective-permute-start(bf16[192,256]{1,0:T(8,128)(2,1)S(1)} %add_convert_fusion.9), channel_id=1, source_target_pairs={{0,16},{4,20},{8,24},{12,28},{16,0},{20,4},{24,8},{28,12},{1,17},{... | collective-permute-start | bytes 294920 | tf_op jit(solution)/shard_map/ppermute | solution.py:1190
  245.9 20.1 %collective-permute-start.49 = (bf16[192,768]{1,0:T(8,128)(2,1)S(1)}, bf16[192,768]{1,0:T(8,128)(2,1)S(1)}, u32[]{:S(2)}, u32[]{:S(2)}) collective-permute-start(bf16[192,768]{1,0:T(8,128)(2,1)S(1)} %get-tuple-element.244), channel_id=1, source_target_pairs={{0,4},{1,5},{2,6},{3,7},{4,0},{5,1},{6,2},{7,3},{8,12},{9,13},{10,... | collective-permute-start | bytes 884744 | tf_op jit(solution)/shard_map/ppermute | solution.py:1204
  246.0 20.0 %collective-permute-start.50 = (bf16[192,768]{1,0:T(8,128)(2,1)S(1)}, bf16[192,768]{1,0:T(8,128)(2,1)S(1)}, u32[]{:S(2)}, u32[]{:S(2)}) collective-permute-start(bf16[192,768]{1,0:T(8,128)(2,1)S(1)} %get-tuple-element.245), channel_id=1, source_target_pairs={{0,8},{1,9},{2,10},{3,11},{4,12},{5,13},{6,14},{7,15},{8,0},{9,1},... | collective-permute-start | bytes 884744 | tf_op jit(solution)/shard_map/ppermute | solution.py:1204
  247.6 18.4 %collective-permute-start.51 = (bf16[192,768]{1,0:T(8,128)(2,1)S(1)}, bf16[192,768]{1,0:T(8,128)(2,1)S(1)}, u32[]{:S(2)}, u32[]{:S(2)}) collective-permute-start(bf16[192,768]{1,0:T(8,128)(2,1)S(1)} %get-tuple-element.246), channel_id=1, source_target_pairs={{0,12},{1,13},{2,14},{3,15},{4,8},{5,9},{6,10},{7,11},{8,4},{9,5},... | collective-permute-start | bytes 884744 | tf_op jit(solution)/shard_map/ppermute | solution.py:1204
  265.8 24.5 %collective-permute-start.54 = (bf16[768,768]{1,0:T(8,128)(2,1)S(1)}, bf16[768,768]{1,0:T(8,128)(2,1)S(1)}, u32[]{:S(2)}, u32[]{:S(2)}) collective-permute-start(bf16[768,768]{1,0:T(8,128)(2,1)S(1)} %heads_far.1), channel_id=1, source_target_pairs={{0,2},{1,3},{2,0},{3,1},{4,6},{5,7},{6,4},{7,5},{8,10},{9,11},{10,... | collective-permute-start | bytes 3538952 | tf_op jit(solution)/shard_map/ppermute | solution.py:1190
  293.6 36.3 %collective-permute-start.26 = (f32[2,128]{1,0:T(2,128)S(1)}, f32[2,128]{1,0:T(2,128)S(1)}, u32[]{:S(2)}, u32[]{:S(2)}) collective-permute-start(f32[2,128]{1,0:T(2,128)S(1)} %broadcast_in_dim.31), channel_id=1, source_target_pairs={{0,1},{1,0},{2,3},{3,2},{4,5},{5,4},{6,7},{7,6},{8,9},{9,8},{10,11... | collective-permute-start | bytes 3080 | tf_op jit(solution)/shard_map/ppermute | solution.py:1190
  294.4 17.9 %collective-permute-start.64 = (bf16[192,512]{1,0:T(8,128)(2,1)S(1)}, bf16[192,512]{1,0:T(8,128)(2,1)S(1)}, u32[]{:S(2)}, u32[]{:S(2)}) collective-permute-start(bf16[192,512]{1,0:T(8,128)(2,1)S(1)} %add_convert_fusion.6), channel_id=1, source_target_pairs={{0,16},{4,20},{8,24},{12,28},{16,0},{20,4},{24,8},{28,12},{1,17},{... | collective-permute-start | bytes 589832 | tf_op jit(solution)/shard_map/ppermute | solution.py:1190
  294.4 24.1 %collective-permute-start.60 = (bf16[192,768]{1,0:T(8,128)(2,1)}, bf16[192,768]{1,0:T(8,128)(2,1)S(1)}, u32[]{:S(2)}, u32[]{:S(2)}) collective-permute-start(bf16[192,768]{1,0:T(8,128)(2,1)} %add_convert_fusion.4), channel_id=1, source_target_pairs={{0,16},{4,20},{8,24},{12,28},{16,0},{20,4},{24,8},{28,12},{1,17},{... | collective-permute-start | bytes 884744 | tf_op jit(solution)/shard_map/ppermute | solution.py:1190
  297.4 21.3 %collective-permute-start.68 = (bf16[192,768]{1,0:T(8,128)(2,1)S(1)}, bf16[192,768]{1,0:T(8,128)(2,1)S(1)}, u32[]{:S(2)}, u32[]{:S(2)}) collective-permute-start(bf16[192,768]{1,0:T(8,128)(2,1)S(1)} %get-tuple-element.277), channel_id=1, source_target_pairs={{0,4},{1,5},{2,6},{3,7},{4,0},{5,1},{6,2},{7,3},{8,12},{9,13},{10,... | collective-permute-start | bytes 884744 | tf_op jit(solution)/shard_map/ppermute | solution.py:1204
  298.7 23.3 %collective-permute-start.69 = (bf16[192,768]{1,0:T(8,128)(2,1)S(1)}, bf16[192,768]{1,0:T(8,128)(2,1)S(1)}, u32[]{:S(2)}, u32[]{:S(2)}) collective-permute-start(bf16[192,768]{1,0:T(8,128)(2,1)S(1)} %get-tuple-element.278), channel_id=1, source_target_pairs={{0,8},{1,9},{2,10},{3,11},{4,12},{5,13},{6,14},{7,15},{8,0},{9,1},... | collective-permute-start | bytes 884744 | tf_op jit(solution)/shard_map/ppermute | solution.py:1204
  337.7 24.5 %collective-permute-start.63 = (bf16[192,768]{1,0:T(8,128)(2,1)S(1)}, bf16[192,768]{1,0:T(8,128)(2,1)S(1)}, u32[]{:S(2)}, u32[]{:S(2)}) collective-permute-start(bf16[192,768]{1,0:T(8,128)(2,1)S(1)} %add_convert_fusion.3.refs_4_), channel_id=1, source_target_pairs={{0,12},{1,13},{2,14},{3,15},{4,8},{5,9},{6,10},{7,11},{8,4},{9,5},... | collective-permute-start | bytes 884744 | tf_op jit(solution)/shard_map/ppermute | solution.py:1204
  341.1 21.2 %collective-permute-start.62 = (bf16[192,768]{1,0:T(8,128)(2,1)S(1)}, bf16[192,768]{1,0:T(8,128)(2,1)S(1)}, u32[]{:S(2)}, u32[]{:S(2)}) collective-permute-start(bf16[192,768]{1,0:T(8,128)(2,1)S(1)} %add_convert_fusion.3.refs_4_), channel_id=1, source_target_pairs={{0,8},{1,9},{2,10},{3,11},{4,12},{5,13},{6,14},{7,15},{8,0},{9,1},... | collective-permute-start | bytes 884744 | tf_op jit(solution)/shard_map/ppermute | solution.py:1204
  343.9 20.5 %collective-permute-start.61 = (bf16[192,768]{1,0:T(8,128)(2,1)S(1)}, bf16[192,768]{1,0:T(8,128)(2,1)S(1)}, u32[]{:S(2)}, u32[]{:S(2)}) collective-permute-start(bf16[192,768]{1,0:T(8,128)(2,1)S(1)} %add_convert_fusion.3.refs_4_), channel_id=1, source_target_pairs={{0,4},{1,5},{2,6},{3,7},{4,0},{5,1},{6,2},{7,3},{8,12},{9,13},{10,... | collective-permute-start | bytes 884744 | tf_op jit(solution)/shard_map/ppermute | solution.py:1204
  (140 other events, 1098.1 us)

commit v3 on v2

--- a/solution.py
+++ b/solution.py
@@ -104,6 +104,10 @@
     return jnp.minimum(jnp.maximum(d, -2), 2) + 2
 
 
+def column(row):
+    return jnp.transpose(jnp.broadcast_to(row, (8, row.shape[1])))[:, 0:1]
+
+
 def attend_kernel(heads, size, most, lo_ref, cnt_ref, qkv_ref, segq_ref, segk_ref, t_ref, ctx_ref, lse_ref, k_s, v_s):
     b = pl.program_id(0)
     inner = heads * size
@@ -118,7 +122,7 @@
     def window(first, count, lo, pairs):
         rows = pl.ds(pl.multiple_of(first * BLOCK, BLOCK), count * BLOCK)
         block = qkv_ref[rows, :inner]
-        seg_col = segq_ref[rows, :]
+        seg_col = column(segq_ref[:, rows])
         spans = [pl.ds(pl.multiple_of((lo + 2 * i) * BLOCK, BLOCK), PAIR) for i in range(pairs)]
         allowed = [seg_col == segk_ref[:, span] for span in spans]
         outs, logs = [], []
@@ -160,7 +164,7 @@
 
 def attend(qkv, ranges, segs, tiles):
     lo, cnt = ranges
-    segq_col, segq_row, segk_col, segk_row = segs
+    seg_q, seg_k = segs
     total, wide = qkv.shape
     heads = tiles.shape[0]
     inner = wide // 3
@@ -174,7 +178,7 @@
             grid=(steps,),
             in_specs=[
                 pl.BlockSpec((total, wide), whole, pipeline_mode=pl.Buffered(1)),
-                pl.BlockSpec((total, 1), whole, pipeline_mode=pl.Buffered(1)),
+                pl.BlockSpec((1, total), whole, pipeline_mode=pl.Buffered(1)),
                 pl.BlockSpec((1, total), whole, pipeline_mode=pl.Buffered(1)),
                 pl.BlockSpec((heads, 5, BLOCK, BLOCK), lambda b, *_: (0, 0, 0, 0), pipeline_mode=pl.Buffered(1)),
             ],
@@ -194,7 +198,7 @@
         compiler_params=params(12),
         cost_estimate=cost(9),
         name="attend",
-    )(lo, cnt, qkv, segq_col, segk_row, tiles)
+    )(lo, cnt, qkv, seg_q, seg_k, tiles)
 
 
 def attend_back_kernel(
@@ -242,7 +246,7 @@
     def window(first, count, lo, pairs):
         rows = pl.ds(pl.multiple_of(first * BLOCK, BLOCK), count * BLOCK)
         block = qkv_ref[rows, inner:]
-        seg_col = segk_ref[rows, :]
+        seg_col = column(segk_ref[:, rows])
         spans = [pl.ds(pl.multiple_of((lo + 2 * i) * BLOCK, BLOCK), PAIR) for i in range(pairs)]
         allowed = [seg_col == segq_ref[:, span] for span in spans]
         dks, dvs = [], []
@@ -320,7 +324,7 @@
 
 def attend_back(qkv, context_grad, context, lse, ranges, segs, tiles, buckets):
     lo, cnt = ranges
-    segq_col, segq_row, segk_col, segk_row = segs
+    seg_q, seg_k = segs
     total, wide = qkv.shape
     heads = tiles.shape[0]
     inner = wide // 3
@@ -338,7 +342,7 @@
                 pl.BlockSpec((total, inner), whole, pipeline_mode=pl.Buffered(1)),
                 pl.BlockSpec((total, inner), whole, pipeline_mode=pl.Buffered(1)),
                 pl.BlockSpec((8, total), whole, pipeline_mode=pl.Buffered(1)),
-                pl.BlockSpec((total, 1), whole, pipeline_mode=pl.Buffered(1)),
+                pl.BlockSpec((1, total), whole, pipeline_mode=pl.Buffered(1)),
                 pl.BlockSpec((1, total), whole, pipeline_mode=pl.Buffered(1)),
                 pl.BlockSpec((heads, 5, BLOCK, BLOCK), lambda b, *_: (0, 0, 0, 0), pipeline_mode=pl.Buffered(1)),
             ],
@@ -361,7 +365,7 @@
         compiler_params=params(16),
         cost_estimate=cost(15),
         name="attend_back",
-    )(lo, cnt, qkv, context_grad, context, lse, segk_col, segq_row, tiles)
+    )(lo, cnt, qkv, context_grad, context, lse, seg_k, seg_q, tiles)
 
 
 def pool_matrix(shape, axis, me, query_len, query_local):
@@ -381,7 +385,7 @@
         acc_s[...] = jnp.zeros(acc_s.shape, f32)
 
     near = jnp.exp(sharpness * (dot_nt(emb_ref[...], qe_ref[...]) - 1.0))
-    seg = seg_ref[...]
+    seg = column(seg_ref[...])
     for d in range(docs):
         acc_s[d : d + 1, :] += jnp.sum(jnp.where(seg == d, near, 0.0), axis=0, keepdims=True)
 
@@ -422,7 +426,7 @@
             in_specs=[
                 pl.BlockSpec((BLOCK, width), lambda b, *_: (b, 0)),
                 pl.BlockSpec((count, width), whole, pipeline_mode=pl.Buffered(1)),
-                pl.BlockSpec((BLOCK, 1), lambda b, *_: (b, 0)),
+                pl.BlockSpec((1, BLOCK), lambda b, *_: (0, b)),
                 pl.BlockSpec((8, count), whole, pipeline_mode=pl.Buffered(1)),
                 pl.BlockSpec((8, lanes), whole, pipeline_mode=pl.Buffered(1)),
             ],
@@ -462,7 +466,7 @@
 
     emb = emb_ref[...]
     near = jnp.exp(sharpness * (dot_nt(emb, qe_ref[...]) - 1.0))
-    seg = seg_ref[...]
+    seg = column(seg_ref[...])
     weight = jnp.broadcast_to(grad_s[0:1, :], near.shape)
     for d in range(1, docs):
         weight = jnp.where(seg == d, grad_s[d : d + 1, :], weight)
@@ -489,7 +493,7 @@
             in_specs=[
                 pl.BlockSpec((BLOCK, width), lambda b, *_: (b, 0)),
                 pl.BlockSpec((count, width), whole, pipeline_mode=pl.Buffered(1)),
-                pl.BlockSpec((BLOCK, 1), lambda b, *_: (b, 0)),
+                pl.BlockSpec((1, BLOCK), lambda b, *_: (0, b)),
                 pl.BlockSpec((8, count), whole, pipeline_mode=pl.Buffered(1)),
                 pl.BlockSpec((8, lanes), whole, pipeline_mode=pl.Buffered(1)),
                 pl.BlockSpec((8, count), whole, pipeline_mode=pl.Buffered(1)),
@@ -535,7 +539,7 @@
     return lax.rsqrt(jnp.mean(values * values, axis=-1, keepdims=True) + epsilon)
 
 
-def choose_kernel(query_local, query_len, steps, place_ref, pos_ref, ret_ref, segq_ref, segk_ref, chosen_ref, rows_ref, colq_ref, colk_ref, ret_s):
+def choose_kernel(query_local, query_len, steps, place_ref, pos_ref, ret_ref, chosen_ref, rows_ref, ret_s):
     core, me = place_ref[0], place_ref[1]
     span = query_local * query_len
     blocks = ret_s.shape[0] // span
@@ -561,53 +565,45 @@
             query = (holder(p) * 2 + core) * query_local + i
             rows = jnp.where(lane == p * query_local + i, pos_ref[query], rows)
     rows_ref[...] = rows
-    for row_ref, col_ref in ((segq_ref, colq_ref), (segk_ref, colk_ref)):
-        whole = jnp.broadcast_to(row_ref[...], (8, row_ref.shape[1]))
-        col_ref[...] = jnp.transpose(whole)[:, 0:1]
-
-
-def choose(place, positives, retrieved, seg_q, seg_k, query_local, query_len, steps):
+
+
+def choose(place, positives, retrieved, query_local, query_len, steps):
     total, docs = retrieved.shape
     lanes = -(-(total // 2 // query_len) // BLOCK) * BLOCK
-    tokens = seg_q.shape[1]
     return pl.pallas_call(
         partial(choose_kernel, query_local, query_len, steps),
-        in_specs=[SCALARS, SCALARS] + [pl.BlockSpec(memory_space=pltpu.VMEM)] * 3,
-        out_shape=(
-            like((8, total // 2), f32),
-            like((8, lanes), jnp.int32),
-            like((tokens, 1), jnp.int32),
-            like((tokens, 1), jnp.int32),
-        ),
+        in_specs=[SCALARS, SCALARS, pl.BlockSpec(memory_space=pltpu.VMEM)],
+        out_shape=(like((8, total // 2), f32), like((8, lanes), jnp.int32)),
         scratch_shapes=[pltpu.VMEM((total // 2, docs), f32)],
-        compiler_params=params(10),
+        compiler_params=params(20),
         cost_estimate=cost(1),
         name="choose",
-    )(place, positives, retrieved, seg_q, seg_k)
-
-
-def pack_kernel(bit_ref, q_ref, k_ref, v_ref, o_ref, g_ref, u_ref, d_ref, b_ref, qkv_ref, half_qkv, half_o, half_gu, half_d):
-    inner = q_ref.shape[1]
-    hidden = g_ref.shape[1]
+    )(place, positives, retrieved)
+
+
+def pack_kernel(bit_ref, q_ref, k_ref, v_ref, o_ref, g_ref, u_ref, d_ref, b_ref, qkv_ref, half_qkv, half_o, half_g, half_u, half_d0, half_d1):
+    inner = q_ref.shape[0]
+
+    def half(ref, bit):
+        rows = ref.shape[0] // 2
+        return ref[pl.ds(pl.multiple_of(bit_ref[bit] * rows, rows), rows), :]
+
     for i, ref in enumerate((q_ref, k_ref, v_ref)):
-        qkv_ref[:, i * inner : (i + 1) * inner] = ref[...]
-    bit = bit_ref[0]
-    rows = half_qkv.shape[0]
-    span = pl.ds(pl.multiple_of(bit * rows, rows), rows)
-    half_qkv[...] = qkv_ref[span, :]
-    half_gu[:, :hidden] = g_ref[span, :]
-    other = pl.ds(pl.multiple_of(bit_ref[1] * rows, rows), rows)
-    half_gu[:, hidden:] = u_ref[other, :]
+        qkv_ref[:, i * inner : (i + 1) * inner] = jnp.transpose(ref[...])
+    half_qkv[...] = half(qkv_ref, 0)
     rows = o_ref.shape[0] // 2
-    half_o[:rows, :] = o_ref[pl.ds(pl.multiple_of(bit * rows, rows), rows), :]
+    half_o[:rows, :] = half(o_ref, 0)
     half_o[rows:, :] = jnp.zeros((half_o.shape[0] - rows, half_o.shape[1]), bf16)
     half_o[rows:, : b_ref.shape[1]] = b_ref[...]
-    rows = half_d.shape[0]
-    half_d[...] = d_ref[pl.ds(pl.multiple_of(bit * rows, rows), rows), :]
-
-
-def pack(bit, q, k, v, o, gate, up, down, bias):
-    depth, inner = q.shape
+    half_g[...] = half(g_ref, 0)
+    half_u[...] = half(u_ref, 1)
+    cut = half_d0.shape[1]
+    half_d0[...] = half(d_ref, 0)[:, :cut]
+    half_d1[...] = half(d_ref, 1)[:, cut:]
+
+
+def pack(bits, q, k, v, o, gate, up, down, bias):
+    inner, depth = q.shape
     hidden = gate.shape[1]
     return pl.pallas_call(
         pack_kernel,
@@ -616,13 +612,15 @@
             like((depth, 3 * inner), bf16),
             like((depth // 2, 3 * inner), bf16),
             like((inner // 2 + bias.shape[0], depth), bf16),
-            like((depth // 2, 2 * hidden), bf16),
-            like((hidden // 2, depth), bf16),
+            like((depth // 2, hidden), bf16),
+            like((depth // 2, hidden), bf16),
+            like((hidden // 2, depth // 2), bf16),
+            like((hidden // 2, depth // 2), bf16),
         ),
         compiler_params=params(12),
         cost_estimate=cost(1),
         name="pack",
-    )(bit, q, k, v, o, gate, up, down, bias)
+    )(bits, q, k, v, o, gate, up, down, bias)
 
 
 def enter_kernel(place_ref, kept_ref, near_ref, far_ref, cross_ref, gain_ref, w_ref, tok_ref, norm_ref, heads_ref):
@@ -966,48 +964,82 @@
     )(near, moved, mid, grad, gain, *contexts, *weights)
 
 
-def heads_far_kernel(norm_ref, grad_ref, ow_ref, out_ref):
+EXTRA = 16
+
+
+def extra_rows(ref, start, final_ref, ffn_ref, attn_ref, bias_ref):
+    rows = [final_ref[0:1, :], ffn_ref[0:1, :]]
+    rows.append(jnp.zeros_like(rows[0]) if attn_ref is None else attn_ref[0:1, :])
+    ones = jnp.ones((8, bias_ref.shape[2]), f32)
+    ref[start : start + EXTRA, :] = jnp.zeros((EXTRA, ref.shape[1]), f32).astype(ref.dtype)
+    for i, row in enumerate(rows):
+        ref[start + i : start + i + 1, :] = row.astype(ref.dtype)
+    for h in range(bias_ref.shape[0]):
+        sums = lax.dot_general(
+            ones,
+            bias_ref[h],
+            (((1,), (1,)), ((), ())),
+            precision=lax.Precision.HIGHEST,
+            preferred_element_type=f32,
+        )
+        ref[start + 3 + h : start + 4 + h, : sums.shape[1]] = sums[0:1, :].astype(ref.dtype)
+
+
+def heads_far_kernel(norm_ref, grad_ref, ow_ref, final_ref, ffn_ref, bias_ref, a_ref, b_ref, all_s):
     wide = grad_ref.shape[1]
-    out_ref[:, :wide] = dot_tn(norm_ref[...], grad_ref[...]).astype(bf16)
-    out_ref[:, wide:] = ow_ref[...]
-
-
-def heads_far(normed, grads, output_grad):
+    depth = norm_ref.shape[1]
+    all_s[:depth, :wide] = dot_tn(norm_ref[...], grad_ref[...])
+    all_s[:depth, wide:] = ow_ref[...].astype(f32)
+    extra_rows(all_s, depth, final_ref, ffn_ref, None, bias_ref)
+    cut = a_ref.shape[1]
+    a_ref[...] = all_s[:, :cut].astype(bf16)
+    b_ref[...] = all_s[:, cut:].astype(bf16)
+
+
+def heads_far(normed, grads, output_grad, final_gain, ffn_gain, bias_grad):
     total, depth = normed.shape
     wide = grads.shape[1] + output_grad.shape[1]
+    cut = wide * 2 // 3 // BLOCK * BLOCK
     return pl.pallas_call(
         heads_far_kernel,
-        in_specs=[pl.BlockSpec(memory_space=pltpu.VMEM)] * 3,
-        out_shape=like((depth, wide), bf16),
-        compiler_params=params(10),
+        in_specs=[pl.BlockSpec(memory_space=pltpu.VMEM)] * 6,
+        out_shape=(like((depth + EXTRA, cut), bf16), like((depth + EXTRA, wide - cut), bf16)),
+        scratch_shapes=[pltpu.VMEM((depth + EXTRA, wide), f32)],
+        compiler_params=params(14),
         cost_estimate=cost(3),
         name="heads_far",
-    )(normed, grads, output_grad)
-
-
-def heads_own_kernel(index_ref, norm_ref, grad_ref, ow_ref, moved_ref, *refs):
-    outs, sum_s = refs[:4], refs[4]
+    )(normed, grads, output_grad, final_gain, ffn_gain, bias_grad)
+
+
+def heads_own_kernel(index_ref, norm_ref, grad_ref, ow_ref, final_ref, ffn_ref, attn_ref, bias_ref, a_ref, b_ref, *refs):
+    outs, all_s = refs[:4], refs[4]
     wide = grad_ref.shape[1]
-    sum_s[:, :wide] = dot_tn(norm_ref[...], grad_ref[...]) + moved_ref[:, :wide].astype(f32)
-    sum_s[:, wide:] = ow_ref[...].astype(f32) + moved_ref[:, wide:].astype(f32)
+    depth = norm_ref.shape[1]
+    all_s[:depth, :wide] = dot_tn(norm_ref[...], grad_ref[...])
+    all_s[:depth, wide:] = ow_ref[...].astype(f32)
+    extra_rows(all_s, depth, final_ref, ffn_ref, attn_ref, bias_ref)
+    cut = a_ref.shape[1]
+    all_s[:, :cut] += a_ref[...].astype(f32)
+    all_s[:, cut:] += b_ref[...].astype(f32)
+    count = depth // 4
     for k, ref in enumerate(outs):
-        count = ref.shape[0]
         start = pl.multiple_of(jnp.bitwise_xor(index_ref[0], k) * count, count)
-        ref[...] = sum_s[pl.ds(start, count), :].astype(bf16)
-
-
-def heads_own(index, normed, grads, output_grad, moved):
+        ref[:count, :] = all_s[pl.ds(start, count), :].astype(bf16)
+        ref[count:, :] = all_s[depth:, :].astype(bf16)
+
+
+def heads_own(index, normed, grads, output_grad, final_gain, ffn_gain, attn_gain, bias_grad, moved, more):
     total, depth = normed.shape
-    wide = moved.shape[1]
+    wide = moved.shape[1] + more.shape[1]
     return pl.pallas_call(
         heads_own_kernel,
-        in_specs=[SCALARS] + [pl.BlockSpec(memory_space=pltpu.VMEM)] * 4,
-        out_shape=(like((depth // 4, wide), bf16),) * 4,
-        scratch_shapes=[pltpu.VMEM((depth, wide), f32)],
-        compiler_params=params(12),
+        in_specs=[SCALARS] + [pl.BlockSpec(memory_space=pltpu.VMEM)] * 9,
+        out_shape=(like((depth // 4 + EXTRA, wide), bf16),) * 4,
+        scratch_shapes=[pltpu.VMEM((depth + EXTRA, wide), f32)],
+        compiler_params=params(16),
         cost_estimate=cost(3),
         name="heads_own",
-    )(index, normed, grads, output_grad, moved)
+    )(index, normed, grads, output_grad, final_gain, ffn_gain, attn_gain, bias_grad, moved, more)
 
 
 def quarter_kernel(index_ref, near_ref, moved_ref, *outs):
@@ -1058,16 +1090,15 @@
         at = 0
         for group, first, last in sources:
             for k, ref in enumerate(refs[4 * group : 4 * group + 4]):
-                count = ref.shape[0]
+                count = target.shape[0] // 4
                 rows = pl.ds(pl.multiple_of(jnp.bitwise_xor(index_ref[0], k) * count, count), count)
-                target[rows, at : at + last - first] = ref[:, first:last].astype(f32)
+                target[rows, at : at + last - first] = ref[:count, first:last].astype(f32)
             at += last - first
         if turned:
             out[...] = jnp.transpose(target[...])
 
 
-def widened(index, groups, cuts, name):
-    depth = groups[0][0].shape[0] * 4
+def widened(index, depth, groups, cuts, name):
     widths = [sum(last - first for _, first, last in sources) for sources, _ in cuts]
     return pl.pallas_call(
         partial(widen_kernel, len(groups), cuts),
@@ -1222,30 +1253,26 @@
     near_tokens = to_core(kept_tokens)
     cross_rows = to_core(far_rows)
 
-    own_qkv, qkv_half, output_half, gate_up_half, down_half = pack(
+    own_qkv, qkv_half, output_half, gate_half, up_half, *down_halves = pack(
         jnp.stack(dp_bit[:2]),
-        after(query_weight, sent_rows),
-        key_weight,
-        value_weight,
+        jnp.transpose(after(query_weight, sent_rows)),
+        jnp.transpose(key_weight),
+        jnp.transpose(value_weight),
         output_weight,
         gate_weight,
         up_weight,
         down_weight,
         position_bias,
     )
+    near_tiles = bias_tiles(after(position_bias.astype(f32), qkv_half))
     qkv_half = to_x(qkv_half)
     output_half = to_x(output_half)
-    gate_up_half = to_x(gate_up_half)
-    down_half = to_x(down_half)
     far_bias = output_half[inner // 2 :, : position_bias.shape[1]]
     output_half = output_half[: inner // 2]
 
-    def other_half(got, b=0):
-        return swapped(dp_bit[b], got, to_dp[b](got))
-
-    near_tiles = bias_tiles(position_bias.astype(f32))
-    far_tiles = bias_tiles(far_bias.astype(f32))
-    tiles = (near_tiles, far_tiles)
+    def other_half(got, b=0, earlier=()):
+        return swapped(dp_bit[b], got, after(to_dp[b](got), earlier))
+
 
     row_segments = lax.dynamic_index_in_dim(doc_segments, x, 0, keepdims=False)
     chip_keep = lax.dynamic_slice_in_dim(
@@ -1267,48 +1294,52 @@
     place = sum((x if axis == "x" else dp_bit[b]) << s for s, (axis, b) in enumerate(order))
     kept_retrieved = (query_keep[:, :, None] * retrieved).reshape(query_total * query_len, doc_local)
     seg_q, seg_k = seg_q[None, :], seg_k[None, :]
-    chosen, pos_rows, col_q, col_k = choose(
-        jnp.stack([core, place, x * docs_row]),
-        positives,
-        kept_retrieved,
-        seg_q,
-        seg_k,
-        query_local,
-        query_len,
-        bits + 1,
-    )
-    segs = (col_q, seg_q, col_k, seg_k)
+    segs = (seg_q, seg_k)
     half_queries = query_total // 2
-    query_lanes = pos_rows.shape[1]
+    query_lanes = -(-half_queries // BLOCK) * BLOCK
 
     place_mp = mp.reshape(1)
     gain_attn, gain_ffn, gain_final = [g.reshape(1, width) for g in (attn_gain, ffn_gain, final_gain)]
     pieces = (kept_tokens, near_tokens, far_rows, cross_rows)
-    own_qkv = after(own_qkv, chosen)
     tokens, normed_attn, own_heads = enter(place_mp, pieces, gain_attn, own_qkv)
-    far_qkv = other_half(after(qkv_half, own_heads))
+    far_tiles = bias_tiles(after(far_bias.astype(f32), own_heads))
+    qkv_half = after(qkv_half, far_tiles)
+    gate_half = to_x(after(gate_half, own_heads))
     own_context, own_log = attend(own_heads, ranges, segs, near_tiles[0])
-    far_heads = dot_nn(normed_attn, after(far_qkv, own_context)).astype(bf16)
-    far_output = other_half(after(output_half, far_qkv))
+    far_qkv = other_half(qkv_half, 0, own_context)
+    gate_half = after(gate_half, own_context)
+    up_half = to_x(after(up_half, own_context))
+    far_heads = dot_nn(normed_attn, after(far_qkv, gate_half)).astype(bf16)
     far_context, far_log = attend(far_heads, ranges, segs, far_tiles[0])
-    far_output = after(far_output, far_context)
-    gate_up_half = after(gate_up_half, far_output)
-    far_gate = other_half(gate_up_half[:, :hidden_local])
-    far_up = other_half(gate_up_half[:, hidden_local:], 1)
+    far_output = other_half(after(output_half, far_qkv), 0, far_context)
+    far_gate = other_half(after(gate_half, far_qkv), 0, far_context)
+    up_half = after(up_half, far_context)
+    down_halves = [to_x(after(half, far_context)) for half in down_halves]
+    tiles = (near_tiles, far_tiles)
     heads = (own_heads, far_heads)
     contexts = (own_context, far_context)
     logs = (own_log, far_log)
     qkv_weights = (own_qkv, far_qkv)
     output_weights = (output_weight, far_output)
-    attn_part = sum(dot_nn(c, w) for c, w in zip(contexts, output_weights)).astype(bf16)
+    attn_part = sum(
+        dot_nn(c, w) for c, w in zip(after(contexts, far_gate, up_half), output_weights)
+    ).astype(bf16)
+    chosen, pos_rows = choose(
+        jnp.stack([core, place, x * docs_row]),
+        positives,
+        after(kept_retrieved, attn_part),
+        query_local,
+        query_len,
+        bits + 1,
+    )
     count = tokens.shape[0] // 3
     mid, normed_ffn, own_gate_up, ffn_sum = ffn_own(
         tokens, attn_part, to_core(attn_part), gain_ffn, gate_weight, up_weight, down_weight, count
     )
-    far_down = other_half(after(down_half, mid))
-    far_gate_up_out, ffn_part = ffn_far(
-        normed_ffn, *after((far_gate, far_up), ffn_sum), far_down, ffn_sum, count
-    )
+    far_up = other_half(after(up_half, attn_part), 1, ffn_sum)
+    down_halves = after(down_halves, ffn_sum)
+    far_down = jnp.concatenate([other_half(half, b) for b, half in enumerate(down_halves)], axis=1)
+    far_gate_up_out, ffn_part = ffn_far(normed_ffn, far_gate, far_up, far_down, ffn_sum, count)
     layer_out, projected, embedded = leave(
         mid, ffn_part, to_core(ffn_part), gain_final, proj_weight, count
     )
@@ -1318,7 +1349,7 @@
     for moves in rounds(order):
         query_emb = jnp.concatenate([query_emb] + [move(query_emb) for move in moves], axis=0)
     first_doc = jnp.stack([dp * doc_local + x * docs_row, place])
-    seg_col = col_q
+    seg_col = seg_q[:, :length]
     sums, logits, stats = score(
         first_doc, doc_embedded, query_emb, seg_col, chosen, pos_rows, query_len, query_local, docs_row
     )
@@ -1434,19 +1465,21 @@
         far_tiles[1],
         buckets,
     )
-    far_all = heads_far(normed_attn, far_grads, far_out)
-
-    down = added(*after(down_moves, far_all))
+    down = added(*after(down_moves, far_grads))
     down_kept, down_moved = down[:, hidden_local:], to_x(down[:, :hidden_local])
+    far_all, far_more = heads_far(normed_attn, after(far_grads, down), far_out, final_gain_part, ffn_gain_part, far_bias_grad)
+
+    down = added(after(down_moved, far_all), down_kept)
     all_moved = to_x(after(far_all, down))
     first = added(*after(first_moves, far_all))
-    first_moved = to_dp[rest[0]](first)
     rest_pieces = quarter_sums(four_index, own_rest, after(rest_moved, far_all))
     rest_moves = scattered(rest_pieces)
+    early = jnp.concatenate([first, down], axis=1)
+    early_moved = to_dp[rest[0]](early)
     proj_part = rest_of(proj_part, after(proj_moved, far_all))
     own_grads, own_bias_grad = attend_back(
         own_heads,
-        after(own_context_grad, rest_pieces, first, down, proj_part),
+        after(own_context_grad, rest_pieces, early, proj_part),
         own_context,
         own_log,
         ranges,
@@ -1455,76 +1488,69 @@
         buckets,
     )
 
+    early = rest_of(early, after(early_moved, own_grads))
+    early_all = gathered(early)
     others = added(*after(rest_moves, own_grads))
     others_moved = to_dp[rest[0]](others)
-    down = added(after(down_moved, own_grads), down_kept)
-    down_moved = to_dp[rest[0]](down)
-    first = rest_of(first, after(first_moved, own_grads))
-    first_all = gathered(first)
+    all_moved = after(all_moved, own_grads)
+    more_moved = to_x(after(far_more, all_moved))
     na_kept, na_sent, attn_gain_part = enter_back(
-        place_mp, tokens, after(own_grads, others, down, first), far_grads, qkv_weights
-    )
-    all_pieces = heads_own(four_index, normed_attn, own_grads, own_out, after(all_moved, na_sent))
+        place_mp, tokens, after(own_grads, others, early, all_moved), far_grads, qkv_weights
+    )
+    early_all = after(early_all, na_sent)
+    proj_moved = to_core(after(proj_part, na_sent))
+    all_pieces = heads_own(
+        four_index,
+        normed_attn,
+        own_grads,
+        own_out,
+        final_gain_part,
+        ffn_gain_part,
+        attn_gain_part,
+        own_bias_grad,
+        all_moved,
+        after(more_moved, na_sent, early_all, proj_moved),
+    )
     all_moves = scattered(all_pieces)
-    na_moved = to_core(after(na_sent, all_pieces))
+    others = rest_of(others, after(others_moved, all_pieces))
+
+    both = added(*after(all_moves, others))
+    both_moved = to_dp[rest[0]](both)
+    others_all = gathered(after(others, both))
+    na_moved = to_core(after(na_sent, both))
 
     stay, leaving, query_grad = inputs_back(place_mp, tokens, mid_grad, na_kept, na_moved, gain_attn)
-    back = to_x(leaving)
-    others = rest_of(others, after(others_moved, leaving))
-    down = rest_of(down, after(down_moved, leaving))
-    others_all = gathered(others)
-    down_all = gathered(down)
-    both = added(*after(all_moves, others, down))
-    both_moved = to_dp[rest[0]](both)
-
-    lanes = BLOCK
-    gains = jnp.concatenate(
-        [
-            (0.5 * final_gain_part[0]).reshape(-1, lanes),
-            (0.5 * ffn_gain_part[0]).reshape(-1, lanes),
-            attn_gain_part[0].reshape(-1, lanes),
-        ],
-        axis=0,
-    )
-    gain_rows = gains.shape[0]
-    bias_rows = [
-        jnp.pad(jnp.sum(g, axis=-1), ((0, 0), (0, lanes - buckets)))
-        for g in (own_bias_grad, far_bias_grad)
-    ]
-    packet = jnp.concatenate([gains, bias_rows[0]], axis=0)
-    packet_moved = to_x(after(jnp.concatenate([gains, bias_rows[1]], axis=0), all_pieces))
-    packet = packet + after(packet_moved, both)
-    packet_moves = [move(packet) for move in four]
-    proj_moved = to_core(after(proj_part, both))
-
-    both = rest_of(both, after(both_moved, packet))
+    both = rest_of(both, after(both_moved, others_all, leaving))
     both_all = gathered(both)
-    packet = sum(after(packet_moves, both), packet)
-    for b in rest:
-        packet = packet + to_dp[b](packet)
+    back = to_x(after(leaving, both))
+    extra = both[width // 4 :]
+    crossing = [(i, i ^ 3) for i in range(tensor_size)]
+    extra_moves = (to_x(extra), to_core(extra), lax.ppermute(extra, "mp", crossing))
     cut = hidden_local // 2
     gate_weight_grad, up_weight_grad, down_weight_grad = widened(
         four_index,
-        after((first_all, others_all, down_all), both),
+        width,
+        after((early_all, others_all), extra_moves),
         (
             (((0, 0, cut), (1, 0, cut)), False),
             (((1, cut, cut + hidden_local),), False),
-            (((2, 0, hidden_local),), True),
+            (((0, cut, cut + hidden_local),), True),
         ),
         "widen_ffn",
     )
-    packet = after(packet, up_weight_grad)
-    position_bias_grad = jnp.transpose(packet[gain_rows:, :buckets])
-    gains = packet[:gain_rows]
-    gains = (gains + to_core(gains)).reshape(3, width)
-    proj_weight_grad = widen(swapped(core, proj_part, after(proj_moved, up_weight_grad)))
-    back = widen(after(back, up_weight_grad))
+    extra_moves, back = after((extra_moves, back), up_weight_grad)
+    extra = widen(extra)
+    attn_gain_grad = extra[2] + sum(widen(moved[2]) for moved in extra_moves)
+    proj_weight_grad = widen(swapped(core, proj_part, proj_moved))
+    position_bias_grad = jnp.transpose(extra[3 : 3 + position_bias.shape[1], :buckets])
+    back = widen(back)
     doc_grad = jnp.stack([jnp.where(x == 0, stay, back), jnp.where(x == 0, back, stay)], axis=0)
 
     query_weight_grad, key_weight_grad, value_weight_grad, output_weight_grad = widened(
         four_index,
-        (after(both_all, doc_grad),),
-        tuple((((0, i * inner, (i + 1) * inner),), i == 3) for i in range(4)),
+        width,
+        (after(both_all, doc_grad, attn_gain_grad, proj_weight_grad),),
+        tuple((((0, i * inner, (i + 1) * inner),), True) for i in range(4)),
         "widen_heads",
     )
 
@@ -1533,17 +1559,17 @@
         found_share,
         doc_grad,
         query_grad.reshape(query_local, query_len, width),
-        gains[2],
-        query_weight_grad,
-        key_weight_grad,
-        value_weight_grad,
+        attn_gain_grad,
+        jnp.transpose(query_weight_grad),
+        jnp.transpose(key_weight_grad),
+        jnp.transpose(value_weight_grad),
         output_weight_grad,
         position_bias_grad,
-        gains[1],
+        extra[1],
         gate_weight_grad,
         up_weight_grad,
         down_weight_grad,
-        gains[0],
+        extra[0],
         proj_weight_grad,
     )
 

time: 391 us -> 339 us (0.87)
  waiting for transfers between devices: 120 us -> 76.3 us
  local copies, waits for them, and re-layouts: 42.5 us -> 34.3 us
    ppermute x34 -> x36, waiting for transfers between devices: 78.3 us -> 30.9 us  [over(): return lambda values: lax.ppermute(values, axis, pairs)]
    ppermute x34 -> x36, starting transfers between devices: 23.8 us -> 29.2 us  [over(): return lambda values: lax.ppermute(values, axis, pairs)]
    ppermute x48 -> x42, starting transfers between devices: 57.5 us -> 52.2 us  [exchange(): return lambda values: lax.ppermute(values, ('dp', 'mp'), pairs)]
    unnamed x177 -> x190, local copies, waits for them, and re-layouts: 33.3 us -> 28.6 us
    ppermute x48 -> x42, waiting for transfers between devices: 42.1 us -> 45.4 us  [exchange(): return lambda values: lax.ppermute(values, ('dp', 'mp'), pairs)]
  transfers between devices with their start and end apart: 82 -> 79, of which waited for: 32 -> 37; matrix products, arithmetic and copies ran while one was open for 5% -> 4% of each run, Pallas kernels for 25% -> 30%
where the time goes in v3:
time: 339 us; the launch traced here: 334 us
  Pallas kernels  126 us (37%)
  starting transfers between devices  81.8 us (24%)
  waiting for transfers between devices  76.3 us (23%)
  local copies, waits for them, and re-layouts  34.3 us (10%)
  other arithmetic  10 us (3%)
    ppermute x42, starting transfers between devices, exchange(): return lambda values: lax.ppermute(values, ('dp', 'mp'), pairs)  52.2 us
    ppermute x42, waiting for transfers between devices, exchange(): return lambda values: lax.ppermute(values, ('dp', 'mp'), pairs)  45.4 us
    ppermute x36, waiting for transfers between devices, over(): return lambda values: lax.ppermute(values, axis, pairs)  30.9 us
    pallas_call x2, Pallas kernels, attend_back(): pl.pallas_call(partial(attend_back_kernel, starts, heads, size, steps - 1...  30.4 us
    ppermute x36, starting transfers between devices, over(): return lambda values: lax.ppermute(values, axis, pairs)  29.2 us
    unnamed x190, local copies, waits for them, and re-layouts  28.6 us
    pallas_call x2, Pallas kernels, ffn_back(): pl.pallas_call(partial(ffn_back_kernel, hidden, own), grid=(total // coun...  18.9 us
    pallas_call x2, Pallas kernels, attend(): pl.pallas_call(partial(attend_kernel, heads, size, steps - 1), grid_spec=...  18.6 us
  transfers between devices with their start and end apart: 79, of which 37 were waited for; matrix products, arithmetic and copies ran while one was open for 4% of the time, Pallas kernels for 30%

profile of v3, /device:TPU:0, one launch (start us, length us, event | category | flops | bytes accessed | tf_op | source)
XLA Modules:
  0.0 333.7 jit_solution(10458020959031785629)
XLA Ops:
  31.2 3.4 %collective-permute-done.3 = bf16[384,576]{1,0:T(8,128)(2,1)} collective-permute-done((bf16[384,576]{1,0:T(8,128)(2,1)}, bf16[384,576]{1,0:T(8,128)(2,1)}, u32[]{:S(2)}, u32[]{:S(2)}) %collective-permute-start.3) | collective-permute-done | bytes 442400 | tf_op jit(solution)/shard_map/ppermute | solution.py:1221
  36.1 9.1 %attend.2 = (bf16[1152,192]{1,0:T(8,128)(2,1)S(1)}, f32[8,1152]{1,0:T(8,128)S(1)}) custom-call(s32[5]{0:T(128)S(1)} %get-tuple-element.409.lo_ref, s32[5]{0:T(128)S(1)} %get-tuple-element.410.cnt_ref, bf16[1152,576]{1,0:T(8,128)(2,1)S(1)} %get-tuple-element.190.qkv_ref, s32[1,1152]{1,0:T(1,128)S(1)} %broadcast_in_dim.27.segq_ref, ...), custom_call_target="tpu_custom_call" | custom-call | flops 27000000512 | bytes 1024 | tf_op jit(solution)/shard_map/attend/pallas_call | solution.py:174
  52.1 9.5 %attend.3 = (bf16[1152,192]{1,0:T(8,128)(2,1)S(1)}, f32[8,1152]{1,0:T(8,128)S(1)}) custom-call(s32[5]{0:T(128)S(1)} %get-tuple-element.409.lo_ref, s32[5]{0:T(128)S(1)} %get-tuple-element.410.cnt_ref, bf16[1152,576]{1,0:T(8,128)(2,1)S(1)} %convolution_convert_fusion.qkv_ref, s32[1,1152]{1,0:T(1,128)S(1)} %broadcast_in_dim.27.segq_ref, ...), custom_call_target="tpu_custom_call" | custom-call | flops 27000000512 | bytes 1024 | tf_op jit(solution)/shard_map/attend/pallas_call | solution.py:174
  71.2 5.5 %ffn_own.1 = (f32[1152,768]{1,0:T(8,128)S(1)}, bf16[1152,768]{1,0:T(8,128)(2,1)S(1)}, bf16[1152,1024]{1,0:T(8,128)(2,1)S(1)}, f32[1152,768]{1,0:T(8,128)S(1)}) custom-call(bf16[1152,768]{1,0:T(8,128)(2,1)S(1)} %copy-done.46, bf16[1152,768]{1,0:T(8,128)(2,1)S(1)} %fusion.near_ref, bf16[1152,768]{1,0:T(8,128)(2,1)} %collective-permute-done.10.moved_ref, ...), custom_call_target="tpu_custom_call" | custom-call | flops 15000000512 | bytes 1024 | tf_op jit(solution)/shard_map/ffn_own/pallas_call | solution.py:680
  80.4 4.8 %collective-permute-done.14 = bf16[256,384]{1,0:T(8,128)(2,1)S(1)} collective-permute-done((bf16[256,384]{1,0:T(8,128)(2,1)S(1)}, bf16[256,384]{1,0:T(8,128)(2,1)S(1)}, u32[]{:S(2)}, u32[]{:S(2)}) %collective-permute-start.14) | collective-permute-done | bytes 196640 | tf_op jit(solution)/shard_map/ppermute | solution.py:1221
  85.5 4.5 %ffn_far.1 = (bf16[1152,1024]{1,0:T(8,128)(2,1)S(1)}, bf16[1152,768]{1,0:T(8,128)(2,1)}) custom-call(bf16[1152,768]{1,0:T(8,128)(2,1)S(1)} %get-tuple-element.217.norm_ref.refs_1_.refs_2_, bf16[768,512]{1,0:T(8,128)(2,1)S(1)} %pad_maximum_fusion.2.g_ref.refs_4_, bf16[768,512]{1,0:T(8,128)(2,1)S(1)} %pad_maximum_fusion.3.u_ref.refs_5_, ...), custom_call_target="tpu_custom_call" | custom-call | flops 15000000512 | bytes 1024 | tf_op jit(solution)/shard_map/ffn_far/pallas_call | solution.py:717
  97.5 3.9 %leave.1 = (f32[1152,768]{1,0:T(8,128)S(1)}, f32[1152,128]{1,0:T(8,128)S(1)}, bf16[1152,128]{1,0:T(8,128)(2,1)S(1)}) custom-call(f32[1152,768]{1,0:T(8,128)S(1)} %copy-done.52, bf16[1152,768]{1,0:T(8,128)(2,1)} %get-tuple-element.227.near_ref, bf16[1152,768]{1,0:T(8,128)(2,1)} %collective-permute-done.16.moved_ref, bf16[1,768]{1,0:T(2,128)(2,1)S(1)} %reshape.82.gain_ref, ...), custom_call_target="tpu_custom_call" | custom-call | flops 12000000000 | bytes 1024 | tf_op jit(solution)/shard_map/leave/pallas_call | solution.py:748
  103.3 4.7 %collective-permute-start.19 = (bf16[64,128]{1,0:T(8,128)(2,1)S(1)}, bf16[64,128]{1,0:T(8,128)(2,1)S(1)}, u32[]{:S(2)}, u32[]{:S(2)}) collective-permute-start(bf16[64,128]{1,0:T(8,128)(2,1)S(1)} %get-tuple-element.372), channel_id=1, source_target_pairs={{0,24},{1,25},{2,26},{3,27},{4,28},{5,29},{6,30},{7,31},{8,16},{9,... | collective-permute-start | bytes 49160 | tf_op jit(solution)/shard_map/ppermute | solution.py:1235
  119.1 5.0 %score.1 = (f32[8,1024]{1,0:T(8,128)S(1)}, f32[8,128]{1,0:T(8,128)S(1)}, f32[8,128]{1,0:T(8,128)S(1)}) custom-call(s32[2]{0:T(128)S(1)} %pad_add_fusion.2.first_ref, bf16[1024,128]{1,0:T(8,128)(2,1)S(1)} %slice.137.emb_ref, bf16[1024,128]{1,0:T(8,128)(2,1)S(1)} %constant_dynamic-update-slice_fusion.qe_ref, s32[1,1024]{1,0:T(1,128)S(1)} %slice.179.seg_ref, ...), custom_call_target="tpu_custom_call" | custom-call | flops 15000000512 | bytes 1024 | tf_op jit(solution)/shard_map/score/pallas_call | solution.py:421
  137.3 5.7 %score_back.1 = (f32[1024,128]{1,0:T(8,128)S(1)}, bf16[1024,128]{1,0:T(8,128)(2,1)S(1)}) custom-call(s32[2]{0:T(128)S(1)} %pad_add_fusion.2.first_ref, bf16[1024,128]{1,0:T(8,128)(2,1)S(1)} %slice.137.emb_ref, bf16[1024,128]{1,0:T(8,128)(2,1)S(1)} %constant_dynamic-update-slice_fusion.qe_ref, s32[1,1024]{1,0:T(1,128)S(1)} %slice.179.seg_ref, ...), custom_call_target="tpu_custom_call" | custom-call | flops 15000000512 | bytes 1024 | tf_op jit(solution)/shard_map/score_back/pallas_call | solution.py:488
  162.2 4.7 %leave_back.1 = (f32[1152,768]{1,0:T(8,128)S(1)}, f32[768,128]{1,0:T(8,128)S(1)}, f32[8,768]{1,0:T(8,128)S(1)}) custom-call(s32[1]{0:T(128)} %bitcast.12.core_ref, f32[1152,768]{1,0:T(8,128)S(1)} %copy-done.55, f32[1152,128]{1,0:T(8,128)S(1)} %copy-done.71, f32[1024,128]{1,0:T(8,128)S(1)} %get-tuple-element.237.near_ref, ...), custom_call_target="tpu_custom_call" | custom-call | flops 15000000512 | bytes 1024 | tf_op jit(solution)/shard_map/leave_back/pallas_call | solution.py:808
  168.0 9.2 %ffn_back.2 = (f32[1152,768]{1,0:T(8,128)S(1)}, bf16[768,256]{1,0:T(8,128)(2,1)S(1)}, bf16[768,768]{1,0:T(8,128)(2,1)S(1)}, bf16[768,512]{1,0:T(8,128)(2,1)S(1)}) custom-call(f32[1152,768]{1,0:T(8,128)S(1)} %get-tuple-element.245.refs_0_.refs_1_.grad_ref, bf16[1152,768]{1,0:T(8,128)(2,1)S(1)} %copy-done.69, bf16[1152,1024]{1,0:T(8,128)(2,1)S(1)} %copy-done.67, ...), custom_call_target="tpu_custom_call" | custom-call | flops 30000001024 | bytes 1024 | tf_op jit(solution)/shard_map/ffn_back/pallas_call | solution.py:886
  182.0 9.7 %ffn_back.3 = (bf16[1152,768]{1,0:T(8,128)(2,1)S(1)}, bf16[768,256]{1,0:T(8,128)(2,1)S(1)}, bf16[768,768]{1,0:T(8,128)(2,1)S(1)}, bf16[192,1024]{1,0:T(8,128)(2,...) custom-call(s32[1]{0:T(128)} %bitcast.21.refs_0_.index_ref, ...), custom_call_target="tpu_custom_call" | custom-call | flops 30000001024 | bytes 1024 | tf_op jit(solution)/shard_map/ffn_back/pallas_call | solution.py:886
  197.7 4.7 %mid_back.1 = (f32[1152,768]{1,0:T(8,128)S(1)}, bf16[1152,192]{1,0:T(8,128)(2,1)S(1)}, bf16[1152,192]{1,0:T(8,128)(2,1)S(1)}, bf16[768,192]{1,0:T(8,128)(2,1)S(1...) custom-call(bf16[1152,768]{1,0:T(8,128)(2,1)S(1)} %get-tuple-element.260.near_ref, ...), custom_call_target="tpu_custom_call" | custom-call | flops 17999998976 | bytes 1024 | tf_op jit(solution)/shard_map/mid_back/pallas_call | solution.py:937
  202.5 15.2 %attend_back.2 = (bf16[1152,576]{1,0:T(8,128)(2,1)S(1)}, f32[3,32,128]{2,1,0:T(8,128)S(1)}) custom-call(s32[5]{0:T(128)S(1)} %copy-done.15, s32[5]{0:T(128)S(1)} %copy-done.17, bf16[1152,576]{1,0:T(8,128)(2,1)S(1)} %copy-done.39, bf16[1152,192]{1,0:T(8,128)(2,1)S(1)} %get-tuple-element.266.do_ref, bf16[1152,192]{1,0:T(8,128)(2,1)S(1)} %copy-done.7, ...), custom_call_target="tpu_custom_call" | custom-call | flops 44999999488 | bytes 1024 | tf_op jit(solution)/shard_map/attend_back/pallas_call | solution.py:335
  232.8 15.2 %attend_back.3 = (bf16[1152,576]{1,0:T(8,128)(2,1)S(1)}, f32[3,32,128]{2,1,0:T(8,128)S(1)}) custom-call(s32[5]{0:T(128)S(1)} %copy-done.15, s32[5]{0:T(128)S(1)} %copy-done.17, bf16[1152,576]{1,0:T(8,128)(2,1)S(1)} %copy-done.63, bf16[1152,192]{1,0:T(8,128)(2,1)S(1)} %get-tuple-element.294.do_ref, bf16[1152,192]{1,0:T(8,128)(2,1)S(1)} %copy-done.5, ...), custom_call_target="tpu_custom_call" | custom-call | flops 44999999488 | bytes 1024 | tf_op jit(solution)/shard_map/attend_back/pallas_call | solution.py:335
  248.5 3.4 %collective-permute-start.59 = (bf16[192,768]{1,0:T(8,128)(2,1)S(1)}, bf16[192,768]{1,0:T(8,128)(2,1)S(1)}, u32[]{:S(2)}, u32[]{:S(2)}) collective-permute-start(bf16[192,768]{1,0:T(8,128)(2,1)S(1)} %add_convert_fusion.4.refs_0_), channel_id=1, source_target_pairs={{0,4},{1,5},{2,6},{3,7},{4,0},{5,1},{6,2},{7,3},{8,12},{9,13},{10,... | collective-permute-start | bytes 884744 | tf_op jit(solution)/shard_map/ppermute | solution.py:1235
  253.3 3.6 %enter_back.1 = (bf16[576,768]{1,0:T(8,128)(2,1)S(1)}, bf16[576,768]{1,0:T(8,128)(2,1)S(1)}, f32[8,768]{1,0:T(8,128)S(1)}) custom-call(s32[1]{0:T(128)} %bitcast.2.place_ref, bf16[1152,768]{1,0:T(8,128)(2,1)S(1)} %copy-done.47, bf16[1152,576]{1,0:T(8,128)(2,1)S(1)} %get-tuple-element.305.own_ref.grad_ref, ...), custom_call_target="tpu_custom_call" | custom-call | flops 12000000000 | bytes 1024 | tf_op jit(solution)/shard_map/enter_back/pallas_call | solution.py:1123
  266.4 7.2 %collective-permute-done.66 = bf16[192,768]{1,0:T(8,128)(2,1)S(1)} collective-permute-done((bf16[192,768]{1,0:T(8,128)(2,1)S(1)}, bf16[192,768]{1,0:T(8,128)(2,1)S(1)}, u32[]{:S(2)}, u32[]{:S(2)}) %collective-permute-start.66) | collective-permute-done | bytes 294944 | tf_op jit(solution)/shard_map/ppermute | solution.py:1221
  273.7 6.6 %collective-permute-done.64 = bf16[208,768]{1,0:T(8,128)(2,1)S(1)} collective-permute-done((bf16[208,768]{1,0:T(8,128)(2,1)S(1)}, bf16[208,768]{1,0:T(8,128)(2,1)S(1)}, u32[]{:S(2)}, u32[]{:S(2)}) %collective-permute-start.64) | collective-permute-done | bytes 319520 | tf_op jit(solution)/shard_map/ppermute | solution.py:1235
  280.4 3.7 %collective-permute-done.65 = bf16[208,768]{1,0:T(8,128)(2,1)S(1)} collective-permute-done((bf16[208,768]{1,0:T(8,128)(2,1)S(1)}, bf16[208,768]{1,0:T(8,128)(2,1)S(1)}, u32[]{:S(2)}, u32[]{:S(2)}) %collective-permute-start.65) | collective-permute-done | bytes 319520 | tf_op jit(solution)/shard_map/ppermute | solution.py:1235
  299.4 7.3 %collective-permute-done.71.refs_7_ = bf16[192,768]{1,0:T(8,128)(2,1)S(1)} collective-permute-done((bf16[192,768]{1,0:T(8,128)(2,1)S(1)}, bf16[192,768]{1,0:T(8,128)(2,1)S(1)}, u32[]{:S(2)}, u32[]{:S(2)}) %collective-permute-start.71) | collective-permute-done | bytes 294944 | tf_op jit(solution)/shard_map/ppermute | solution.py:1235
  306.7 5.5 %collective-permute-done.70.refs_6_ = bf16[192,768]{1,0:T(8,128)(2,1)S(1)} collective-permute-done((bf16[192,768]{1,0:T(8,128)(2,1)S(1)}, bf16[192,768]{1,0:T(8,128)(2,1)S(1)}, u32[]{:S(2)}, u32[]{:S(2)}) %collective-permute-start.70) | collective-permute-done | bytes 294944 | tf_op jit(solution)/shard_map/ppermute | solution.py:1235
  322.5 6.0 %collective-permute-done.75 = bf16[256,768]{1,0:T(8,128)(2,1)S(1)} collective-permute-done((bf16[256,768]{1,0:T(8,128)(2,1)S(1)}, bf16[256,768]{1,0:T(8,128)(2,1)S(1)}, u32[]{:S(2)}, u32[]{:S(2)}) %collective-permute-start.75) | collective-permute-done | bytes 393248 | tf_op jit(solution)/shard_map/ppermute | solution.py:1221
  (431 shorter events, 172.9 us)
Async XLA Ops:
  2.8 21.2 %collective-permute-start.1 = (bf16[256,768]{1,0:T(8,128)(2,1)}, bf16[256,768]{1,0:T(8,128)(2,1)}, u32[]{:S(2)}, u32[]{:S(2)}) collective-permute-start(bf16[256,768]{1,0:T(8,128)(2,1)} %get-tuple-element.385), channel_id=1, source_target_pairs={{0,2},{1,3},{2,0},{3,1},{4,6},{5,7},{6,4},{7,5},{8,10},{9,11},{10,... | collective-permute-start | bytes 1179656 | tf_op jit(solution)/shard_map/ppermute | solution.py:1221
  6.6 17.6 %collective-permute-start = (bf16[320,768]{1,0:T(8,128)(2,1)S(1)}, bf16[320,768]{1,0:T(8,128)(2,1)}, u32[]{:S(2)}, u32[]{:S(2)}) collective-permute-start(bf16[320,768]{1,0:T(8,128)(2,1)S(1)} %pad_maximum_fusion.4.kept_ref), channel_id=1, source_target_pairs={{0,1},{1,0},{2,3},{3,2},{4,5},{5,4},{6,7},{7,6},{8,9},{9,8},{10,11... | collective-permute-start | bytes 1474568 | tf_op jit(solution)/shard_map/ppermute | solution.py:1221
  16.0 18.5 %collective-permute-start.3 = (bf16[384,576]{1,0:T(8,128)(2,1)}, bf16[384,576]{1,0:T(8,128)(2,1)}, u32[]{:S(2)}, u32[]{:S(2)}) collective-permute-start(bf16[384,576]{1,0:T(8,128)(2,1)} %get-tuple-element.191), channel_id=1, source_target_pairs={{0,2},{1,3},{2,0},{3,1},{4,6},{5,7},{6,4},{7,5},{8,10},{9,11},{10,... | collective-permute-start | bytes 1327112 | tf_op jit(solution)/shard_map/ppermute | solution.py:1221
  29.0 16.9 %collective-permute-start.6 = (bf16[384,512]{1,0:T(8,128)(2,1)S(1)}, bf16[384,512]{1,0:T(8,128)(2,1)S(1)}, u32[]{:S(2)}, u32[]{:S(2)}) collective-permute-start(bf16[384,512]{1,0:T(8,128)(2,1)S(1)} %copy-done.29), channel_id=1, source_target_pairs={{0,2},{1,3},{2,0},{3,1},{4,6},{5,7},{6,4},{7,5},{8,10},{9,11},{10,... | collective-permute-start | bytes 1179656 | tf_op jit(solution)/shard_map/ppermute | solution.py:1221
  45.3 16.4 %collective-permute-start.8 = (bf16[384,512]{1,0:T(8,128)(2,1)S(1)}, bf16[384,512]{1,0:T(8,128)(2,1)S(1)}, u32[]{:S(2)}, u32[]{:S(2)}) collective-permute-start(bf16[384,512]{1,0:T(8,128)(2,1)S(1)} %copy-done.27), channel_id=1, source_target_pairs={{0,2},{1,3},{2,0},{3,1},{4,6},{5,7},{6,4},{7,5},{8,10},{9,11},{10,... | collective-permute-start | bytes 1179656 | tf_op jit(solution)/shard_map/ppermute | solution.py:1221
  192.7 25.0 %collective-permute-start.45 = (bf16[192,1024]{1,0:T(8,128)(2,1)S(1)}, bf16[192,1024]{1,0:T(8,128)(2,1)S(1)}, u32[]{:S(2)}, u32[]{:S(2)}) collective-permute-start(bf16[192,1024]{1,0:T(8,128)(2,1)S(1)} %get-tuple-element.270), channel_id=1, source_target_pairs={{0,4},{1,5},{2,6},{3,7},{4,0},{5,1},{6,2},{7,3},{8,12},{9,13},{10,... | collective-permute-start | bytes 1179656 | tf_op jit(solution)/shard_map/ppermute | solution.py:1235
  194.3 23.5 %collective-permute-start.46 = (bf16[192,1024]{1,0:T(8,128)(2,1)S(1)}, bf16[192,1024]{1,0:T(8,128)(2,1)S(1)}, u32[]{:S(2)}, u32[]{:S(2)}) collective-permute-start(bf16[192,1024]{1,0:T(8,128)(2,1)S(1)} %get-tuple-element.271), channel_id=1, source_target_pairs={{0,8},{1,9},{2,10},{3,11},{4,12},{5,13},{6,14},{7,15},{8,0},{9,1},... | collective-permute-start | bytes 1179656 | tf_op jit(solution)/shard_map/ppermute | solution.py:1235
  194.5 23.4 %collective-permute-start.47 = (bf16[192,1024]{1,0:T(8,128)(2,1)S(1)}, bf16[192,1024]{1,0:T(8,128)(2,1)S(1)}, u32[]{:S(2)}, u32[]{:S(2)}) collective-permute-start(bf16[192,1024]{1,0:T(8,128)(2,1)S(1)} %get-tuple-element.272), channel_id=1, source_target_pairs={{0,12},{1,13},{2,14},{3,15},{4,8},{5,9},{6,10},{7,11},{8,4},{9,5},... | collective-permute-start | bytes 1179656 | tf_op jit(solution)/shard_map/ppermute | solution.py:1235
  196.3 27.1 %collective-permute-start.52 = (bf16[384,128]{1,0:T(8,128)(2,1)S(1)}, bf16[384,128]{1,0:T(8,128)(2,1)S(1)}, u32[]{:S(2)}, u32[]{:S(2)}) collective-permute-start(bf16[384,128]{1,0:T(8,128)(2,1)S(1)} %add_convert_fusion.9), channel_id=1, source_target_pairs={{0,16},{4,20},{8,24},{12,28},{16,0},{20,4},{24,8},{28,12},{1,17},{... | collective-permute-start | bytes 294920 | tf_op jit(solution)/shard_map/ppermute | solution.py:1221
  196.8 28.1 %collective-permute-start.44 = (bf16[768,768]{1,0:T(8,128)(2,1)S(1)}, bf16[768,768]{1,0:T(8,128)(2,1)S(1)}, u32[]{:S(2)}, u32[]{:S(2)}) collective-permute-start(bf16[768,768]{1,0:T(8,128)(2,1)S(1)} %get-tuple-element.265), channel_id=1, source_target_pairs={{0,2},{1,3},{2,0},{3,1},{4,6},{5,7},{6,4},{7,5},{8,10},{9,11},{10,... | collective-permute-start | bytes 3538952 | tf_op jit(solution)/shard_map/ppermute | solution.py:1221
  225.2 22.8 %collective-permute-start.53 = (bf16[192,768]{1,0:T(8,128)(2,1)S(1)}, bf16[192,768]{1,0:T(8,128)(2,1)S(1)}, u32[]{:S(2)}, u32[]{:S(2)}) collective-permute-start(bf16[192,768]{1,0:T(8,128)(2,1)S(1)} %get-tuple-element.285), channel_id=1, source_target_pairs={{0,4},{1,5},{2,6},{3,7},{4,0},{5,1},{6,2},{7,3},{8,12},{9,13},{10,... | collective-permute-start | bytes 884744 | tf_op jit(solution)/shard_map/ppermute | solution.py:1235
  226.4 21.7 %collective-permute-start.54 = (bf16[192,768]{1,0:T(8,128)(2,1)S(1)}, bf16[192,768]{1,0:T(8,128)(2,1)S(1)}, u32[]{:S(2)}, u32[]{:S(2)}) collective-permute-start(bf16[192,768]{1,0:T(8,128)(2,1)S(1)} %get-tuple-element.286), channel_id=1, source_target_pairs={{0,8},{1,9},{2,10},{3,11},{4,12},{5,13},{6,14},{7,15},{8,0},{9,1},... | collective-permute-start | bytes 884744 | tf_op jit(solution)/shard_map/ppermute | solution.py:1235
  228.7 19.4 %collective-permute-start.55 = (bf16[192,768]{1,0:T(8,128)(2,1)S(1)}, bf16[192,768]{1,0:T(8,128)(2,1)S(1)}, u32[]{:S(2)}, u32[]{:S(2)}) collective-permute-start(bf16[192,768]{1,0:T(8,128)(2,1)S(1)} %get-tuple-element.287), channel_id=1, source_target_pairs={{0,12},{1,13},{2,14},{3,15},{4,8},{5,9},{6,10},{7,11},{8,4},{9,5},... | collective-permute-start | bytes 884744 | tf_op jit(solution)/shard_map/ppermute | solution.py:1235
  229.3 19.0 %collective-permute-start.56 = (bf16[192,768]{1,0:T(8,128)(2,1)S(1)}, bf16[192,768]{1,0:T(8,128)(2,1)S(1)}, u32[]{:S(2)}, u32[]{:S(2)}) collective-permute-start(bf16[192,768]{1,0:T(8,128)(2,1)S(1)} %pad_maximum_fusion.6), channel_id=1, source_target_pairs={{0,16},{4,20},{8,24},{12,28},{16,0},{20,4},{24,8},{28,12},{1,17},{... | collective-permute-start | bytes 884744 | tf_op jit(solution)/shard_map/ppermute | solution.py:1221
  232.1 19.8 %collective-permute-start.57 = (bf16[784,512]{1,0:T(8,128)(2,1)S(1)}, bf16[784,512]{1,0:T(8,128)(2,1)S(1)}, u32[]{:S(2)}, u32[]{:S(2)}) collective-permute-start(bf16[784,512]{1,0:T(8,128)(2,1)S(1)} %get-tuple-element.303), channel_id=1, source_target_pairs={{0,2},{1,3},{2,0},{3,1},{4,6},{5,7},{6,4},{7,5},{8,10},{9,11},{10,... | collective-permute-start | bytes 2408456 | tf_op jit(solution)/shard_map/ppermute | solution.py:1221
  257.9 15.8 %collective-permute-start.66 = (bf16[192,768]{1,0:T(8,128)(2,1)S(1)}, bf16[192,768]{1,0:T(8,128)(2,1)S(1)}, u32[]{:S(2)}, u32[]{:S(2)}) collective-permute-start(bf16[192,768]{1,0:T(8,128)(2,1)S(1)} %add_convert_fusion.5), channel_id=1, source_target_pairs={{0,16},{4,20},{8,24},{12,28},{16,0},{20,4},{24,8},{28,12},{1,17},{... | collective-permute-start | bytes 884744 | tf_op jit(solution)/shard_map/ppermute | solution.py:1221
  264.3 16.1 %collective-permute-start.64 = (bf16[208,768]{1,0:T(8,128)(2,1)S(1)}, bf16[208,768]{1,0:T(8,128)(2,1)S(1)}, u32[]{:S(2)}, u32[]{:S(2)}) collective-permute-start(bf16[208,768]{1,0:T(8,128)(2,1)S(1)} %get-tuple-element.321), channel_id=1, source_target_pairs={{0,8},{1,9},{2,10},{3,11},{4,12},{5,13},{6,14},{7,15},{8,0},{9,1},... | collective-permute-start | bytes 958472 | tf_op jit(solution)/shard_map/ppermute | solution.py:1235
  264.3 19.8 %collective-permute-start.65 = (bf16[208,768]{1,0:T(8,128)(2,1)S(1)}, bf16[208,768]{1,0:T(8,128)(2,1)S(1)}, u32[]{:S(2)}, u32[]{:S(2)}) collective-permute-start(bf16[208,768]{1,0:T(8,128)(2,1)S(1)} %get-tuple-element.322), channel_id=1, source_target_pairs={{0,12},{1,13},{2,14},{3,15},{4,8},{5,9},{6,10},{7,11},{8,4},{9,5},... | collective-permute-start | bytes 958472 | tf_op jit(solution)/shard_map/ppermute | solution.py:1235
  289.1 17.6 %collective-permute-start.71 = (bf16[192,768]{1,0:T(8,128)(2,1)S(1)}, bf16[192,768]{1,0:T(8,128)(2,1)S(1)}, u32[]{:S(2)}, u32[]{:S(2)}) collective-permute-start(bf16[192,768]{1,0:T(8,128)(2,1)S(1)} %add_convert_fusion.3.refs_4_), channel_id=1, source_target_pairs={{0,12},{1,13},{2,14},{3,15},{4,8},{5,9},{6,10},{7,11},{8,4},{9,5},... | collective-permute-start | bytes 884744 | tf_op jit(solution)/shard_map/ppermute | solution.py:1235
  289.1 23.1 %collective-permute-start.70 = (bf16[192,768]{1,0:T(8,128)(2,1)S(1)}, bf16[192,768]{1,0:T(8,128)(2,1)S(1)}, u32[]{:S(2)}, u32[]{:S(2)}) collective-permute-start(bf16[192,768]{1,0:T(8,128)(2,1)S(1)} %add_convert_fusion.3.refs_4_), channel_id=1, source_target_pairs={{0,8},{1,9},{2,10},{3,11},{4,12},{5,13},{6,14},{7,15},{8,0},{9,1},... | collective-permute-start | bytes 884744 | tf_op jit(solution)/shard_map/ppermute | solution.py:1235
  291.8 20.4 %collective-permute-start.69 = (bf16[192,768]{1,0:T(8,128)(2,1)S(1)}, bf16[192,768]{1,0:T(8,128)(2,1)S(1)}, u32[]{:S(2)}, u32[]{:S(2)}) collective-permute-start(bf16[192,768]{1,0:T(8,128)(2,1)S(1)} %add_convert_fusion.3.refs_4_), channel_id=1, source_target_pairs={{0,4},{1,5},{2,6},{3,7},{4,0},{5,1},{6,2},{7,3},{8,12},{9,13},{10,... | collective-permute-start | bytes 884744 | tf_op jit(solution)/shard_map/ppermute | solution.py:1235
  292.6 19.6 %collective-permute-start.68 = (bf16[208,768]{1,0:T(8,128)(2,1)}, bf16[208,768]{1,0:T(8,128)(2,1)S(1)}, u32[]{:S(2)}, u32[]{:S(2)}) collective-permute-start(bf16[208,768]{1,0:T(8,128)(2,1)} %add_convert_fusion.2), channel_id=1, source_target_pairs={{0,16},{4,20},{8,24},{12,28},{16,0},{20,4},{24,8},{28,12},{1,17},{... | collective-permute-start | bytes 958472 | tf_op jit(solution)/shard_map/ppermute | solution.py:1221
  314.5 16.0 %collective-permute-start.78 = (bf16[208,768]{1,0:T(8,128)(2,1)S(1)}, bf16[208,768]{1,0:T(8,128)(2,1)S(1)}, u32[]{:S(2)}, u32[]{:S(2)}) collective-permute-start(bf16[208,768]{1,0:T(8,128)(2,1)S(1)} %add_convert_fusion.1.refs_0_), channel_id=1, source_target_pairs={{0,12},{1,13},{2,14},{3,15},{4,8},{5,9},{6,10},{7,11},{8,4},{9,5},... | collective-permute-start | bytes 958472 | tf_op jit(solution)/shard_map/ppermute | solution.py:1235
  315.7 15.1 %collective-permute-start.77 = (bf16[208,768]{1,0:T(8,128)(2,1)S(1)}, bf16[208,768]{1,0:T(8,128)(2,1)S(1)}, u32[]{:S(2)}, u32[]{:S(2)}) collective-permute-start(bf16[208,768]{1,0:T(8,128)(2,1)S(1)} %add_convert_fusion.1.refs_0_), channel_id=1, source_target_pairs={{0,8},{1,9},{2,10},{3,11},{4,12},{5,13},{6,14},{7,15},{8,0},{9,1},... | collective-permute-start | bytes 958472 | tf_op jit(solution)/shard_map/ppermute | solution.py:1235
  (146 other events, 1008.8 us)

commit v4 on v3

--- a/solution.py
+++ b/solution.py
@@ -416,7 +416,7 @@
     count, width = query_emb.shape
     lanes = positives.shape[1]
     length = emb.shape[0]
-    blocks = length // BLOCK
+    blocks = length // PAIR
     whole = lambda b, *_: (0, 0)
     return pl.pallas_call(
         partial(score_kernel, query_len, query_local, docs),
@@ -424,9 +424,9 @@
             num_scalar_prefetch=1,
             grid=(blocks,),
             in_specs=[
-                pl.BlockSpec((BLOCK, width), lambda b, *_: (b, 0)),
+                pl.BlockSpec((PAIR, width), lambda b, *_: (b, 0)),
                 pl.BlockSpec((count, width), whole, pipeline_mode=pl.Buffered(1)),
-                pl.BlockSpec((1, BLOCK), lambda b, *_: (0, b)),
+                pl.BlockSpec((1, PAIR), lambda b, *_: (0, b)),
                 pl.BlockSpec((8, count), whole, pipeline_mode=pl.Buffered(1)),
                 pl.BlockSpec((8, lanes), whole, pipeline_mode=pl.Buffered(1)),
             ],
@@ -442,7 +442,7 @@
             jax.ShapeDtypeStruct((8, lanes), f32),
             jax.ShapeDtypeStruct((8, lanes), f32),
         ),
-        compiler_params=params(10),
+        compiler_params=params(14),
         cost_estimate=cost(5),
         name="score",
     )(first, emb, query_emb, seg_col, chosen, positives)
@@ -483,7 +483,7 @@
     count, width = query_emb.shape
     lanes = positives.shape[1]
     length = emb.shape[0]
-    blocks = length // BLOCK
+    blocks = length // PAIR
     whole = lambda b, *_: (0, 0)
     return pl.pallas_call(
         partial(score_back_kernel, query_len, query_local, docs),
@@ -491,9 +491,9 @@
             num_scalar_prefetch=1,
             grid=(blocks,),
             in_specs=[
-                pl.BlockSpec((BLOCK, width), lambda b, *_: (b, 0)),
+                pl.BlockSpec((PAIR, width), lambda b, *_: (b, 0)),
                 pl.BlockSpec((count, width), whole, pipeline_mode=pl.Buffered(1)),
-                pl.BlockSpec((1, BLOCK), lambda b, *_: (0, b)),
+                pl.BlockSpec((1, PAIR), lambda b, *_: (0, b)),
                 pl.BlockSpec((8, count), whole, pipeline_mode=pl.Buffered(1)),
                 pl.BlockSpec((8, lanes), whole, pipeline_mode=pl.Buffered(1)),
                 pl.BlockSpec((8, count), whole, pipeline_mode=pl.Buffered(1)),
@@ -501,7 +501,7 @@
                 pl.BlockSpec((8, lanes), whole, pipeline_mode=pl.Buffered(1)),
             ],
             out_specs=[
-                pl.BlockSpec((BLOCK, width), lambda b, *_: (b, 0)),
+                pl.BlockSpec((PAIR, width), lambda b, *_: (b, 0)),
                 pl.BlockSpec((count, width), whole),
             ],
             scratch_shapes=[pltpu.VMEM((8, count), f32), pltpu.VMEM((width, count), f32)],
@@ -510,7 +510,7 @@
             jax.ShapeDtypeStruct((length, width), f32),
             jax.ShapeDtypeStruct((count, width), bf16),
         ),
-        compiler_params=params(12),
+        compiler_params=params(18),
         cost_estimate=cost(5),
         name="score_back",
     )(first, emb, query_emb, seg_col, chosen, positives, sums, logits, stats)
@@ -605,22 +605,26 @@
 def pack(bits, q, k, v, o, gate, up, down, bias):
     inner, depth = q.shape
     hidden = gate.shape[1]
+    shapes = (
+        (depth, 3 * inner),
+        (depth // 2, 3 * inner),
+        (inner // 2 + bias.shape[0], depth),
+        (depth // 2, hidden),
+        (depth // 2, hidden),
+        (hidden // 2, depth // 2),
+        (hidden // 2, depth // 2),
+    )
+    weights = (q, k, v, o, gate, up, down, bias)
     return pl.pallas_call(
         pack_kernel,
-        in_specs=[SCALARS] + [pl.BlockSpec(memory_space=pltpu.VMEM)] * 8,
-        out_shape=(
-            like((depth, 3 * inner), bf16),
-            like((depth // 2, 3 * inner), bf16),
-            like((inner // 2 + bias.shape[0], depth), bf16),
-            like((depth // 2, hidden), bf16),
-            like((depth // 2, hidden), bf16),
-            like((hidden // 2, depth // 2), bf16),
-            like((hidden // 2, depth // 2), bf16),
-        ),
-        compiler_params=params(12),
-        cost_estimate=cost(1),
+        grid=(1,),
+        in_specs=[SCALARS] + [kept(*w.shape) for w in weights],
+        out_specs=[kept(*shape) for shape in shapes],
+        out_shape=tuple(like(shape, bf16) for shape in shapes),
+        compiler_params=params(60),
+        cost_estimate=cost(3),
         name="pack",
-    )(bits, q, k, v, o, gate, up, down, bias)
+    )(bits, *weights)
 
 
 def enter_kernel(place_ref, kept_ref, near_ref, far_ref, cross_ref, gain_ref, w_ref, tok_ref, norm_ref, heads_ref):
@@ -664,14 +668,14 @@
 def ffn_own_kernel(tok_ref, near_ref, moved_ref, gain_ref, g_ref, u_ref, d_ref, mid_ref, norm_ref, gu_ref, part_ref):
     hidden = g_ref.shape[1]
     mid = tok_ref[...].astype(f32) + (near_ref[...].astype(f32) + moved_ref[...].astype(f32))
-    mid_ref[...] = mid
+    mid_ref[...] = mid.astype(bf16)
     normed = (mid * rms(mid) * gain_ref[...].astype(f32)).astype(bf16)
     norm_ref[...] = normed
     gate = dot_nn(normed, g_ref[...])
     up = dot_nn(normed, u_ref[...])
     gu_ref[:, :hidden] = gate.astype(bf16)
     gu_ref[:, hidden:] = up.astype(bf16)
-    part_ref[...] = dot_nn((gate * gelu_parts(gate) * up).astype(bf16), d_ref[...])
+    part_ref[...] = dot_nn((gate * gelu_parts(gate) * up).astype(bf16), d_ref[...]).astype(bf16)
 
 
 def ffn_own(tokens, near, moved, gain, gate, up, down, count):
@@ -689,10 +693,10 @@
             rows_of(count, depth),
         ],
         out_shape=(
-            like((total, depth), f32),
+            like((total, depth), bf16),
             like((total, depth), bf16),
             like((total, 2 * hidden), bf16),
-            like((total, depth), f32),
+            like((total, depth), bf16),
         ),
         compiler_params=params(16),
         cost_estimate=cost(5),
@@ -708,7 +712,7 @@
     gu_ref[:, :hidden] = gate.astype(bf16)
     gu_ref[:, hidden:] = up.astype(bf16)
     more = dot_nn((gate * gelu_parts(gate) * up).astype(bf16), d_ref[...])
-    out_ref[...] = (part_ref[...] + more).astype(bf16)
+    out_ref[...] = (part_ref[...].astype(f32) + more).astype(bf16)
 
 
 def ffn_far(normed, gate, up, down, partial_sum, count):
@@ -733,8 +737,8 @@
 
 
 def leave_kernel(mid_ref, near_ref, moved_ref, gain_ref, w_ref, out_ref, proj_ref, emb_ref):
-    out = mid_ref[...] + (near_ref[...].astype(f32) + moved_ref[...].astype(f32))
-    out_ref[...] = out
+    out = mid_ref[...].astype(f32) + (near_ref[...].astype(f32) + moved_ref[...].astype(f32))
+    out_ref[...] = out.astype(bf16)
     normed = (out * rms(out) * gain_ref[...].astype(f32)).astype(bf16)
     projected = dot_nn(normed, w_ref[...])
     proj_ref[...] = projected
@@ -750,7 +754,7 @@
         grid=(total // count,),
         in_specs=[rows_of(count, depth)] * 3 + [full(1, depth), full(depth, wide)],
         out_specs=[rows_of(count, depth), rows_of(count, wide), rows_of(count, wide)],
-        out_shape=(like((total, depth), f32), like((total, wide), f32), like((total, wide), bf16)),
+        out_shape=(like((total, depth), bf16), like((total, wide), f32), like((total, wide), bf16)),
         compiler_params=params(10),
         cost_estimate=cost(4),
         name="leave",
@@ -767,62 +771,55 @@
 
 def leave_back_kernel(core_ref, out_ref, proj_ref, near_ref, moved_ref, qn_ref, qm_ref, gain_ref, w_ref, grad_ref, wg_ref, gg_ref, emb_s):
     b = pl.program_id(0)
-    last = pl.num_programs(0) - 1
 
     @pl.when(b == 0)
     def _():
         wg_ref[...] = jnp.zeros(wg_ref.shape, f32)
         gg_ref[...] = jnp.zeros(gg_ref.shape, f32)
-
-    @pl.when(b < last)
-    def _():
-        emb_s[...] = near_ref[...] + moved_ref[...].astype(f32)
-
-    @pl.when(b == last)
-    def _():
-        half = qn_ref.shape[0]
+        length, half = near_ref.shape[0], qn_ref.shape[0]
         core = core_ref[0]
-        emb_s[pl.ds(pl.multiple_of(core * half, half), half), :] = qn_ref[...].astype(f32)
-        emb_s[pl.ds(pl.multiple_of((1 - core) * half, half), half), :] = qm_ref[...].astype(f32)
-
+        emb_s[:length, :] = near_ref[...] + moved_ref[...].astype(f32)
+        start = pl.multiple_of(length + core * half, half)
+        emb_s[pl.ds(start, half), :] = qn_ref[...].astype(f32)
+        start = pl.multiple_of(length + (1 - core) * half, half)
+        emb_s[pl.ds(start, half), :] = qm_ref[...].astype(f32)
+
+    count = out_ref.shape[0]
     projected = proj_ref[...]
     scale = lax.rsqrt(jnp.sum(projected * projected, axis=-1, keepdims=True) + epsilon)
     unit = projected * scale
-    grad = emb_s[...]
+    grad = emb_s[pl.ds(pl.multiple_of(b * count, count), count), :]
     grad = (scale * (grad - unit * jnp.sum(grad * unit, axis=-1, keepdims=True))).astype(bf16)
-    out = out_ref[...]
+    out = out_ref[...].astype(f32)
     gain = gain_ref[...].astype(f32)
     normed = (out * rms(out) * gain).astype(bf16)
     wg_ref[...] += dot_tn(normed, grad)
     back, addends = norm_back(out, gain, dot_nt(grad, w_ref[...]))
-    grad_ref[...] = back
+    grad_ref[...] = back.astype(bf16)
     gg_ref[0:1, :] += jnp.sum(addends, axis=0, keepdims=True)
 
 
-def leave_back(core, layer_out, projected, near, moved, query_near, query_moved, gain, weight):
+def leave_back(core, layer_out, projected, near, moved, query_near, query_moved, gain, weight, count):
     total, depth = layer_out.shape
     wide = weight.shape[1]
-    count = total - near.shape[0]
-    steps = total // count
-    clamp = pl.BlockSpec((count, wide), lambda b, *_: (jnp.minimum(b, steps - 2), 0))
     return pl.pallas_call(
         leave_back_kernel,
-        grid=(steps,),
+        grid=(total // count,),
         in_specs=[
             SCALARS,
             rows_of(count, depth),
             rows_of(count, wide),
-            clamp,
-            clamp,
-            full(count // 2, wide),
-            full(count // 2, wide),
+            full(*near.shape),
+            full(*moved.shape),
+            full(*query_near.shape),
+            full(*query_moved.shape),
             full(1, depth),
             full(depth, wide),
         ],
         out_specs=[rows_of(count, depth), kept(depth, wide), kept(8, depth)],
-        out_shape=(like((total, depth), f32), like((depth, wide), f32), like((8, depth), f32)),
-        scratch_shapes=[pltpu.VMEM((count, wide), f32)],
-        compiler_params=params(8),
+        out_shape=(like((total, depth), bf16), like((depth, wide), f32), like((8, depth), f32)),
+        scratch_shapes=[pltpu.VMEM((total, wide), f32)],
+        compiler_params=params(14),
         cost_estimate=cost(5),
         name="leave_back",
     )(core, layer_out, projected, near, moved, query_near, query_moved, gain, weight)
@@ -843,7 +840,7 @@
         up_s[...] = jnp.zeros(up_s.shape, f32)
         down_s[...] = jnp.zeros(down_s.shape, f32)
 
-    grad = grad_ref[...].astype(bf16)
+    grad = grad_ref[...]
     gate = gu_ref[:, :hidden].astype(f32)
     up = gu_ref[:, hidden:].astype(f32)
     hidden_grad = dot_nt(grad, d_ref[...])
@@ -858,7 +855,7 @@
     up_s[...] += dot_tn(normed, up_grad)
     down_s[...] += dot_tn(grad, (act * up).astype(bf16))
     back = dot_nt(gate_grad, g_ref[...]) + dot_nt(up_grad, u_ref[...])
-    nf_ref[...] = (part_in[...] + back).astype(bf16) if own else back
+    nf_ref[...] = (part_in[...].astype(f32) + back if own else back).astype(bf16)
 
     @pl.when(b == pl.num_programs(0) - 1)
     def _():
@@ -897,7 +894,7 @@
         ]
         + ([rows_of(count, depth), full(depth, hidden)] if own else []),
         out_specs=[rows_of(count, depth)] + [kept(*shape) for shape in shapes],
-        out_shape=(like((total, depth), bf16 if own else f32),) + tuple(like(shape, bf16) for shape in shapes),
+        out_shape=(like((total, depth), bf16),) + tuple(like(shape, bf16) for shape in shapes),
         scratch_shapes=[pltpu.VMEM((depth, hidden), f32)] * 3,
         compiler_params=params(28),
         cost_estimate=cost(10),
@@ -915,11 +912,10 @@
         gg_ref[...] = jnp.zeros(gg_ref.shape, f32)
 
     gradient = near_ref[...].astype(f32) + moved_ref[...].astype(f32)
-    back, addends = norm_back(mid_ref[...], gain_ref[...].astype(f32), gradient)
-    mid_grad = grad_ref[...] + back
-    out_ref[...] = mid_grad
+    back, addends = norm_back(mid_ref[...].astype(f32), gain_ref[...].astype(f32), gradient)
+    rounded = (grad_ref[...].astype(f32) + back).astype(bf16)
+    out_ref[...] = rounded
     gg_ref[0:1, :] += jnp.sum(addends, axis=0, keepdims=True)
-    rounded = mid_grad.astype(bf16)
     dc0_ref[...] = dot_nt(rounded, w0_ref[...]).astype(bf16)
     dc1_ref[...] = dot_nt(rounded, w1_ref[...]).astype(bf16)
     o0_s[...] += dot_tn(rounded, c0_ref[...])
@@ -950,7 +946,7 @@
             kept(8, depth),
         ],
         out_shape=(
-            like((total, depth), f32),
+            like((total, depth), bf16),
             like((total, inner), bf16),
             like((total, inner), bf16),
             like((depth, inner), bf16),
@@ -1142,7 +1138,7 @@
         at = pl.ds(pl.multiple_of(at, count), count)
         gradient = near_ref[at, :].astype(f32) + moved_ref[at, :].astype(f32)
         back, _ = norm_back(tok_ref[rows, :].astype(f32), gain, gradient)
-        return mid_ref[rows, :] + back
+        return mid_ref[rows, :].astype(f32) + back
 
     leave_ref[...] = piece((core + 2 * (1 - x)) * shard, (1 - x) * shard, shard).astype(bf16)
     stay_ref[...] = piece((core + 2 * x) * shard, x * shard, shard)
@@ -1422,7 +1418,7 @@
         )
 
     layer_out_grad, proj_grad, final_gain_part = leave_back(
-        core.reshape(1), layer_out, projected, demb, demb_moved, dqe, dqe_moved, gain_final, proj_weight
+        core.reshape(1), layer_out, projected, demb, demb_moved, dqe, dqe_moved, gain_final, proj_weight, count
     )
     proj_part = narrow(part(proj_grad, core, 2))
     proj_moved = to_x(proj_part)

time: 339 us -> 333 us (0.982); the launches traced: 334 us -> 333 us
  starting transfers between devices: 81.8 us -> 96 us
  local copies, waits for them, and re-layouts: 34.3 us -> 26.4 us
  waiting for transfers between devices: 76.3 us -> 71.7 us
    ppermute x36, starting transfers between devices: 29.2 us -> 41.2 us  [over(): return lambda values: lax.ppermute(values, axis, pairs)]
    pallas_call x1, Pallas kernels: 3.92 us -> 14.5 us  [leave(): pl.pallas_call(leave_kernel, grid=(total // count,), in_specs=[rows_of(co...]
    unnamed x190 -> x168, local copies, waits for them, and re-layouts: 28.6 us -> 21.7 us
    pallas_call x2, Pallas kernels: 30.4 us -> 24.3 us  [attend_back(): pl.pallas_call(partial(attend_back_kernel, starts, heads, size, steps - 1...]
    ppermute x42, waiting for transfers between devices: 45.4 us -> 41.4 us  [exchange(): return lambda values: lax.ppermute(values, ('dp', 'mp'), pairs)]
  transfers between devices with their start and end apart: 79 -> 79, of which waited for: 37 -> 35; matrix products, arithmetic and copies ran while one was open for 4% -> 4% of each run, Pallas kernels for 30% -> 28%
where the time goes in v4:
time: 333 us
  Pallas kernels  124 us (37%)
  starting transfers between devices  96 us (29%)
  waiting for transfers between devices  71.7 us (22%)
  local copies, waits for them, and re-layouts  26.4 us (8%)
  other arithmetic  9.57 us (3%)
    ppermute x42, starting transfers between devices, exchange(): return lambda values: lax.ppermute(values, ('dp', 'mp'), pairs)  53.7 us
    ppermute x42, waiting for transfers between devices, exchange(): return lambda values: lax.ppermute(values, ('dp', 'mp'), pairs)  41.4 us
    ppermute x36, starting transfers between devices, over(): return lambda values: lax.ppermute(values, axis, pairs)  41.2 us
    ppermute x36, waiting for transfers between devices, over(): return lambda values: lax.ppermute(values, axis, pairs)  30.3 us
    pallas_call x2, Pallas kernels, attend_back(): pl.pallas_call(partial(attend_back_kernel, starts, heads, size, steps - 1...  24.3 us
    unnamed x168, local copies, waits for them, and re-layouts  21.7 us
    pallas_call x2, Pallas kernels, ffn_back(): pl.pallas_call(partial(ffn_back_kernel, hidden, own), grid=(total // coun...  18.6 us
    pallas_call x2, Pallas kernels, attend(): pl.pallas_call(partial(attend_kernel, heads, size, steps - 1), grid_spec=...  15.4 us
  transfers between devices with their start and end apart: 79, of which 35 were waited for; matrix products, arithmetic and copies ran while one was open for 4% of the time, Pallas kernels for 28%

profile of v4, /device:TPU:0, one launch (start us, length us, event | category | flops | bytes accessed | tf_op | source)
XLA Modules:
  0.0 332.8 jit_solution(8395379963214501453)
XLA Ops:
  7.2 4.0 %pack.1 = (bf16[768,576]{1,0:T(8,128)(2,1)}, bf16[384,576]{1,0:T(8,128)(2,1)}, bf16[128,768]{1,0:T(8,128)(2,1)}, bf16[384,512]{1,0:T(8,128)(2,1)}, bf16[384,512]...) custom-call(s32[2]{0:T(128)} %pad_add_fusion.3.bit_ref, bf16[192,768]{1,0:T(8,128)(2,1)} %bitcast.49, ...), custom_call_target="tpu_custom_call" | custom-call | flops 8999999488 | bytes 1024 | tf_op jit(solution)/shard_map/pack/pallas_call | solution.py:618
  31.2 7.7 %attend.2 = (bf16[1152,192]{1,0:T(8,128)(2,1)S(1)}, f32[8,1152]{1,0:T(8,128)S(1)}) custom-call(s32[5]{0:T(128)S(1)} %get-tuple-element.409.lo_ref, s32[5]{0:T(128)S(1)} %get-tuple-element.410.cnt_ref, bf16[1152,576]{1,0:T(8,128)(2,1)S(1)} %get-tuple-element.190.qkv_ref, s32[1,1152]{1,0:T(1,128)S(1)} %broadcast_in_dim.27.segq_ref, ...), custom_call_target="tpu_custom_call" | custom-call | flops 27000000512 | bytes 1024 | tf_op jit(solution)/shard_map/attend/pallas_call | solution.py:174
  46.0 7.7 %attend.3 = (bf16[1152,192]{1,0:T(8,128)(2,1)S(1)}, f32[8,1152]{1,0:T(8,128)S(1)}) custom-call(s32[5]{0:T(128)S(1)} %get-tuple-element.409.lo_ref, s32[5]{0:T(128)S(1)} %get-tuple-element.410.cnt_ref, bf16[1152,576]{1,0:T(8,128)(2,1)S(1)} %convolution_convert_fusion.qkv_ref, s32[1,1152]{1,0:T(1,128)S(1)} %broadcast_in_dim.27.segq_ref, ...), custom_call_target="tpu_custom_call" | custom-call | flops 27000000512 | bytes 1024 | tf_op jit(solution)/shard_map/attend/pallas_call | solution.py:174
  64.1 5.8 %ffn_own.1 = (bf16[1152,768]{1,0:T(8,128)(2,1)S(1)}, bf16[1152,768]{1,0:T(8,128)(2,1)S(1)}, bf16[1152,1024]{1,0:T(8,128)(2,1)S(1)}, bf16[1152,768]{1,0:T(8,128)(2,1)S(1)}) custom-call(bf16[1152,768]{1,0:T(8,128)(2,1)S(1)} %copy-done.31, bf16[1152,768]{1,0:T(8,128)(2,1)S(1)} %fusion.near_ref, bf16[1152,768]{1,0:T(8,128)(2,1)} %collective-permute-done.10.moved_ref, ...), custom_call_target="tpu_custom_call" | custom-call | flops 15000000512 | bytes 1024 | tf_op jit(solution)/shard_map/ffn_own/pallas_call | solution.py:684
  74.5 3.8 %collective-permute-done.14 = bf16[256,384]{1,0:T(8,128)(2,1)S(1)} collective-permute-done((bf16[256,384]{1,0:T(8,128)(2,1)S(1)}, bf16[256,384]{1,0:T(8,128)(2,1)S(1)}, u32[]{:S(2)}, u32[]{:S(2)}) %collective-permute-start.14) | collective-permute-done | bytes 196640 | tf_op jit(solution)/shard_map/ppermute | solution.py:1217
  79.7 4.6 %ffn_far.1 = (bf16[1152,1024]{1,0:T(8,128)(2,1)S(1)}, bf16[1152,768]{1,0:T(8,128)(2,1)}) custom-call(bf16[1152,768]{1,0:T(8,128)(2,1)S(1)} %get-tuple-element.217.norm_ref.refs_1_.refs_2_, bf16[768,512]{1,0:T(8,128)(2,1)S(1)} %pad_maximum_fusion.2.g_ref.refs_4_, bf16[768,512]{1,0:T(8,128)(2,1)S(1)} %pad_maximum_fusion.3.u_ref.refs_5_, ...), custom_call_target="tpu_custom_call" | custom-call | flops 15000000512 | bytes 1024 | tf_op jit(solution)/shard_map/ffn_far/pallas_call | solution.py:721
  91.2 14.5 %leave.1 = (bf16[1152,768]{1,0:T(8,128)(2,1)S(1)}, f32[1152,128]{1,0:T(8,128)S(1)}, bf16[1152,128]{1,0:T(8,128)(2,1)S(1)}) custom-call(bf16[1152,768]{1,0:T(8,128)(2,1)S(1)} %copy-done.45, bf16[1152,768]{1,0:T(8,128)(2,1)} %get-tuple-element.227.near_ref, bf16[1152,768]{1,0:T(8,128)(2,1)} %collective-permute-done.16.moved_ref, ...), custom_call_target="tpu_custom_call" | custom-call | flops 12000000000 | bytes 1024 | tf_op jit(solution)/shard_map/leave/pallas_call | solution.py:752
  107.8 5.4 %collective-permute-start.19 = (bf16[64,128]{1,0:T(8,128)(2,1)S(1)}, bf16[64,128]{1,0:T(8,128)(2,1)S(1)}, u32[]{:S(2)}, u32[]{:S(2)}) collective-permute-start(bf16[64,128]{1,0:T(8,128)(2,1)S(1)} %get-tuple-element.372), channel_id=1, source_target_pairs={{0,24},{1,25},{2,26},{3,27},{4,28},{5,29},{6,30},{7,31},{8,16},{9,... | collective-permute-start | bytes 49160 | tf_op jit(solution)/shard_map/ppermute | solution.py:1231
  124.3 4.1 %score.1 = (f32[8,1024]{1,0:T(8,128)S(1)}, f32[8,128]{1,0:T(8,128)S(1)}, f32[8,128]{1,0:T(8,128)S(1)}) custom-call(s32[2]{0:T(128)S(1)} %pad_add_fusion.2.first_ref, bf16[1024,128]{1,0:T(8,128)(2,1)S(1)} %slice.137.emb_ref, bf16[1024,128]{1,0:T(8,128)(2,1)S(1)} %constant_dynamic-update-slice_fusion.qe_ref, s32[1,1024]{1,0:T(1,128)S(1)} %slice.179.seg_ref, ...), custom_call_target="tpu_custom_call" | custom-call | flops 15000000512 | bytes 1024 | tf_op jit(solution)/shard_map/score/pallas_call | solution.py:421
  141.4 4.2 %score_back.1 = (f32[1024,128]{1,0:T(8,128)S(1)}, bf16[1024,128]{1,0:T(8,128)(2,1)S(1)}) custom-call(s32[2]{0:T(128)S(1)} %pad_add_fusion.2.first_ref, bf16[1024,128]{1,0:T(8,128)(2,1)S(1)} %slice.137.emb_ref, bf16[1024,128]{1,0:T(8,128)(2,1)S(1)} %constant_dynamic-update-slice_fusion.qe_ref, s32[1,1024]{1,0:T(1,128)S(1)} %slice.179.seg_ref, ...), custom_call_target="tpu_custom_call" | custom-call | flops 15000000512 | bytes 1024 | tf_op jit(solution)/shard_map/score_back/pallas_call | solution.py:488
  168.4 9.3 %ffn_back.2 = (bf16[1152,768]{1,0:T(8,128)(2,1)S(1)}, bf16[768,256]{1,0:T(8,128)(2,1)S(1)}, bf16[768,768]{1,0:T(8,128)(2,1)S(1)}, bf16[768,512]{1,0:T(8,128)(2,1)S(1)}) custom-call(bf16[1152,768]{1,0:T(8,128)(2,1)S(1)} %get-tuple-element.245.refs_0_.refs_1_.grad_ref, bf16[1152,768]{1,0:T(8,128)(2,1)S(1)} %copy-done.56, bf16[1152,1024]{1,0:T(8,128)(2,1)S(1)} %copy-done.54, ...), custom_call_target="tpu_custom_call" | custom-call | flops 30000001024 | bytes 1024 | tf_op jit(solution)/shard_map/ffn_back/pallas_call | solution.py:883
  182.4 9.3 %ffn_back.3 = (bf16[1152,768]{1,0:T(8,128)(2,1)S(1)}, bf16[768,256]{1,0:T(8,128)(2,1)S(1)}, bf16[768,768]{1,0:T(8,128)(2,1)S(1)}, bf16[192,1024]{1,0:T(8,128)(2,...) custom-call(s32[1]{0:T(128)} %bitcast.21.refs_0_.index_ref, ...), custom_call_target="tpu_custom_call" | custom-call | flops 30000001024 | bytes 1024 | tf_op jit(solution)/shard_map/ffn_back/pallas_call | solution.py:883
  197.7 4.8 %mid_back.1 = (bf16[1152,768]{1,0:T(8,128)(2,1)S(1)}, bf16[1152,192]{1,0:T(8,128)(2,1)S(1)}, bf16[1152,192]{1,0:T(8,128)(2,1)S(1)}, bf16[768,192]{1,0:T(8,128)(2...) custom-call(bf16[1152,768]{1,0:T(8,128)(2,1)S(1)} %get-tuple-element.260.near_ref, ...), custom_call_target="tpu_custom_call" | custom-call | flops 17999998976 | bytes 1024 | tf_op jit(solution)/shard_map/mid_back/pallas_call | solution.py:933
  202.6 12.2 %attend_back.2 = (bf16[1152,576]{1,0:T(8,128)(2,1)S(1)}, f32[3,32,128]{2,1,0:T(8,128)S(1)}) custom-call(s32[5]{0:T(128)S(1)} %copy-done.15, s32[5]{0:T(128)S(1)} %copy-done.17, bf16[1152,576]{1,0:T(8,128)(2,1)S(1)} %copy-done.29, bf16[1152,192]{1,0:T(8,128)(2,1)S(1)} %get-tuple-element.266.do_ref, bf16[1152,192]{1,0:T(8,128)(2,1)S(1)} %copy-done.7, ...), custom_call_target="tpu_custom_call" | custom-call | flops 44999999488 | bytes 1024 | tf_op jit(solution)/shard_map/attend_back/pallas_call | solution.py:335
  220.5 4.6 %collective-permute-start.51 = (bf16[192,512]{1,0:T(8,128)(2,1)S(1)}, bf16[192,512]{1,0:T(8,128)(2,1)S(1)}, u32[]{:S(2)}, u32[]{:S(2)}) collective-permute-start(bf16[192,512]{1,0:T(8,128)(2,1)S(1)} %slice.181), channel_id=1, source_target_pairs={{0,2},{1,3},{2,0},{3,1},{4,6},{5,7},{6,4},{7,5},{8,10},{9,11},{10,... | collective-permute-start | bytes 589832 | tf_op jit(solution)/shard_map/ppermute | solution.py:1217
  232.0 12.1 %attend_back.3 = (bf16[1152,576]{1,0:T(8,128)(2,1)S(1)}, f32[3,32,128]{2,1,0:T(8,128)S(1)}) custom-call(s32[5]{0:T(128)S(1)} %copy-done.15, s32[5]{0:T(128)S(1)} %copy-done.17, bf16[1152,576]{1,0:T(8,128)(2,1)S(1)} %copy-done.43, bf16[1152,192]{1,0:T(8,128)(2,1)S(1)} %get-tuple-element.294.do_ref, bf16[1152,192]{1,0:T(8,128)(2,1)S(1)} %copy-done.5, ...), custom_call_target="tpu_custom_call" | custom-call | flops 44999999488 | bytes 1024 | tf_op jit(solution)/shard_map/attend_back/pallas_call | solution.py:335
  249.7 3.5 %collective-permute-start.58 = (bf16[784,256]{1,0:T(8,128)(2,1)S(1)}, bf16[784,256]{1,0:T(8,128)(2,1)S(1)}, u32[]{:S(2)}, u32[]{:S(2)}) collective-permute-start(bf16[784,256]{1,0:T(8,128)(2,1)S(1)} %get-tuple-element.312), channel_id=1, source_target_pairs={{0,2},{1,3},{2,0},{3,1},{4,6},{5,7},{6,4},{7,5},{8,10},{9,11},{10,... | collective-permute-start | bytes 1204232 | tf_op jit(solution)/shard_map/ppermute | solution.py:1217
  253.2 3.5 %enter_back.1 = (bf16[576,768]{1,0:T(8,128)(2,1)S(1)}, bf16[576,768]{1,0:T(8,128)(2,1)S(1)}, f32[8,768]{1,0:T(8,128)S(1)}) custom-call(s32[1]{0:T(128)} %bitcast.2.place_ref, bf16[1152,768]{1,0:T(8,128)(2,1)S(1)} %copy-done.32, bf16[1152,576]{1,0:T(8,128)(2,1)S(1)} %get-tuple-element.305.own_ref.grad_ref, ...), custom_call_target="tpu_custom_call" | custom-call | flops 12000000000 | bytes 1024 | tf_op jit(solution)/shard_map/enter_back/pallas_call | solution.py:1119
  264.6 8.7 %collective-permute-done.66 = bf16[192,768]{1,0:T(8,128)(2,1)S(1)} collective-permute-done((bf16[192,768]{1,0:T(8,128)(2,1)S(1)}, bf16[192,768]{1,0:T(8,128)(2,1)S(1)}, u32[]{:S(2)}, u32[]{:S(2)}) %collective-permute-start.66) | collective-permute-done | bytes 294944 | tf_op jit(solution)/shard_map/ppermute | solution.py:1217
  273.4 4.9 %collective-permute-done.64 = bf16[208,768]{1,0:T(8,128)(2,1)S(1)} collective-permute-done((bf16[208,768]{1,0:T(8,128)(2,1)S(1)}, bf16[208,768]{1,0:T(8,128)(2,1)S(1)}, u32[]{:S(2)}, u32[]{:S(2)}) %collective-permute-start.64) | collective-permute-done | bytes 319520 | tf_op jit(solution)/shard_map/ppermute | solution.py:1231
  278.3 4.9 %collective-permute-done.65 = bf16[208,768]{1,0:T(8,128)(2,1)S(1)} collective-permute-done((bf16[208,768]{1,0:T(8,128)(2,1)S(1)}, bf16[208,768]{1,0:T(8,128)(2,1)S(1)}, u32[]{:S(2)}, u32[]{:S(2)}) %collective-permute-start.65) | collective-permute-done | bytes 319520 | tf_op jit(solution)/shard_map/ppermute | solution.py:1231
  299.7 6.2 %collective-permute-done.71.refs_7_ = bf16[192,768]{1,0:T(8,128)(2,1)S(1)} collective-permute-done((bf16[192,768]{1,0:T(8,128)(2,1)S(1)}, bf16[192,768]{1,0:T(8,128)(2,1)S(1)}, u32[]{:S(2)}, u32[]{:S(2)}) %collective-permute-start.71) | collective-permute-done | bytes 294944 | tf_op jit(solution)/shard_map/ppermute | solution.py:1231
  305.9 5.1 %collective-permute-done.70.refs_6_ = bf16[192,768]{1,0:T(8,128)(2,1)S(1)} collective-permute-done((bf16[192,768]{1,0:T(8,128)(2,1)S(1)}, bf16[192,768]{1,0:T(8,128)(2,1)S(1)}, u32[]{:S(2)}, u32[]{:S(2)}) %collective-permute-start.70) | collective-permute-done | bytes 294944 | tf_op jit(solution)/shard_map/ppermute | solution.py:1231
  322.0 5.9 %collective-permute-done.75 = bf16[256,768]{1,0:T(8,128)(2,1)S(1)} collective-permute-done((bf16[256,768]{1,0:T(8,128)(2,1)S(1)}, bf16[256,768]{1,0:T(8,128)(2,1)S(1)}, u32[]{:S(2)}, u32[]{:S(2)}) %collective-permute-start.75) | collective-permute-done | bytes 393248 | tf_op jit(solution)/shard_map/ppermute | solution.py:1217
  (409 shorter events, 173.7 us)
Async XLA Ops:
  1.9 16.3 %collective-permute-start.1 = (bf16[256,768]{1,0:T(8,128)(2,1)S(1)}, bf16[256,768]{1,0:T(8,128)(2,1)S(1)}, u32[]{:S(2)}, u32[]{:S(2)}) collective-permute-start(bf16[256,768]{1,0:T(8,128)(2,1)S(1)} %get-tuple-element.385), channel_id=1, source_target_pairs={{0,2},{1,3},{2,0},{3,1},{4,6},{5,7},{6,4},{7,5},{8,10},{9,11},{10,... | collective-permute-start | bytes 1179656 | tf_op jit(solution)/shard_map/ppermute | solution.py:1217
  11.2 18.4 %collective-permute-start.3 = (bf16[384,576]{1,0:T(8,128)(2,1)}, bf16[384,576]{1,0:T(8,128)(2,1)S(1)}, u32[]{:S(2)}, u32[]{:S(2)}) collective-permute-start(bf16[384,576]{1,0:T(8,128)(2,1)} %get-tuple-element.191), channel_id=1, source_target_pairs={{0,2},{1,3},{2,0},{3,1},{4,6},{5,7},{6,4},{7,5},{8,10},{9,11},{10,... | collective-permute-start | bytes 1327112 | tf_op jit(solution)/shard_map/ppermute | solution.py:1217
  23.1 18.9 %collective-permute-start.6 = (bf16[384,512]{1,0:T(8,128)(2,1)S(1)}, bf16[384,512]{1,0:T(8,128)(2,1)S(1)}, u32[]{:S(2)}, u32[]{:S(2)}) collective-permute-start(bf16[384,512]{1,0:T(8,128)(2,1)S(1)} %copy-done.79), channel_id=1, source_target_pairs={{0,2},{1,3},{2,0},{3,1},{4,6},{5,7},{6,4},{7,5},{8,10},{9,11},{10,... | collective-permute-start | bytes 1179656 | tf_op jit(solution)/shard_map/ppermute | solution.py:1217
  38.9 14.9 %collective-permute-start.8 = (bf16[384,512]{1,0:T(8,128)(2,1)S(1)}, bf16[384,512]{1,0:T(8,128)(2,1)S(1)}, u32[]{:S(2)}, u32[]{:S(2)}) collective-permute-start(bf16[384,512]{1,0:T(8,128)(2,1)S(1)} %copy-done.78), channel_id=1, source_target_pairs={{0,2},{1,3},{2,0},{3,1},{4,6},{5,7},{6,4},{7,5},{8,10},{9,11},{10,... | collective-permute-start | bytes 1179656 | tf_op jit(solution)/shard_map/ppermute | solution.py:1217
  56.5 14.8 %collective-permute-start.12 = (bf16[256,384]{1,0:T(8,128)(2,1)}, bf16[256,384]{1,0:T(8,128)(2,1)S(1)}, u32[]{:S(2)}, u32[]{:S(2)}) collective-permute-start(bf16[256,384]{1,0:T(8,128)(2,1)} %get-tuple-element.222), channel_id=1, source_target_pairs={{0,2},{1,3},{2,0},{3,1},{4,6},{5,7},{6,4},{7,5},{8,10},{9,11},{10,... | collective-permute-start | bytes 589832 | tf_op jit(solution)/shard_map/ppermute | solution.py:1217
  192.7 22.0 %collective-permute-start.45 = (bf16[192,1024]{1,0:T(8,128)(2,1)S(1)}, bf16[192,1024]{1,0:T(8,128)(2,1)S(1)}, u32[]{:S(2)}, u32[]{:S(2)}) collective-permute-start(bf16[192,1024]{1,0:T(8,128)(2,1)S(1)} %get-tuple-element.270), channel_id=1, source_target_pairs={{0,4},{1,5},{2,6},{3,7},{4,0},{5,1},{6,2},{7,3},{8,12},{9,13},{10,... | collective-permute-start | bytes 1179656 | tf_op jit(solution)/shard_map/ppermute | solution.py:1231
  194.3 21.8 %collective-permute-start.46 = (bf16[192,1024]{1,0:T(8,128)(2,1)S(1)}, bf16[192,1024]{1,0:T(8,128)(2,1)S(1)}, u32[]{:S(2)}, u32[]{:S(2)}) collective-permute-start(bf16[192,1024]{1,0:T(8,128)(2,1)S(1)} %get-tuple-element.271), channel_id=1, source_target_pairs={{0,8},{1,9},{2,10},{3,11},{4,12},{5,13},{6,14},{7,15},{8,0},{9,1},... | collective-permute-start | bytes 1179656 | tf_op jit(solution)/shard_map/ppermute | solution.py:1231
  194.5 23.6 %collective-permute-start.47 = (bf16[192,1024]{1,0:T(8,128)(2,1)S(1)}, bf16[192,1024]{1,0:T(8,128)(2,1)S(1)}, u32[]{:S(2)}, u32[]{:S(2)}) collective-permute-start(bf16[192,1024]{1,0:T(8,128)(2,1)S(1)} %get-tuple-element.272), channel_id=1, source_target_pairs={{0,12},{1,13},{2,14},{3,15},{4,8},{5,9},{6,10},{7,11},{8,4},{9,5},... | collective-permute-start | bytes 1179656 | tf_op jit(solution)/shard_map/ppermute | solution.py:1231
  196.3 24.2 %collective-permute-start.52 = (bf16[384,128]{1,0:T(8,128)(2,1)S(1)}, bf16[384,128]{1,0:T(8,128)(2,1)S(1)}, u32[]{:S(2)}, u32[]{:S(2)}) collective-permute-start(bf16[384,128]{1,0:T(8,128)(2,1)S(1)} %add_convert_fusion.9), channel_id=1, source_target_pairs={{0,16},{4,20},{8,24},{12,28},{16,0},{20,4},{24,8},{28,12},{1,17},{... | collective-permute-start | bytes 294920 | tf_op jit(solution)/shard_map/ppermute | solution.py:1217
  196.8 28.3 %collective-permute-start.44 = (bf16[768,768]{1,0:T(8,128)(2,1)S(1)}, bf16[768,768]{1,0:T(8,128)(2,1)S(1)}, u32[]{:S(2)}, u32[]{:S(2)}) collective-permute-start(bf16[768,768]{1,0:T(8,128)(2,1)S(1)} %get-tuple-element.265), channel_id=1, source_target_pairs={{0,2},{1,3},{2,0},{3,1},{4,6},{5,7},{6,4},{7,5},{8,10},{9,11},{10,... | collective-permute-start | bytes 3538952 | tf_op jit(solution)/shard_map/ppermute | solution.py:1217
  225.4 18.7 %collective-permute-start.53 = (bf16[192,768]{1,0:T(8,128)(2,1)S(1)}, bf16[192,768]{1,0:T(8,128)(2,1)S(1)}, u32[]{:S(2)}, u32[]{:S(2)}) collective-permute-start(bf16[192,768]{1,0:T(8,128)(2,1)S(1)} %get-tuple-element.285), channel_id=1, source_target_pairs={{0,4},{1,5},{2,6},{3,7},{4,0},{5,1},{6,2},{7,3},{8,12},{9,13},{10,... | collective-permute-start | bytes 884744 | tf_op jit(solution)/shard_map/ppermute | solution.py:1231
  226.7 17.4 %collective-permute-start.54 = (bf16[192,768]{1,0:T(8,128)(2,1)S(1)}, bf16[192,768]{1,0:T(8,128)(2,1)S(1)}, u32[]{:S(2)}, u32[]{:S(2)}) collective-permute-start(bf16[192,768]{1,0:T(8,128)(2,1)S(1)} %get-tuple-element.286), channel_id=1, source_target_pairs={{0,8},{1,9},{2,10},{3,11},{4,12},{5,13},{6,14},{7,15},{8,0},{9,1},... | collective-permute-start | bytes 884744 | tf_op jit(solution)/shard_map/ppermute | solution.py:1231
  229.4 16.4 %collective-permute-start.55 = (bf16[192,768]{1,0:T(8,128)(2,1)S(1)}, bf16[192,768]{1,0:T(8,128)(2,1)S(1)}, u32[]{:S(2)}, u32[]{:S(2)}) collective-permute-start(bf16[192,768]{1,0:T(8,128)(2,1)S(1)} %get-tuple-element.287), channel_id=1, source_target_pairs={{0,12},{1,13},{2,14},{3,15},{4,8},{5,9},{6,10},{7,11},{8,4},{9,5},... | collective-permute-start | bytes 884744 | tf_op jit(solution)/shard_map/ppermute | solution.py:1231
  229.6 16.4 %collective-permute-start.56 = (bf16[192,768]{1,0:T(8,128)(2,1)S(1)}, bf16[192,768]{1,0:T(8,128)(2,1)S(1)}, u32[]{:S(2)}, u32[]{:S(2)}) collective-permute-start(bf16[192,768]{1,0:T(8,128)(2,1)S(1)} %pad_maximum_fusion.6), channel_id=1, source_target_pairs={{0,16},{4,20},{8,24},{12,28},{16,0},{20,4},{24,8},{28,12},{1,17},{... | collective-permute-start | bytes 884744 | tf_op jit(solution)/shard_map/ppermute | solution.py:1217
  231.9 17.8 %collective-permute-start.57 = (bf16[784,512]{1,0:T(8,128)(2,1)S(1)}, bf16[784,512]{1,0:T(8,128)(2,1)S(1)}, u32[]{:S(2)}, u32[]{:S(2)}) collective-permute-start(bf16[784,512]{1,0:T(8,128)(2,1)S(1)} %get-tuple-element.303), channel_id=1, source_target_pairs={{0,2},{1,3},{2,0},{3,1},{4,6},{5,7},{6,4},{7,5},{8,10},{9,11},{10,... | collective-permute-start | bytes 2408456 | tf_op jit(solution)/shard_map/ppermute | solution.py:1217
  256.8 16.5 %collective-permute-start.66 = (bf16[192,768]{1,0:T(8,128)(2,1)S(1)}, bf16[192,768]{1,0:T(8,128)(2,1)S(1)}, u32[]{:S(2)}, u32[]{:S(2)}) collective-permute-start(bf16[192,768]{1,0:T(8,128)(2,1)S(1)} %add_convert_fusion.5), channel_id=1, source_target_pairs={{0,16},{4,20},{8,24},{12,28},{16,0},{20,4},{24,8},{28,12},{1,17},{... | collective-permute-start | bytes 884744 | tf_op jit(solution)/shard_map/ppermute | solution.py:1217
  262.0 16.4 %collective-permute-start.64 = (bf16[208,768]{1,0:T(8,128)(2,1)S(1)}, bf16[208,768]{1,0:T(8,128)(2,1)S(1)}, u32[]{:S(2)}, u32[]{:S(2)}) collective-permute-start(bf16[208,768]{1,0:T(8,128)(2,1)S(1)} %get-tuple-element.321), channel_id=1, source_target_pairs={{0,8},{1,9},{2,10},{3,11},{4,12},{5,13},{6,14},{7,15},{8,0},{9,1},... | collective-permute-start | bytes 958472 | tf_op jit(solution)/shard_map/ppermute | solution.py:1231
  263.8 19.4 %collective-permute-start.65 = (bf16[208,768]{1,0:T(8,128)(2,1)S(1)}, bf16[208,768]{1,0:T(8,128)(2,1)S(1)}, u32[]{:S(2)}, u32[]{:S(2)}) collective-permute-start(bf16[208,768]{1,0:T(8,128)(2,1)S(1)} %get-tuple-element.322), channel_id=1, source_target_pairs={{0,12},{1,13},{2,14},{3,15},{4,8},{5,9},{6,10},{7,11},{8,4},{9,5},... | collective-permute-start | bytes 958472 | tf_op jit(solution)/shard_map/ppermute | solution.py:1231
  288.3 17.6 %collective-permute-start.71 = (bf16[192,768]{1,0:T(8,128)(2,1)S(1)}, bf16[192,768]{1,0:T(8,128)(2,1)S(1)}, u32[]{:S(2)}, u32[]{:S(2)}) collective-permute-start(bf16[192,768]{1,0:T(8,128)(2,1)S(1)} %add_convert_fusion.3.refs_4_), channel_id=1, source_target_pairs={{0,12},{1,13},{2,14},{3,15},{4,8},{5,9},{6,10},{7,11},{8,4},{9,5},... | collective-permute-start | bytes 884744 | tf_op jit(solution)/shard_map/ppermute | solution.py:1231
  288.3 22.7 %collective-permute-start.70 = (bf16[192,768]{1,0:T(8,128)(2,1)S(1)}, bf16[192,768]{1,0:T(8,128)(2,1)S(1)}, u32[]{:S(2)}, u32[]{:S(2)}) collective-permute-start(bf16[192,768]{1,0:T(8,128)(2,1)S(1)} %add_convert_fusion.3.refs_4_), channel_id=1, source_target_pairs={{0,8},{1,9},{2,10},{3,11},{4,12},{5,13},{6,14},{7,15},{8,0},{9,1},... | collective-permute-start | bytes 884744 | tf_op jit(solution)/shard_map/ppermute | solution.py:1231
  290.5 20.4 %collective-permute-start.69 = (bf16[192,768]{1,0:T(8,128)(2,1)S(1)}, bf16[192,768]{1,0:T(8,128)(2,1)S(1)}, u32[]{:S(2)}, u32[]{:S(2)}) collective-permute-start(bf16[192,768]{1,0:T(8,128)(2,1)S(1)} %add_convert_fusion.3.refs_4_), channel_id=1, source_target_pairs={{0,4},{1,5},{2,6},{3,7},{4,0},{5,1},{6,2},{7,3},{8,12},{9,13},{10,... | collective-permute-start | bytes 884744 | tf_op jit(solution)/shard_map/ppermute | solution.py:1231
  291.8 19.2 %collective-permute-start.68 = (bf16[208,768]{1,0:T(8,128)(2,1)}, bf16[208,768]{1,0:T(8,128)(2,1)S(1)}, u32[]{:S(2)}, u32[]{:S(2)}) collective-permute-start(bf16[208,768]{1,0:T(8,128)(2,1)} %add_convert_fusion.2), channel_id=1, source_target_pairs={{0,16},{4,20},{8,24},{12,28},{16,0},{20,4},{24,8},{28,12},{1,17},{... | collective-permute-start | bytes 958472 | tf_op jit(solution)/shard_map/ppermute | solution.py:1217
  313.3 16.7 %collective-permute-start.78 = (bf16[208,768]{1,0:T(8,128)(2,1)S(1)}, bf16[208,768]{1,0:T(8,128)(2,1)S(1)}, u32[]{:S(2)}, u32[]{:S(2)}) collective-permute-start(bf16[208,768]{1,0:T(8,128)(2,1)S(1)} %add_convert_fusion.1.refs_0_), channel_id=1, source_target_pairs={{0,12},{1,13},{2,14},{3,15},{4,8},{5,9},{6,10},{7,11},{8,4},{9,5},... | collective-permute-start | bytes 958472 | tf_op jit(solution)/shard_map/ppermute | solution.py:1231
  315.2 14.8 %collective-permute-start.77 = (bf16[208,768]{1,0:T(8,128)(2,1)S(1)}, bf16[208,768]{1,0:T(8,128)(2,1)S(1)}, u32[]{:S(2)}, u32[]{:S(2)}) collective-permute-start(bf16[208,768]{1,0:T(8,128)(2,1)S(1)} %add_convert_fusion.1.refs_0_), channel_id=1, source_target_pairs={{0,8},{1,9},{2,10},{3,11},{4,12},{5,13},{6,14},{7,15},{8,0},{9,1},... | collective-permute-start | bytes 958472 | tf_op jit(solution)/shard_map/ppermute | solution.py:1231
  (135 other events, 963.5 us)

commit v5 on v4

--- a/solution.py
+++ b/solution.py
@@ -769,7 +769,7 @@
     return back, gradient * values * scale
 
 
-def leave_back_kernel(core_ref, out_ref, proj_ref, near_ref, moved_ref, qn_ref, qm_ref, gain_ref, w_ref, grad_ref, wg_ref, gg_ref, emb_s):
+def leave_back_kernel(core_ref, out_ref, proj_ref, near_ref, moved_ref, qn_ref, qm_ref, gain_ref, w_ref, grad_ref, round_ref, gg_ref, emb_s, wg_ref):
     b = pl.program_id(0)
 
     @pl.when(b == 0)
@@ -797,6 +797,10 @@
     back, addends = norm_back(out, gain, dot_nt(grad, w_ref[...]))
     grad_ref[...] = back.astype(bf16)
     gg_ref[0:1, :] += jnp.sum(addends, axis=0, keepdims=True)
+
+    @pl.when(b == pl.num_programs(0) - 1)
+    def _():
+        round_ref[...] = wg_ref[...].astype(bf16)
 
 
 def leave_back(core, layer_out, projected, near, moved, query_near, query_moved, gain, weight, count):
@@ -817,8 +821,8 @@
             full(depth, wide),
         ],
         out_specs=[rows_of(count, depth), kept(depth, wide), kept(8, depth)],
-        out_shape=(like((total, depth), bf16), like((depth, wide), f32), like((8, depth), f32)),
-        scratch_shapes=[pltpu.VMEM((total, wide), f32)],
+        out_shape=(like((total, depth), bf16), like((depth, wide), bf16), like((8, depth), f32)),
+        scratch_shapes=[pltpu.VMEM((total, wide), f32), pltpu.VMEM((depth, wide), f32)],
         compiler_params=params(14),
         cost_estimate=cost(5),
         name="leave_back",
@@ -828,10 +832,10 @@
 def ffn_back_kernel(hidden, own, *refs):
     gate_s, up_s, down_s = refs[-3:]
     if own:
-        index_ref, grad_ref, norm_ref, gu_ref, d_ref, g_ref, u_ref, part_in, down_in = refs[:9]
-        nf_ref, a_ref, b_ref, *downs = refs[9:-3]
+        index_ref, grad_ref, norm_ref, gu_ref, d_ref, g_ref, u_ref, more_ref, part_in, down_in = refs[:10]
+        nf_ref, a_ref, b_ref, *downs = refs[10:-3]
     else:
-        grad_ref, norm_ref, gu_ref, d_ref, g_ref, u_ref, nf_ref, a_ref, b_ref, down_ref = refs[:-3]
+        grad_ref, norm_ref, gu_ref, d_ref, g_ref, u_ref, more_ref, nf_ref, a_ref, b_ref, down_ref = refs[:-3]
     b = pl.program_id(0)
 
     @pl.when(b == 0)
@@ -859,7 +863,7 @@
 
     @pl.when(b == pl.num_programs(0) - 1)
     def _():
-        cut = a_ref.shape[1]
+        cut = hidden // 2
         a_ref[...] = gate_s[:, :cut].astype(bf16)
         b_ref[:, : hidden - cut] = gate_s[:, cut:].astype(bf16)
         b_ref[:, hidden - cut :] = up_s[...].astype(bf16)
@@ -869,16 +873,19 @@
             for k, ref in enumerate(downs):
                 size = ref.shape[0]
                 rows = pl.ds(pl.multiple_of(jnp.bitwise_xor(index_ref[0], k) * size, size), size)
+                wide = ref.shape[1] // 2
                 ref[:, :hidden] = down_in[rows, :]
-                ref[:, hidden:] = down_s[rows, :].astype(bf16)
-
-
-def ffn_back(grad, normed, gate_up, down, gate, up, count, index=None, part_sum=None, far_down=None):
+                ref[:, hidden:wide] = more_ref[rows, :]
+                ref[:, wide : wide + hidden] = down_s[rows, :].astype(bf16)
+                ref[:, wide + hidden :] = more_ref[rows, :]
+
+
+def ffn_back(grad, normed, gate_up, down, gate, up, more, count, index=None, part_sum=None, far_down=None):
     total, depth = normed.shape
     hidden = down.shape[0]
     own = index is not None
     quarter = depth // 4
-    downs = [(quarter, 2 * hidden)] * 4 if own else [(depth, hidden)]
+    downs = [(quarter, 2 * (hidden + more.shape[1]))] * 4 if own else [(depth, hidden)]
     shapes = [(depth, hidden // 2), (depth, hidden + hidden // 2)] + downs
     return pl.pallas_call(
         partial(ffn_back_kernel, hidden, own),
@@ -891,6 +898,7 @@
             full(hidden, depth),
             full(depth, hidden),
             full(depth, hidden),
+            full(*more.shape),
         ]
         + ([rows_of(count, depth), full(depth, hidden)] if own else []),
         out_specs=[rows_of(count, depth)] + [kept(*shape) for shape in shapes],
@@ -899,7 +907,7 @@
         compiler_params=params(28),
         cost_estimate=cost(10),
         name="ffn_back",
-    )(*([index] if own else []), grad, normed, gate_up, down, gate, up, *([part_sum, far_down] if own else []))
+    )(*([index] if own else []), grad, normed, gate_up, down, gate, up, more, *([part_sum, far_down] if own else []))
 
 
 def mid_back_kernel(near_ref, moved_ref, mid_ref, grad_ref, gain_ref, c0_ref, c1_ref, w0_ref, w1_ref, out_ref, dc0_ref, dc1_ref, ow0_ref, ow1_ref, gg_ref, o0_s, o1_s):
@@ -1420,21 +1428,18 @@
     layer_out_grad, proj_grad, final_gain_part = leave_back(
         core.reshape(1), layer_out, projected, demb, demb_moved, dqe, dqe_moved, gain_final, proj_weight, count
     )
-    proj_part = narrow(part(proj_grad, core, 2))
-    proj_moved = to_x(proj_part)
     nf_sum, far_first, far_rest, far_down_grad = ffn_back(
-        after(layer_out_grad, proj_part), normed_ffn, far_gate_up_out, far_down, far_gate, far_up, count
+        layer_out_grad, normed_ffn, far_gate_up_out, far_down, far_gate, far_up, proj_grad, count
     )
     first_moved = to_x(far_first)
-    proj_part = added(proj_part, after(proj_moved, far_first))
-    proj_moves = [move(proj_part) for move in four]
     nf_part, own_first, own_rest, *down_pieces = ffn_back(
-        after(layer_out_grad, proj_part),
+        after(layer_out_grad, far_first),
         normed_ffn,
         own_gate_up,
         down_weight,
         gate_weight,
         up_weight,
+        proj_grad,
         count,
         four_index,
         nf_sum,
@@ -1444,9 +1449,7 @@
     first_moves = scattered(first_pieces)
     rest_moved = to_x(after(far_rest, first_pieces))
     down_moves = scattered(tuple(down_pieces))
-    proj_part = added(*after((proj_part, *proj_moves), first_pieces))
-    proj_moved = to_dp[rest[0]](proj_part)
-    nf_part = after(nf_part, proj_part)
+    nf_part = after(nf_part, first_pieces)
     mid_grad, own_context_grad, far_context_grad, own_out, far_out, ffn_gain_part = mid_back(
         nf_part, to_core(nf_part), mid, layer_out_grad, gain_ffn, contexts, output_weights, count
     )
@@ -1461,8 +1464,9 @@
         far_tiles[1],
         buckets,
     )
-    down = added(*after(down_moves, far_grads))
-    down_kept, down_moved = down[:, hidden_local:], to_x(down[:, :hidden_local])
+    down = added(*after(down_moves, far_grads, rest_moved))
+    down_wide = hidden_local + vector_width
+    down_kept, down_moved = down[:, down_wide:], to_x(down[:, :down_wide])
     far_all, far_more = heads_far(normed_attn, after(far_grads, down), far_out, final_gain_part, ffn_gain_part, far_bias_grad)
 
     down = added(after(down_moved, far_all), down_kept)
@@ -1472,10 +1476,9 @@
     rest_moves = scattered(rest_pieces)
     early = jnp.concatenate([first, down], axis=1)
     early_moved = to_dp[rest[0]](early)
-    proj_part = rest_of(proj_part, after(proj_moved, far_all))
     own_grads, own_bias_grad = attend_back(
         own_heads,
-        after(own_context_grad, rest_pieces, early, proj_part),
+        after(own_context_grad, rest_pieces, early),
         own_context,
         own_log,
         ranges,
@@ -1494,7 +1497,6 @@
         place_mp, tokens, after(own_grads, others, early, all_moved), far_grads, qkv_weights
     )
     early_all = after(early_all, na_sent)
-    proj_moved = to_core(after(proj_part, na_sent))
     all_pieces = heads_own(
         four_index,
         normed_attn,
@@ -1505,7 +1507,7 @@
         attn_gain_part,
         own_bias_grad,
         all_moved,
-        after(more_moved, na_sent, early_all, proj_moved),
+        after(more_moved, na_sent, early_all),
     )
     all_moves = scattered(all_pieces)
     others = rest_of(others, after(others_moved, all_pieces))
@@ -1523,7 +1525,7 @@
     crossing = [(i, i ^ 3) for i in range(tensor_size)]
     extra_moves = (to_x(extra), to_core(extra), lax.ppermute(extra, "mp", crossing))
     cut = hidden_local // 2
-    gate_weight_grad, up_weight_grad, down_weight_grad = widened(
+    gate_weight_grad, up_weight_grad, down_weight_grad, proj_weight_grad = widened(
         four_index,
         width,
         after((early_all, others_all), extra_moves),
@@ -1531,13 +1533,13 @@
             (((0, 0, cut), (1, 0, cut)), False),
             (((1, cut, cut + hidden_local),), False),
             (((0, cut, cut + hidden_local),), True),
+            (((0, cut + hidden_local, cut + down_wide),), False),
         ),
         "widen_ffn",
     )
     extra_moves, back = after((extra_moves, back), up_weight_grad)
     extra = widen(extra)
     attn_gain_grad = extra[2] + sum(widen(moved[2]) for moved in extra_moves)
-    proj_weight_grad = widen(swapped(core, proj_part, proj_moved))
     position_bias_grad = jnp.transpose(extra[3 : 3 + position_bias.shape[1], :buckets])
     back = widen(back)
     doc_grad = jnp.stack([jnp.where(x == 0, stay, back), jnp.where(x == 0, back, stay)], axis=0)
@@ -1545,7 +1547,7 @@
     query_weight_grad, key_weight_grad, value_weight_grad, output_weight_grad = widened(
         four_index,
         width,
-        (after(both_all, doc_grad, attn_gain_grad, proj_weight_grad),),
+        (after(both_all, doc_grad, attn_gain_grad),),
         tuple((((0, i * inner, (i + 1) * inner),), True) for i in range(4)),
         "widen_heads",
     )

time: 333 us -> 332 us (level)
  starting transfers between devices: 96 us -> 75 us
  waiting for transfers between devices: 71.7 us -> 83.9 us
  Pallas kernels: 124 us -> 132 us
    ppermute x42 -> x39, waiting for transfers between devices: 41.4 us -> 57.2 us  [exchange(): return lambda values: lax.ppermute(values, ('dp', 'mp'), pairs)]
    ppermute x36 -> x33, starting transfers between devices: 41.2 us -> 25.9 us  [over(): return lambda values: lax.ppermute(values, axis, pairs)]
    pallas_call x2, Pallas kernels: 24.3 us -> 29.3 us  [attend_back(): pl.pallas_call(partial(attend_back_kernel, starts, heads, size, steps - 1...]
    ppermute x42 -> x39, starting transfers between devices: 53.7 us -> 49 us  [exchange(): return lambda values: lax.ppermute(values, ('dp', 'mp'), pairs)]
    ppermute x36 -> x33, waiting for transfers between devices: 30.3 us -> 26.7 us  [over(): return lambda values: lax.ppermute(values, axis, pairs)]
  transfers between devices with their start and end apart: 79 -> 73, of which waited for: 35 -> 36; matrix products, arithmetic and copies ran while one was open for 4% -> 4% of each run, Pallas kernels for 28% -> 27%
where the time goes in v5:
time: 332 us
  Pallas kernels  132 us (40%)
  waiting for transfers between devices  83.9 us (25%)
  starting transfers between devices  75 us (23%)
  local copies, waits for them, and re-layouts  27.5 us (8%)
  other arithmetic  8.71 us (3%)
    ppermute x39, waiting for transfers between devices, exchange(): return lambda values: lax.ppermute(values, ('dp', 'mp'), pairs)  57.2 us
    ppermute x39, starting transfers between devices, exchange(): return lambda values: lax.ppermute(values, ('dp', 'mp'), pairs)  49 us
    pallas_call x2, Pallas kernels, attend_back(): pl.pallas_call(partial(attend_back_kernel, starts, heads, size, steps - 1...  29.3 us
    ppermute x33, waiting for transfers between devices, over(): return lambda values: lax.ppermute(values, axis, pairs)  26.7 us
    ppermute x33, starting transfers between devices, over(): return lambda values: lax.ppermute(values, axis, pairs)  25.9 us
    unnamed x168, local copies, waits for them, and re-layouts  22.7 us
    pallas_call x2, Pallas kernels, ffn_back(): pl.pallas_call(partial(ffn_back_kernel, hidden, own), grid=(total // coun...  18.6 us
    pallas_call x2, Pallas kernels, attend(): pl.pallas_call(partial(attend_kernel, heads, size, steps - 1), grid_spec=...  18.3 us
  transfers between devices with their start and end apart: 73, of which 36 were waited for; matrix products, arithmetic and copies ran while one was open for 4% of the time, Pallas kernels for 27%

profile of v5, /device:TPU:0, one launch (start us, length us, event | category | flops | bytes accessed | tf_op | source)
XLA Modules:
  0.0 332.1 jit_solution(15940565600239742095)
XLA Ops:
  7.2 4.0 %pack.1 = (bf16[768,576]{1,0:T(8,128)(2,1)}, bf16[384,576]{1,0:T(8,128)(2,1)}, bf16[128,768]{1,0:T(8,128)(2,1)}, bf16[384,512]{1,0:T(8,128)(2,1)}, bf16[384,512]...) custom-call(s32[2]{0:T(128)} %pad_add_fusion.3.bit_ref, bf16[192,768]{1,0:T(8,128)(2,1)} %bitcast.49, ...), custom_call_target="tpu_custom_call" | custom-call | flops 8999999488 | bytes 1024 | tf_op jit(solution)/shard_map/pack/pallas_call | solution.py:618
  31.2 9.0 %attend.2 = (bf16[1152,192]{1,0:T(8,128)(2,1)S(1)}, f32[8,1152]{1,0:T(8,128)S(1)}) custom-call(s32[5]{0:T(128)S(1)} %get-tuple-element.393.lo_ref, s32[5]{0:T(128)S(1)} %get-tuple-element.394.cnt_ref, bf16[1152,576]{1,0:T(8,128)(2,1)S(1)} %get-tuple-element.183.qkv_ref, s32[1,1152]{1,0:T(1,128)S(1)} %broadcast_in_dim.27.segq_ref, ...), custom_call_target="tpu_custom_call" | custom-call | flops 27000000512 | bytes 1024 | tf_op jit(solution)/shard_map/attend/pallas_call | solution.py:174
  46.0 9.2 %attend.3 = (bf16[1152,192]{1,0:T(8,128)(2,1)S(1)}, f32[8,1152]{1,0:T(8,128)S(1)}) custom-call(s32[5]{0:T(128)S(1)} %get-tuple-element.393.lo_ref, s32[5]{0:T(128)S(1)} %get-tuple-element.394.cnt_ref, bf16[1152,576]{1,0:T(8,128)(2,1)S(1)} %convolution_convert_fusion.qkv_ref, s32[1,1152]{1,0:T(1,128)S(1)} %broadcast_in_dim.27.segq_ref, ...), custom_call_target="tpu_custom_call" | custom-call | flops 27000000512 | bytes 1024 | tf_op jit(solution)/shard_map/attend/pallas_call | solution.py:174
  65.6 5.8 %ffn_own.1 = (bf16[1152,768]{1,0:T(8,128)(2,1)S(1)}, bf16[1152,768]{1,0:T(8,128)(2,1)S(1)}, bf16[1152,1024]{1,0:T(8,128)(2,1)S(1)}, bf16[1152,768]{1,0:T(8,128)(2,1)S(1)}) custom-call(bf16[1152,768]{1,0:T(8,128)(2,1)S(1)} %copy-done.31, bf16[1152,768]{1,0:T(8,128)(2,1)S(1)} %fusion.near_ref, bf16[1152,768]{1,0:T(8,128)(2,1)} %collective-permute-done.10.moved_ref, ...), custom_call_target="tpu_custom_call" | custom-call | flops 15000000512 | bytes 1024 | tf_op jit(solution)/shard_map/ffn_own/pallas_call | solution.py:684
  74.8 4.9 %collective-permute-done.14 = bf16[256,384]{1,0:T(8,128)(2,1)S(1)} collective-permute-done((bf16[256,384]{1,0:T(8,128)(2,1)S(1)}, bf16[256,384]{1,0:T(8,128)(2,1)S(1)}, u32[]{:S(2)}, u32[]{:S(2)}) %collective-permute-start.14) | collective-permute-done | bytes 196640 | tf_op jit(solution)/shard_map/ppermute | solution.py:1225
  80.1 4.5 %ffn_far.1 = (bf16[1152,1024]{1,0:T(8,128)(2,1)S(1)}, bf16[1152,768]{1,0:T(8,128)(2,1)}) custom-call(bf16[1152,768]{1,0:T(8,128)(2,1)S(1)} %get-tuple-element.210.norm_ref.refs_1_.refs_2_, bf16[768,512]{1,0:T(8,128)(2,1)S(1)} %pad_maximum_fusion.2.g_ref.refs_4_, bf16[768,512]{1,0:T(8,128)(2,1)S(1)} %pad_maximum_fusion.3.u_ref.refs_5_, ...), custom_call_target="tpu_custom_call" | custom-call | flops 15000000512 | bytes 1024 | tf_op jit(solution)/shard_map/ffn_far/pallas_call | solution.py:721
  91.6 14.3 %leave.1 = (bf16[1152,768]{1,0:T(8,128)(2,1)S(1)}, f32[1152,128]{1,0:T(8,128)S(1)}, bf16[1152,128]{1,0:T(8,128)(2,1)S(1)}) custom-call(bf16[1152,768]{1,0:T(8,128)(2,1)S(1)} %copy-done.45, bf16[1152,768]{1,0:T(8,128)(2,1)} %get-tuple-element.220.near_ref, bf16[1152,768]{1,0:T(8,128)(2,1)} %collective-permute-done.16.moved_ref, ...), custom_call_target="tpu_custom_call" | custom-call | flops 12000000000 | bytes 1024 | tf_op jit(solution)/shard_map/leave/pallas_call | solution.py:752
  108.0 5.0 %collective-permute-start.19 = (bf16[64,128]{1,0:T(8,128)(2,1)S(1)}, bf16[64,128]{1,0:T(8,128)(2,1)S(1)}, u32[]{:S(2)}, u32[]{:S(2)}) collective-permute-start(bf16[64,128]{1,0:T(8,128)(2,1)S(1)} %get-tuple-element.358), channel_id=1, source_target_pairs={{0,24},{1,25},{2,26},{3,27},{4,28},{5,29},{6,30},{7,31},{8,16},{9,... | collective-permute-start | bytes 49160 | tf_op jit(solution)/shard_map/ppermute | solution.py:1239
  124.1 4.1 %score.1 = (f32[8,1024]{1,0:T(8,128)S(1)}, f32[8,128]{1,0:T(8,128)S(1)}, f32[8,128]{1,0:T(8,128)S(1)}) custom-call(s32[2]{0:T(128)S(1)} %pad_add_fusion.2.first_ref, bf16[1024,128]{1,0:T(8,128)(2,1)S(1)} %slice.137.emb_ref, bf16[1024,128]{1,0:T(8,128)(2,1)S(1)} %constant_dynamic-update-slice_fusion.qe_ref, s32[1,1024]{1,0:T(1,128)S(1)} %slice.179.seg_ref, ...), custom_call_target="tpu_custom_call" | custom-call | flops 15000000512 | bytes 1024 | tf_op jit(solution)/shard_map/score/pallas_call | solution.py:421
  142.0 4.2 %score_back.1 = (f32[1024,128]{1,0:T(8,128)S(1)}, bf16[1024,128]{1,0:T(8,128)(2,1)S(1)}) custom-call(s32[2]{0:T(128)S(1)} %pad_add_fusion.2.first_ref, bf16[1024,128]{1,0:T(8,128)(2,1)S(1)} %slice.137.emb_ref, bf16[1024,128]{1,0:T(8,128)(2,1)S(1)} %constant_dynamic-update-slice_fusion.qe_ref, s32[1,1024]{1,0:T(1,128)S(1)} %slice.179.seg_ref, ...), custom_call_target="tpu_custom_call" | custom-call | flops 15000000512 | bytes 1024 | tf_op jit(solution)/shard_map/score_back/pallas_call | solution.py:488
  167.2 9.3 %ffn_back.2 = (bf16[1152,768]{1,0:T(8,128)(2,1)S(1)}, bf16[768,256]{1,0:T(8,128)(2,1)S(1)}, bf16[768,768]{1,0:T(8,128)(2,1)S(1)}, bf16[768,512]{1,0:T(8,128)(2,1)S(1)}) custom-call(bf16[1152,768]{1,0:T(8,128)(2,1)S(1)} %get-tuple-element.236.refs_0_.refs_1_.grad_ref, bf16[1152,768]{1,0:T(8,128)(2,1)S(1)} %copy-done.56, bf16[1152,1024]{1,0:T(8,128)(2,1)S(1)} %copy-done.54, ...), custom_call_target="tpu_custom_call" | custom-call | flops 30000001024 | bytes 1024 | tf_op jit(solution)/shard_map/ffn_back/pallas_call | solution.py:890
  177.5 9.3 %ffn_back.3 = (bf16[1152,768]{1,0:T(8,128)(2,1)S(1)}, bf16[768,256]{1,0:T(8,128)(2,1)S(1)}, bf16[768,768]{1,0:T(8,128)(2,1)S(1)}, bf16[192,1280]{1,0:T(8,128)(2,...) custom-call(s32[1]{0:T(128)} %bitcast.21.refs_0_.index_ref, ...), custom_call_target="tpu_custom_call" | custom-call | flops 30000001024 | bytes 1024 | tf_op jit(solution)/shard_map/ffn_back/pallas_call | solution.py:890
  194.6 4.8 %mid_back.1 = (bf16[1152,768]{1,0:T(8,128)(2,1)S(1)}, bf16[1152,192]{1,0:T(8,128)(2,1)S(1)}, bf16[1152,192]{1,0:T(8,128)(2,1)S(1)}, bf16[768,192]{1,0:T(8,128)(2...) custom-call(bf16[1152,768]{1,0:T(8,128)(2,1)S(1)} %get-tuple-element.247.near_ref, ...), custom_call_target="tpu_custom_call" | custom-call | flops 17999998976 | bytes 1024 | tf_op jit(solution)/shard_map/mid_back/pallas_call | solution.py:941
  199.5 14.6 %attend_back.2 = (bf16[1152,576]{1,0:T(8,128)(2,1)S(1)}, f32[3,32,128]{2,1,0:T(8,128)S(1)}) custom-call(s32[5]{0:T(128)S(1)} %copy-done.15, s32[5]{0:T(128)S(1)} %copy-done.17, bf16[1152,576]{1,0:T(8,128)(2,1)S(1)} %copy-done.29, bf16[1152,192]{1,0:T(8,128)(2,1)S(1)} %get-tuple-element.253.do_ref, bf16[1152,192]{1,0:T(8,128)(2,1)S(1)} %copy-done.7, ...), custom_call_target="tpu_custom_call" | custom-call | flops 44999999488 | bytes 1024 | tf_op jit(solution)/shard_map/attend_back/pallas_call | solution.py:335
  215.2 5.2 %collective-permute-done.40.moved_ref = bf16[768,768]{1,0:T(8,128)(2,1)S(1)} collective-permute-done((bf16[768,768]{1,0:T(8,128)(2,1)S(1)}, bf16[768,768]{1,0:T(8,128)(2,1)S(1)}, u32[]{:S(2)}, u32[]{:S(2)}) %collective-permute-start.40) | collective-permute-done | bytes 1179680 | tf_op jit(solution)/shard_map/ppermute | solution.py:1225
  229.4 14.7 %attend_back.3 = (bf16[1152,576]{1,0:T(8,128)(2,1)S(1)}, f32[3,32,128]{2,1,0:T(8,128)S(1)}) custom-call(s32[5]{0:T(128)S(1)} %copy-done.15, s32[5]{0:T(128)S(1)} %copy-done.17, bf16[1152,576]{1,0:T(8,128)(2,1)S(1)} %copy-done.43, bf16[1152,192]{1,0:T(8,128)(2,1)S(1)} %get-tuple-element.280.do_ref, bf16[1152,192]{1,0:T(8,128)(2,1)S(1)} %copy-done.5, ...), custom_call_target="tpu_custom_call" | custom-call | flops 44999999488 | bytes 1024 | tf_op jit(solution)/shard_map/attend_back/pallas_call | solution.py:335
  250.4 3.6 %enter_back.1 = (bf16[576,768]{1,0:T(8,128)(2,1)S(1)}, bf16[576,768]{1,0:T(8,128)(2,1)S(1)}, f32[8,768]{1,0:T(8,128)S(1)}) custom-call(s32[1]{0:T(128)} %bitcast.2.place_ref, bf16[1152,768]{1,0:T(8,128)(2,1)S(1)} %copy-done.32, bf16[1152,576]{1,0:T(8,128)(2,1)S(1)} %get-tuple-element.291.own_ref.grad_ref, ...), custom_call_target="tpu_custom_call" | custom-call | flops 12000000000 | bytes 1024 | tf_op jit(solution)/shard_map/enter_back/pallas_call | solution.py:1127
  254.0 8.5 %collective-permute-done.56.refs_3_ = bf16[192,896]{1,0:T(8,128)(2,1)S(1)} collective-permute-done((bf16[192,896]{1,0:T(8,128)(2,1)S(1)}, bf16[192,896]{1,0:T(8,128)(2,1)S(1)}, u32[]{:S(2)}, u32[]{:S(2)}) %collective-permute-start.56) | collective-permute-done | bytes 344096 | tf_op jit(solution)/shard_map/ppermute | solution.py:1239
  262.6 4.7 %collective-permute-done.55.refs_2_ = bf16[192,896]{1,0:T(8,128)(2,1)S(1)} collective-permute-done((bf16[192,896]{1,0:T(8,128)(2,1)S(1)}, bf16[192,896]{1,0:T(8,128)(2,1)S(1)}, u32[]{:S(2)}, u32[]{:S(2)}) %collective-permute-start.55) | collective-permute-done | bytes 344096 | tf_op jit(solution)/shard_map/ppermute | solution.py:1239
  272.9 6.8 %collective-permute-done.57 = bf16[208,768]{1,0:T(8,128)(2,1)S(1)} collective-permute-done((bf16[208,768]{1,0:T(8,128)(2,1)S(1)}, bf16[208,768]{1,0:T(8,128)(2,1)S(1)}, u32[]{:S(2)}, u32[]{:S(2)}) %collective-permute-start.57) | collective-permute-done | bytes 319520 | tf_op jit(solution)/shard_map/ppermute | solution.py:1239
  279.7 4.1 %collective-permute-done.59 = bf16[208,768]{1,0:T(8,128)(2,1)S(1)} collective-permute-done((bf16[208,768]{1,0:T(8,128)(2,1)S(1)}, bf16[208,768]{1,0:T(8,128)(2,1)S(1)}, u32[]{:S(2)}, u32[]{:S(2)}) %collective-permute-start.59) | collective-permute-done | bytes 319520 | tf_op jit(solution)/shard_map/ppermute | solution.py:1239
  297.2 8.5 %collective-permute-done.65.refs_7_ = bf16[192,768]{1,0:T(8,128)(2,1)S(1)} collective-permute-done((bf16[192,768]{1,0:T(8,128)(2,1)S(1)}, bf16[192,768]{1,0:T(8,128)(2,1)S(1)}, u32[]{:S(2)}, u32[]{:S(2)}) %collective-permute-start.65) | collective-permute-done | bytes 294944 | tf_op jit(solution)/shard_map/ppermute | solution.py:1239
  305.7 4.6 %collective-permute-done.64.refs_6_ = bf16[192,768]{1,0:T(8,128)(2,1)S(1)} collective-permute-done((bf16[192,768]{1,0:T(8,128)(2,1)S(1)}, bf16[192,768]{1,0:T(8,128)(2,1)S(1)}, u32[]{:S(2)}, u32[]{:S(2)}) %collective-permute-start.64) | collective-permute-done | bytes 294944 | tf_op jit(solution)/shard_map/ppermute | solution.py:1239
  320.4 6.2 %collective-permute-done.69 = bf16[256,768]{1,0:T(8,128)(2,1)S(1)} collective-permute-done((bf16[256,768]{1,0:T(8,128)(2,1)S(1)}, bf16[256,768]{1,0:T(8,128)(2,1)S(1)}, u32[]{:S(2)}, u32[]{:S(2)}) %collective-permute-start.69) | collective-permute-done | bytes 393248 | tf_op jit(solution)/shard_map/ppermute | solution.py:1225
  (391 shorter events, 159.6 us)
Async XLA Ops:
  1.9 16.3 %collective-permute-start.1 = (bf16[256,768]{1,0:T(8,128)(2,1)S(1)}, bf16[256,768]{1,0:T(8,128)(2,1)S(1)}, u32[]{:S(2)}, u32[]{:S(2)}) collective-permute-start(bf16[256,768]{1,0:T(8,128)(2,1)S(1)} %get-tuple-element.371), channel_id=1, source_target_pairs={{0,2},{1,3},{2,0},{3,1},{4,6},{5,7},{6,4},{7,5},{8,10},{9,11},{10,... | collective-permute-start | bytes 1179656 | tf_op jit(solution)/shard_map/ppermute | solution.py:1225
  11.2 18.4 %collective-permute-start.3 = (bf16[384,576]{1,0:T(8,128)(2,1)}, bf16[384,576]{1,0:T(8,128)(2,1)S(1)}, u32[]{:S(2)}, u32[]{:S(2)}) collective-permute-start(bf16[384,576]{1,0:T(8,128)(2,1)} %get-tuple-element.184), channel_id=1, source_target_pairs={{0,2},{1,3},{2,0},{3,1},{4,6},{5,7},{6,4},{7,5},{8,10},{9,11},{10,... | collective-permute-start | bytes 1327112 | tf_op jit(solution)/shard_map/ppermute | solution.py:1225
  23.1 18.6 %collective-permute-start.6 = (bf16[384,512]{1,0:T(8,128)(2,1)S(1)}, bf16[384,512]{1,0:T(8,128)(2,1)S(1)}, u32[]{:S(2)}, u32[]{:S(2)}) collective-permute-start(bf16[384,512]{1,0:T(8,128)(2,1)S(1)} %copy-done.79), channel_id=1, source_target_pairs={{0,2},{1,3},{2,0},{3,1},{4,6},{5,7},{6,4},{7,5},{8,10},{9,11},{10,... | collective-permute-start | bytes 1179656 | tf_op jit(solution)/shard_map/ppermute | solution.py:1225
  188.7 25.4 %collective-permute-start.41 = (bf16[192,1280]{1,0:T(8,128)(2,1)S(1)}, bf16[192,1280]{1,0:T(8,128)(2,1)S(1)}, u32[]{:S(2)}, u32[]{:S(2)}) collective-permute-start(bf16[192,1280]{1,0:T(8,128)(2,1)S(1)} %get-tuple-element.257), channel_id=1, source_target_pairs={{0,4},{1,5},{2,6},{3,7},{4,0},{5,1},{6,2},{7,3},{8,12},{9,13},{10,... | collective-permute-start | bytes 1474568 | tf_op jit(solution)/shard_map/ppermute | solution.py:1239
  190.3 24.9 %collective-permute-start.42 = (bf16[192,1280]{1,0:T(8,128)(2,1)S(1)}, bf16[192,1280]{1,0:T(8,128)(2,1)S(1)}, u32[]{:S(2)}, u32[]{:S(2)}) collective-permute-start(bf16[192,1280]{1,0:T(8,128)(2,1)S(1)} %get-tuple-element.258), channel_id=1, source_target_pairs={{0,8},{1,9},{2,10},{3,11},{4,12},{5,13},{6,14},{7,15},{8,0},{9,1},... | collective-permute-start | bytes 1474568 | tf_op jit(solution)/shard_map/ppermute | solution.py:1239
  190.5 24.7 %collective-permute-start.43 = (bf16[192,1280]{1,0:T(8,128)(2,1)S(1)}, bf16[192,1280]{1,0:T(8,128)(2,1)S(1)}, u32[]{:S(2)}, u32[]{:S(2)}) collective-permute-start(bf16[192,1280]{1,0:T(8,128)(2,1)S(1)} %get-tuple-element.259), channel_id=1, source_target_pairs={{0,12},{1,13},{2,14},{3,15},{4,8},{5,9},{6,10},{7,11},{8,4},{9,5},... | collective-permute-start | bytes 1474568 | tf_op jit(solution)/shard_map/ppermute | solution.py:1239
  192.3 31.3 %collective-permute-start.44 = (bf16[192,256]{1,0:T(8,128)(2,1)S(1)}, bf16[192,256]{1,0:T(8,128)(2,1)S(1)}, u32[]{:S(2)}, u32[]{:S(2)}) collective-permute-start(bf16[192,256]{1,0:T(8,128)(2,1)S(1)} %get-tuple-element.244), channel_id=1, source_target_pairs={{0,4},{1,5},{2,6},{3,7},{4,0},{5,1},{6,2},{7,3},{8,12},{9,13},{10,... | collective-permute-start | bytes 294920 | tf_op jit(solution)/shard_map/ppermute | solution.py:1239
  193.8 26.6 %collective-permute-start.40 = (bf16[768,768]{1,0:T(8,128)(2,1)S(1)}, bf16[768,768]{1,0:T(8,128)(2,1)S(1)}, u32[]{:S(2)}, u32[]{:S(2)}) collective-permute-start(bf16[768,768]{1,0:T(8,128)(2,1)S(1)} %get-tuple-element.252), channel_id=1, source_target_pairs={{0,2},{1,3},{2,0},{3,1},{4,6},{5,7},{6,4},{7,5},{8,10},{9,11},{10,... | collective-permute-start | bytes 3538952 | tf_op jit(solution)/shard_map/ppermute | solution.py:1225
  223.6 20.5 %collective-permute-start.48 = (bf16[192,768]{1,0:T(8,128)(2,1)S(1)}, bf16[192,768]{1,0:T(8,128)(2,1)S(1)}, u32[]{:S(2)}, u32[]{:S(2)}) collective-permute-start(bf16[192,768]{1,0:T(8,128)(2,1)S(1)} %get-tuple-element.272), channel_id=1, source_target_pairs={{0,4},{1,5},{2,6},{3,7},{4,0},{5,1},{6,2},{7,3},{8,12},{9,13},{10,... | collective-permute-start | bytes 884744 | tf_op jit(solution)/shard_map/ppermute | solution.py:1239
  224.5 19.6 %collective-permute-start.49 = (bf16[192,768]{1,0:T(8,128)(2,1)S(1)}, bf16[192,768]{1,0:T(8,128)(2,1)S(1)}, u32[]{:S(2)}, u32[]{:S(2)}) collective-permute-start(bf16[192,768]{1,0:T(8,128)(2,1)S(1)} %get-tuple-element.273), channel_id=1, source_target_pairs={{0,8},{1,9},{2,10},{3,11},{4,12},{5,13},{6,14},{7,15},{8,0},{9,1},... | collective-permute-start | bytes 884744 | tf_op jit(solution)/shard_map/ppermute | solution.py:1239
  224.8 20.1 %collective-permute-start.50 = (bf16[192,768]{1,0:T(8,128)(2,1)S(1)}, bf16[192,768]{1,0:T(8,128)(2,1)S(1)}, u32[]{:S(2)}, u32[]{:S(2)}) collective-permute-start(bf16[192,768]{1,0:T(8,128)(2,1)S(1)} %get-tuple-element.274), channel_id=1, source_target_pairs={{0,12},{1,13},{2,14},{3,15},{4,8},{5,9},{6,10},{7,11},{8,4},{9,5},... | collective-permute-start | bytes 884744 | tf_op jit(solution)/shard_map/ppermute | solution.py:1239
  227.3 17.8 %collective-permute-start.51 = (bf16[192,896]{1,0:T(8,128)(2,1)S(1)}, bf16[192,896]{1,0:T(8,128)(2,1)S(1)}, u32[]{:S(2)}, u32[]{:S(2)}) collective-permute-start(bf16[192,896]{1,0:T(8,128)(2,1)S(1)} %pad_maximum_fusion.5), channel_id=1, source_target_pairs={{0,16},{4,20},{8,24},{12,28},{16,0},{20,4},{24,8},{28,12},{1,17},{... | collective-permute-start | bytes 1032200 | tf_op jit(solution)/shard_map/ppermute | solution.py:1225
  228.0 21.8 %collective-permute-start.52 = (bf16[784,512]{1,0:T(8,128)(2,1)S(1)}, bf16[784,512]{1,0:T(8,128)(2,1)S(1)}, u32[]{:S(2)}, u32[]{:S(2)}) collective-permute-start(bf16[784,512]{1,0:T(8,128)(2,1)S(1)} %get-tuple-element.289), channel_id=1, source_target_pairs={{0,2},{1,3},{2,0},{3,1},{4,6},{5,7},{6,4},{7,5},{8,10},{9,11},{10,... | collective-permute-start | bytes 2408456 | tf_op jit(solution)/shard_map/ppermute | solution.py:1225
  245.0 27.8 %collective-permute-start.60 = (bf16[192,768]{1,0:T(8,128)(2,1)S(1)}, bf16[192,768]{1,0:T(8,128)(2,1)S(1)}, u32[]{:S(2)}, u32[]{:S(2)}) collective-permute-start(bf16[192,768]{1,0:T(8,128)(2,1)S(1)} %add_convert_fusion.5), channel_id=1, source_target_pairs={{0,16},{4,20},{8,24},{12,28},{16,0},{20,4},{24,8},{28,12},{1,17},{... | collective-permute-start | bytes 884744 | tf_op jit(solution)/shard_map/ppermute | solution.py:1225
  245.2 17.3 %collective-permute-start.56 = (bf16[192,896]{1,0:T(8,128)(2,1)S(1)}, bf16[192,896]{1,0:T(8,128)(2,1)S(1)}, u32[]{:S(2)}, u32[]{:S(2)}) collective-permute-start(bf16[192,896]{1,0:T(8,128)(2,1)S(1)} %add_convert_fusion.1.refs_0_), channel_id=1, source_target_pairs={{0,12},{1,13},{2,14},{3,15},{4,8},{5,9},{6,10},{7,11},{8,4},{9,5},... | collective-permute-start | bytes 1032200 | tf_op jit(solution)/shard_map/ppermute | solution.py:1239
  248.0 19.2 %collective-permute-start.55 = (bf16[192,896]{1,0:T(8,128)(2,1)S(1)}, bf16[192,896]{1,0:T(8,128)(2,1)S(1)}, u32[]{:S(2)}, u32[]{:S(2)}) collective-permute-start(bf16[192,896]{1,0:T(8,128)(2,1)S(1)} %add_convert_fusion.1.refs_0_), channel_id=1, source_target_pairs={{0,8},{1,9},{2,10},{3,11},{4,12},{5,13},{6,14},{7,15},{8,0},{9,1},... | collective-permute-start | bytes 1032200 | tf_op jit(solution)/shard_map/ppermute | solution.py:1239
  249.9 17.4 %collective-permute-start.54 = (bf16[192,896]{1,0:T(8,128)(2,1)S(1)}, bf16[192,896]{1,0:T(8,128)(2,1)S(1)}, u32[]{:S(2)}, u32[]{:S(2)}) collective-permute-start(bf16[192,896]{1,0:T(8,128)(2,1)S(1)} %add_convert_fusion.1.refs_0_), channel_id=1, source_target_pairs={{0,4},{1,5},{2,6},{3,7},{4,0},{5,1},{6,2},{7,3},{8,12},{9,13},{10,... | collective-permute-start | bytes 1032200 | tf_op jit(solution)/shard_map/ppermute | solution.py:1239
  249.9 17.4 %collective-permute-start.53 = (bf16[784,256]{1,0:T(8,128)(2,1)S(1)}, bf16[784,256]{1,0:T(8,128)(2,1)S(1)}, u32[]{:S(2)}, u32[]{:S(2)}) collective-permute-start(bf16[784,256]{1,0:T(8,128)(2,1)S(1)} %get-tuple-element.298), channel_id=1, source_target_pairs={{0,2},{1,3},{2,0},{3,1},{4,6},{5,7},{6,4},{7,5},{8,10},{9,11},{10,... | collective-permute-start | bytes 1204232 | tf_op jit(solution)/shard_map/ppermute | solution.py:1225
  288.1 17.6 %collective-permute-start.65 = (bf16[192,768]{1,0:T(8,128)(2,1)S(1)}, bf16[192,768]{1,0:T(8,128)(2,1)S(1)}, u32[]{:S(2)}, u32[]{:S(2)}) collective-permute-start(bf16[192,768]{1,0:T(8,128)(2,1)S(1)} %add_convert_fusion.4.refs_4_), channel_id=1, source_target_pairs={{0,12},{1,13},{2,14},{3,15},{4,8},{5,9},{6,10},{7,11},{8,4},{9,5},... | collective-permute-start | bytes 884744 | tf_op jit(solution)/shard_map/ppermute | solution.py:1239
  288.2 22.1 %collective-permute-start.64 = (bf16[192,768]{1,0:T(8,128)(2,1)S(1)}, bf16[192,768]{1,0:T(8,128)(2,1)S(1)}, u32[]{:S(2)}, u32[]{:S(2)}) collective-permute-start(bf16[192,768]{1,0:T(8,128)(2,1)S(1)} %add_convert_fusion.4.refs_4_), channel_id=1, source_target_pairs={{0,8},{1,9},{2,10},{3,11},{4,12},{5,13},{6,14},{7,15},{8,0},{9,1},... | collective-permute-start | bytes 884744 | tf_op jit(solution)/shard_map/ppermute | solution.py:1239
  289.9 20.4 %collective-permute-start.63 = (bf16[192,768]{1,0:T(8,128)(2,1)S(1)}, bf16[192,768]{1,0:T(8,128)(2,1)S(1)}, u32[]{:S(2)}, u32[]{:S(2)}) collective-permute-start(bf16[192,768]{1,0:T(8,128)(2,1)S(1)} %add_convert_fusion.4.refs_4_), channel_id=1, source_target_pairs={{0,4},{1,5},{2,6},{3,7},{4,0},{5,1},{6,2},{7,3},{8,12},{9,13},{10,... | collective-permute-start | bytes 884744 | tf_op jit(solution)/shard_map/ppermute | solution.py:1239
  291.6 18.8 %collective-permute-start.62 = (bf16[208,768]{1,0:T(8,128)(2,1)}, bf16[208,768]{1,0:T(8,128)(2,1)S(1)}, u32[]{:S(2)}, u32[]{:S(2)}) collective-permute-start(bf16[208,768]{1,0:T(8,128)(2,1)} %add_convert_fusion.3), channel_id=1, source_target_pairs={{0,16},{4,20},{8,24},{12,28},{16,0},{20,4},{24,8},{28,12},{1,17},{... | collective-permute-start | bytes 958472 | tf_op jit(solution)/shard_map/ppermute | solution.py:1225
  312.7 16.1 %collective-permute-start.72 = (bf16[208,768]{1,0:T(8,128)(2,1)S(1)}, bf16[208,768]{1,0:T(8,128)(2,1)S(1)}, u32[]{:S(2)}, u32[]{:S(2)}) collective-permute-start(bf16[208,768]{1,0:T(8,128)(2,1)S(1)} %add_convert_fusion.2.refs_0_), channel_id=1, source_target_pairs={{0,12},{1,13},{2,14},{3,15},{4,8},{5,9},{6,10},{7,11},{8,4},{9,5},... | collective-permute-start | bytes 958472 | tf_op jit(solution)/shard_map/ppermute | solution.py:1239
  313.7 16.1 %collective-permute-start.71 = (bf16[208,768]{1,0:T(8,128)(2,1)S(1)}, bf16[208,768]{1,0:T(8,128)(2,1)S(1)}, u32[]{:S(2)}, u32[]{:S(2)}) collective-permute-start(bf16[208,768]{1,0:T(8,128)(2,1)S(1)} %add_convert_fusion.2.refs_0_), channel_id=1, source_target_pairs={{0,8},{1,9},{2,10},{3,11},{4,12},{5,13},{6,14},{7,15},{8,0},{9,1},... | collective-permute-start | bytes 958472 | tf_op jit(solution)/shard_map/ppermute | solution.py:1239
  (129 other events, 896.2 us)
